TPU v7x, 32 devices: a whole 2x2x4 slice. The times are simulated.
32 devices in a mesh: dp: 4 (over y, core), mp: 8 (over z, x).
Axes of the slice: x: 2, y: 2, z: 4, core: 2. Of those that a mesh axis runs over, the one named last changes fastest.
Arguments:
- inputs: bfloat16 [2048, 16384], P('dp', 'mp'), may hold values from -6 to 6
- out_grad: bfloat16 [2048, 16384], P('dp', 'mp'), may hold values from -6 to 6
- w_up: bfloat16 [2, 256, 256, 256], P(None, 'mp'), may hold values from -0.25 to 0.25
- w_down: bfloat16 [2, 256, 256, 256], P(None, 'mp'), may hold values from -0.125 to 0.125
- partners: int32 [2, 256], P(None, 'mp'), may hold values from 0 to 63, as said below
Outputs:
- outputs: bfloat16 [2048, 16384], P('dp', 'mp')
- in_grad: bfloat16 [2048, 16384], P('dp', 'mp')
- up_grad: float32 [2, 256, 256, 256], P(None, 'mp', 'dp')
- down_grad: float32 [2, 256, 256, 256], P(None, 'mp', 'dp')
Inputs may be any that keep to these rules, and one draw needn't show every extreme that they name: partners[s, c] = (c // 4) XOR m, where m is 0 or a power of two below 64; the two slots of a column name different blocks.
All inputs are finite; a program needn't handle non-finite values.
Results may differ from a plain program's by a relative error of at most 0.0056.
Values may be sent and summed in bfloat16 or wider, within the bound.
No kernel may reach another device: no remote copies, remote signals or barrier semaphores. Data moves between devices by JAX's collectives and lax.ppermute only.
A program may use at most 256 MiB of HBM per device.

v0:
```python
import jax
import jax.numpy as jnp
from jax import lax
from jax.sharding import PartitionSpec as P


def partner(value, axis, distance):
    mask = 2**distance
    pairs = [(source, source ^ mask) for source in range(lax.axis_size(axis))]
    return lax.ppermute(value, axis, pairs)


def gelu_pair(hidden):
    erf_part = jax.scipy.special.erf(hidden * 0.7071067811865476)
    value = 0.5 * hidden * (1.0 + erf_part)
    slope = 0.5 * (1.0 + erf_part) + hidden * jnp.exp(-0.5 * hidden * hidden) * 0.3989422804014327
    return (value, slope)


def place_terms(term_block, flat_slots, slot_total):
    row_count = term_block.shape[0]
    block_width = term_block.shape[-1]
    flat_terms = term_block.reshape(row_count, -1, block_width)
    empty = jnp.zeros((row_count, slot_total, block_width), jnp.float32)
    return empty.at[:, flat_slots].add(flat_terms)


def shards(inputs, out_grad, w_up, w_down, partners):
    row_count, feature_count = inputs.shape
    block_width = w_up.shape[-1]
    local_blocks = feature_count // block_width
    axis_bits = lax.axis_size("mp").bit_length() - 1
    group_count = axis_bits + 1
    device = lax.axis_index("mp")
    stacked = jnp.stack([inputs, out_grad]).reshape(2, row_count, local_blocks, block_width)
    pieces = [stacked]
    for bit_pos in range(axis_bits):
        pieces.append(partner(stacked, "mp", bit_pos))
    candidates = jnp.concatenate(pieces, axis=2)
    distance = jnp.bitwise_xor(partners // local_blocks, device)
    within = partners % local_blocks
    depth_level = jnp.zeros_like(distance)
    for bit_pos in range(axis_bits):
        depth_level = depth_level + (distance > 1 << bit_pos).astype(jnp.int32)
    slot_index = jnp.where(distance == 0, within, local_blocks * (1 + depth_level) + within)
    flat_slots = slot_index.reshape(-1)
    slot_total = group_count * local_blocks
    chosen = jnp.take(candidates, slot_index, axis=2)
    in_blocks = chosen[0]
    grad_blocks = chosen[1]
    pre_act = jnp.einsum("tsck,sckn->tcn", in_blocks, w_up, preferred_element_type=jnp.float32)
    value, slope = gelu_pair(pre_act)
    activated = value.astype(jnp.bfloat16)
    out_terms = jnp.einsum("tcn,scnk->tsck", activated, w_down, preferred_element_type=jnp.float32)
    out_groups = place_terms(out_terms, flat_slots, slot_total).reshape(
        row_count, group_count, local_blocks, block_width
    )
    down_local = jnp.einsum(
        "tcn,tsck->scnk", activated, grad_blocks, preferred_element_type=jnp.float32
    )
    out_total = out_groups[:, 0]
    for bit_pos in range(axis_bits):
        arrived_out = partner(out_groups[:, bit_pos + 1].astype(jnp.bfloat16), "mp", bit_pos)
        out_total = out_total + arrived_out.astype(jnp.float32)
    hidden_grad = jnp.einsum(
        "tsck,scnk->tcn", grad_blocks, w_down, preferred_element_type=jnp.float32
    )
    pre_grad = (hidden_grad * slope).astype(jnp.bfloat16)
    in_terms = jnp.einsum("tcn,sckn->tsck", pre_grad, w_up, preferred_element_type=jnp.float32)
    in_groups = place_terms(in_terms, flat_slots, slot_total).reshape(
        row_count, group_count, local_blocks, block_width
    )
    up_local = jnp.einsum("tsck,tcn->sckn", in_blocks, pre_grad, preferred_element_type=jnp.float32)
    in_total = in_groups[:, 0]
    for bit_pos in range(axis_bits):
        arrived_in = partner(in_groups[:, bit_pos + 1].astype(jnp.bfloat16), "mp", bit_pos)
        in_total = in_total + arrived_in.astype(jnp.float32)
    up_shared, down_shared = (
        lax.psum_scatter(up_local, "dp", scatter_dimension=2, tiled=True),
        lax.psum_scatter(down_local, "dp", scatter_dimension=2, tiled=True),
    )
    outputs = out_total.reshape(row_count, feature_count).astype(jnp.bfloat16)
    in_grad = in_total.reshape(row_count, feature_count).astype(jnp.bfloat16)
    return (outputs, in_grad, up_shared, down_shared)


def solution(mesh):
    in_specs = (
        P("dp", "mp"),
        P("dp", "mp"),
        P(None, "mp", None, None),
        P(None, "mp", None, None),
        P(None, "mp"),
    )
    out_specs = (P("dp", "mp"), P("dp", "mp"), P(None, "mp", "dp", None), P(None, "mp", "dp", None))
    return jax.shard_map(shards, mesh=mesh, in_specs=in_specs, out_specs=out_specs, check_vma=False)
```

profile of v0, /device:TPU:0, one launch (start us, length us, event | category | flops | bytes accessed | tf_op | source)
XLA Modules:
  0.0 851.1 jit_solution(8087068698788981291)
XLA Ops:
  7.2 0.0 reduce-scatter.5.cloned.1.call-start
  7.2 3.9 copy.57
  11.1 2.8 copy.59
  14.0 0.0 copy-start.2
  14.0 3.9 copy.58
  17.9 3.9 copy.60
  21.8 4.0 pad_maximum_fusion.1
  25.8 4.1 collective-permute-start.2
  29.9 1.6 collective-permute-start.1
  31.5 1.5 collective-permute-start
  33.0 0.0 copy-start
  33.0 0.6 copy-done
  33.6 0.1 reshape.78
  33.6 0.1 copy.56
  33.7 177.0 %collective-permute-done.2 = bf16[2,512,8,256]{3,1,2,0:T(8,128)(2,1)} collective-permute-done((bf16[2,512,8,256]{3,1,2,0:T(8,128)(2,1)}, bf16[2,512,8,256]{3,1,2,0:T(8,128)(2,1)}, u32[]{:S(2)}, u32[]{:S(2)}) %collective-permute-start.2) | collective-permute-done | bytes 4194336 | tf_op jit(solution)/shard_map/ppermute | solution.py:10
  210.8 0.2 collective-permute-done.1
  211.0 0.0 collective-permute-done
  211.0 13.1 %pad_maximum_fusion = bf16[2,512,32,256]{3,1,2,0:T(8,128)(2,1)} fusion(bf16[2,512,8,256]{3,1,2,0:T(8,128)(2,1)} %collective-permute-done.2, bf16[2,512,8,256]{3,1,2,0:T(8,128)(2,1)} %collective-permute-done.1, bf16[2,512,8,256]{3,1,2,0:T(8,128)(2,1)} %collective-permute-done, bf16[1,512,8,256]{3,1,2,0:T(8,128)(2,1)} %copy.60, ...), kind=kLoop, calls=%fused_computation.14 | loop fusion | flops 33554432 | bytes 33554432 | tf_op jit(solution)/shard_map/concatenate | solution.py:39
  224.1 18.4 %gather_fusion = bf16[64,2,512,256]{3,2,1,0:T(8,128)(2,1)} fusion(bf16[2,512,32,256]{3,1,2,0:T(8,128)(2,1)} %pad_maximum_fusion, s32[1024]{0:T(1024)S(1)} %pad_clamp_fusion), kind=kCustom, calls=%fused_computation | custom fusion | bytes 67109120 | tf_op jit(solution)/shard_map/jit(_take)/gather | solution.py:48
  242.5 22.8 %fusion = bf16[2,512,2,32,256]{4,1,2,3,0:T(8,128)(2,1)} fusion(bf16[2,32,2,512,256]{4,3,2,1,0:T(8,128)(2,1)} %bitcast.125, pred[2,32]{0,1:T(8,128)(4,1)S(1)} %copy.56), kind=kLoop, calls=%fused_computation.4 | loop fusion | flops 16777216 | bytes 67108928 | tf_op jit(solution)/shard_map/jit(_take)/select_n | solution.py:48
  265.3 13.8 %fusion.12 = f32[32,512,256,1]{2,1,3,0:T(8,128)} fusion(bf16[2,512,2,32,256]{4,1,2,3,0:T(8,128)(2,1)} %fusion, bf16[2,32,256,256]{3,2,1,0:T(8,128)(2,1)} %param.7), kind=kOutput, calls=%fused_computation.22 | convolution fusion | flops 4294967296 | bytes 41943040 | tf_op jit(solution)/shard_map/tsck,sckn->tcn/dot_general | solution.py:51
  279.2 10.0 %fusion.17 = bf16[512,32,256,1]{2,0,3,1:T(8,128)(2,1)} fusion(f32[32,512,256,1]{2,1,3,0:T(8,128)} %fusion.12), kind=kLoop, calls=%fused_computation.29 | loop fusion | flops 20971520 | bytes 25165824 | tf_op jit(solution)/shard_map/convert_element_type | solution.py:53
  289.1 13.9 %fusion.15 = f32[2,32,256,256]{2,3,0,1:T(8,128)} fusion(bf16[512,32,256,1]{2,0,3,1:T(8,128)(2,1)} %fusion.17, bf16[2,512,2,32,256]{4,1,2,3,0:T(8,128)(2,1)} %fusion), kind=kOutput, calls=%fused_computation.27 | convolution fusion | flops 4294967296 | bytes 41943040 | tf_op jit(solution)/shard_map/tcn,tsck->scnk/dot_general | solution.py:58
  303.0 20.3 %copy.75 = f32[2,32,256,256]{3,1,0,2:T(8,128)} copy(f32[2,32,256,256]{2,3,0,1:T(8,128)} %fusion.15) | data formatting | bytes 33554432 | tf_op jit(solution)/shard_map/tcn,tsck->scnk/transpose | solution.py:58
  323.3 0.0 reduce-scatter.5.cloned.1.call-update
  323.3 0.5 reduce-scatter.3.cloned.1.call-start
  323.8 25.2 %fusion.6 = bf16[512,32,256]{2,0,1:T(8,128)(2,1)} fusion(f32[32,512,256,1]{2,1,3,0:T(8,128)} %fusion.12, bf16[2,512,2,32,256]{4,1,2,3,0:T(8,128)(2,1)} %fusion, bf16[2,32,256,256]{3,2,1,0:T(8,128)(2,1)} %param.8), kind=kOutput, calls=%fused_computation.11 | convolution fusion | flops 4336910336 | bytes 50331648 | tf_op jit(solution)/shard_map/tsck,scnk->tcn/dot_general | solution.py:65
  349.0 16.3 %fusion.16 = f32[2,32,256,256]{2,3,0,1:T(8,128)} fusion(bf16[2,512,2,32,256]{4,1,2,3,0:T(8,128)(2,1)} %fusion, bf16[512,32,256]{2,0,1:T(8,128)(2,1)} %fusion.6), kind=kOutput, calls=%fused_computation.28 | convolution fusion | flops 4294967296 | bytes 41943040 | tf_op jit(solution)/shard_map/tsck,tcn->sckn/dot_general | solution.py:73
  365.3 20.4 %copy.73 = f32[2,32,256,256]{3,1,0,2:T(8,128)} copy(f32[2,32,256,256]{2,3,0,1:T(8,128)} %fusion.16) | data formatting | bytes 33554432 | tf_op jit(solution)/shard_map/tsck,tcn->sckn/transpose | solution.py:73
  385.8 0.0 reduce-scatter.3.cloned.1.call-update
  385.8 0.7 copy-done.1
  386.5 0.1 reshape.71
  386.5 17.2 %convolution_bitcast_fusion = f32[512,2,32,256]{3,0,1,2:T(8,128)} fusion(bf16[512,32,256]{2,0,1:T(8,128)(2,1)} %fusion.6, bf16[2,32,256,256]{3,2,1,0:T(8,128)(2,1)} %param.7), kind=kOutput, calls=%fused_computation.25 | convolution fusion | flops 4294967296 | bytes 50331648 | tf_op jit(solution)/shard_map/tcn,sckn->tsck/dot_general | solution.py:69
  403.8 28.5 %copy.69 = f32[512,2,32,256]{3,2,1,0:T(8,128)S(1)} copy(f32[512,2,32,256]{3,0,1,2:T(8,128)} %convolution_bitcast_fusion) | data formatting | bytes 67108864 | tf_op jit(solution)/shard_map/tcn,sckn->tsck/transpose | solution.py:69
  432.3 37.5 %copy.70 = f32[64,512,256]{2,1,0:T(8,128)} copy(f32[64,512,256]{2,0,1:T(8,128)S(1)} %bitcast.126) | data formatting | bytes 67108864 | tf_op jit(solution)/shard_map/reshape | solution.py:23
  469.8 9.0 %broadcast.46.clone.1 = f32[512,32,256]{2,0,1:T(8,128)} broadcast(f32[]{:T(128)} %constant.28.clone.1), dimensions={} | broadcast | bytes 16777220 | tf_op jit(solution)/shard_map/broadcast.10
  478.7 72.1 %scatter_fusion.1 = f32[512,32,256]{2,0,1:T(8,128)} fusion(f32[512,32,256]{2,0,1:T(8,128)} %broadcast.46.clone.1, s32[64]{0:T(128)S(1)} %fusion.38, f32[64,512,256]{2,1,0:T(8,128)} %copy.70), kind=kCustom, calls=%fused_computation.2 | custom fusion | flops 8388608 | bytes 100663552 | tf_op jit(solution)/shard_map/scatter-add | solution.py:25
  550.9 6.5 convert.11
  557.4 2.8 slice_bitcast_fusion.16
  560.3 1.0 collective-permute-start.6
  561.3 0.4 collective-permute-start.8
  561.7 3.3 collective-permute-start.7
  565.0 18.0 %convolution_bitcast_fusion.1 = f32[512,2,32,256]{3,0,1,2:T(8,128)} fusion(bf16[512,32,256,1]{2,0,3,1:T(8,128)(2,1)} %fusion.17, bf16[2,32,256,256]{3,2,1,0:T(8,128)(2,1)} %param.8), kind=kOutput, calls=%fused_computation.26 | convolution fusion | flops 4294967296 | bytes 50331648 | tf_op jit(solution)/shard_map/tcn,scnk->tsck/dot_general | solution.py:54
  583.0 28.5 %copy.64 = f32[512,2,32,256]{3,2,1,0:T(8,128)S(1)} copy(f32[512,2,32,256]{3,0,1,2:T(8,128)} %convolution_bitcast_fusion.1) | data formatting | bytes 67108864 | tf_op jit(solution)/shard_map/tcn,scnk->tsck/transpose | solution.py:54
  611.4 36.5 %copy.65 = f32[64,512,256]{2,1,0:T(8,128)} copy(f32[64,512,256]{2,0,1:T(8,128)S(1)} %bitcast.127) | data formatting | bytes 67108864 | tf_op jit(solution)/shard_map/reshape | solution.py:23
  647.9 7.8 broadcast.46.clone
  655.7 70.9 %scatter_fusion = f32[512,32,256]{2,0,1:T(8,128)} fusion(f32[512,32,256]{2,0,1:T(8,128)} %broadcast.46.clone, s32[64]{0:T(128)S(1)} %fusion.38, f32[64,512,256]{2,1,0:T(8,128)} %copy.65), kind=kCustom, calls=%fused_computation.1 | custom fusion | flops 8388608 | bytes 100663552 | tf_op jit(solution)/shard_map/scatter-add | solution.py:25
  726.6 6.6 convert.10
  733.2 0.6 slice_bitcast_fusion.19
  733.8 0.1 collective-permute-start.3
  733.9 0.8 collective-permute-start.5
  734.8 0.0 collective-permute-done.6
  734.8 0.8 collective-permute-start.4
  735.6 0.0 collective-permute-done.8
  735.6 0.0 collective-permute-done.7
  735.6 4.5 fusion.33
  740.1 1.6 copy.87
  741.7 38.8 %collective-permute-done.3 = bf16[512,8,256]{2,0,1:T(8,128)(2,1)S(1)} collective-permute-done((bf16[512,8,256]{2,0,1:T(8,128)(2,1)S(1)}, bf16[512,8,256]{2,0,1:T(8,128)(2,1)S(1)}, u32[]{:S(2)}, u32[]{:S(2)}) %collective-permute-start.3) | collective-permute-done | bytes 2097184 | tf_op jit(solution)/shard_map/ppermute | solution.py:10
  780.6 45.2 %collective-permute-done.5 = bf16[512,8,256]{2,0,1:T(8,128)(2,1)S(1)} collective-permute-done((bf16[512,8,256]{2,0,1:T(8,128)(2,1)S(1)}, bf16[512,8,256]{2,0,1:T(8,128)(2,1)S(1)}, u32[]{:S(2)}, u32[]{:S(2)}) %collective-permute-start.5) | collective-permute-done | bytes 2097184 | tf_op jit(solution)/shard_map/ppermute | solution.py:10
  825.8 0.0 collective-permute-done.4
  825.8 3.2 fusion.32
  829.0 1.6 copy.86
  830.6 6.6 copy.77
  837.2 6.6 copy.76
  (8 shorter events, 0.0 us)
Async XLA Ops:
  7.2 823.4 %reduce-scatter.5.cloned.1.call-start = ((), (), s32[]{:S(2)}) async-start(), calls=%async_computation.3 | async-start | bytes 20971520 | tf_op jit(solution)/shard_map/reduce_scatter | solution.py:80
  14.0 19.0 %copy-start.2 = (s32[2,32]{1,0:T(2,128)S(1)}, s32[2,32]{1,0:T(2,128)}, u32[]{:S(2)}) copy-start(s32[2,32]{1,0:T(2,128)} %param.9) | copy-start | bytes 772
  25.8 184.9 %collective-permute-start.2 = (bf16[2,512,8,256]{3,1,2,0:T(8,128)(2,1)}, bf16[2,512,8,256]{3,1,2,0:T(8,128)(2,1)}, u32[]{:S(2)}, u32[]{:S(2)}) collective-permute-start(bf16[2,512,8,256]{3,1,2,0:T(8,128)(2,1)} %pad_maximum_fusion.1), channel_id=1, source_target_pairs={{0,4},{1,5},{2,6},{3,7},{4,0},{5,1},{6,2},{7,3},{8,12},{9,13},{10,... | collective-permute-start | bytes 12582920 | tf_op jit(solution)/shard_map/ppermute | solution.py:10
  29.9 181.1 %collective-permute-start.1 = (bf16[2,512,8,256]{3,1,2,0:T(8,128)(2,1)}, bf16[2,512,8,256]{3,1,2,0:T(8,128)(2,1)}, u32[]{:S(2)}, u32[]{:S(2)}) collective-permute-start(bf16[2,512,8,256]{3,1,2,0:T(8,128)(2,1)} %pad_maximum_fusion.1), channel_id=1, source_target_pairs={{0,2},{1,3},{2,0},{3,1},{4,6},{5,7},{6,4},{7,5},{8,10},{9,11},{10,... | collective-permute-start | bytes 12582920 | tf_op jit(solution)/shard_map/ppermute | solution.py:10
  31.5 179.5 %collective-permute-start = (bf16[2,512,8,256]{3,1,2,0:T(8,128)(2,1)}, bf16[2,512,8,256]{3,1,2,0:T(8,128)(2,1)}, u32[]{:S(2)}, u32[]{:S(2)}) collective-permute-start(bf16[2,512,8,256]{3,1,2,0:T(8,128)(2,1)} %pad_maximum_fusion.1), channel_id=1, source_target_pairs={{0,1},{1,0},{2,3},{3,2},{4,5},{5,4},{6,7},{7,6},{8,9},{9,8},{10,11... | collective-permute-start | bytes 12582920 | tf_op jit(solution)/shard_map/ppermute | solution.py:10
  33.0 0.6 copy-start
  323.3 513.9 %reduce-scatter.3.cloned.1.call-start = ((), (), s32[]{:S(2)}) async-start(), calls=%async_computation.2 | async-start | bytes 20971520 | tf_op jit(solution)/shard_map/reduce_scatter | solution.py:79
  385.8 0.7 copy-start.1
  560.3 174.5 %collective-permute-start.6 = (bf16[512,8,256]{2,0,1:T(8,128)(2,1)}, bf16[512,8,256]{2,0,1:T(8,128)(2,1)S(1)}, u32[]{:S(2)}, u32[]{:S(2)}) collective-permute-start(bf16[512,8,256]{2,0,1:T(8,128)(2,1)} %get-tuple-element.22), channel_id=1, source_target_pairs={{0,1},{1,0},{2,3},{3,2},{4,5},{5,4},{6,7},{7,6},{8,9},{9,8},{10,11... | collective-permute-start | bytes 6291464 | tf_op jit(solution)/shard_map/ppermute | solution.py:10
  561.3 174.3 %collective-permute-start.8 = (bf16[512,8,256]{2,0,1:T(8,128)(2,1)}, bf16[512,8,256]{2,0,1:T(8,128)(2,1)}, u32[]{:S(2)}, u32[]{:S(2)}) collective-permute-start(bf16[512,8,256]{2,0,1:T(8,128)(2,1)} %get-tuple-element.23), channel_id=1, source_target_pairs={{0,4},{1,5},{2,6},{3,7},{4,0},{5,1},{6,2},{7,3},{8,12},{9,13},{10,... | collective-permute-start | bytes 6291464 | tf_op jit(solution)/shard_map/ppermute | solution.py:10
  561.7 173.9 %collective-permute-start.7 = (bf16[512,8,256]{2,0,1:T(8,128)(2,1)}, bf16[512,8,256]{2,0,1:T(8,128)(2,1)}, u32[]{:S(2)}, u32[]{:S(2)}) collective-permute-start(bf16[512,8,256]{2,0,1:T(8,128)(2,1)} %get-tuple-element.24), channel_id=1, source_target_pairs={{0,2},{1,3},{2,0},{3,1},{4,6},{5,7},{6,4},{7,5},{8,10},{9,11},{10,... | collective-permute-start | bytes 6291464 | tf_op jit(solution)/shard_map/ppermute | solution.py:10
  733.8 46.7 %collective-permute-start.3 = (bf16[512,8,256]{2,0,1:T(8,128)(2,1)S(1)}, bf16[512,8,256]{2,0,1:T(8,128)(2,1)S(1)}, u32[]{:S(2)}, u32[]{:S(2)}) collective-permute-start(bf16[512,8,256]{2,0,1:T(8,128)(2,1)S(1)} %get-tuple-element.25), channel_id=1, source_target_pairs={{0,1},{1,0},{2,3},{3,2},{4,5},{5,4},{6,7},{7,6},{8,9},{9,8},{10,11... | collective-permute-start | bytes 6291464 | tf_op jit(solution)/shard_map/ppermute | solution.py:10
  733.9 91.9 %collective-permute-start.5 = (bf16[512,8,256]{2,0,1:T(8,128)(2,1)S(1)}, bf16[512,8,256]{2,0,1:T(8,128)(2,1)S(1)}, u32[]{:S(2)}, u32[]{:S(2)}) collective-permute-start(bf16[512,8,256]{2,0,1:T(8,128)(2,1)S(1)} %get-tuple-element.26), channel_id=1, source_target_pairs={{0,4},{1,5},{2,6},{3,7},{4,0},{5,1},{6,2},{7,3},{8,12},{9,13},{10,... | collective-permute-start | bytes 6291464 | tf_op jit(solution)/shard_map/ppermute | solution.py:10
  734.8 91.0 %collective-permute-start.4 = (bf16[512,8,256]{2,0,1:T(8,128)(2,1)S(1)}, bf16[512,8,256]{2,0,1:T(8,128)(2,1)S(1)}, u32[]{:S(2)}, u32[]{:S(2)}) collective-permute-start(bf16[512,8,256]{2,0,1:T(8,128)(2,1)S(1)} %get-tuple-element.27), channel_id=1, source_target_pairs={{0,2},{1,3},{2,0},{3,1},{4,6},{5,7},{6,4},{7,5},{8,10},{9,11},{10,... | collective-permute-start | bytes 6291464 | tf_op jit(solution)/shard_map/ppermute | solution.py:10
Sparse Core Ops, SparseCore 0:
  323.5 125.8 reduce-scatter.4
  451.9 125.0 reduce-scatter.2
where the time goes:
time: 859 us; the launch traced here: 851 us
  waiting for transfers between devices  261 us (30%)
  local copies, waits for them, and re-layouts  243 us (28%)
  other arithmetic  214 us (25%)
  matrix products  104 us (12%)
  between operations  14.6 us (2%)
  starting transfers between devices  14.2 us (2%)
    ppermute x9, waiting for transfers between devices, partner(): return lax.ppermute(value, axis, pairs)  261 us
    scatter-add x2, other arithmetic, place_terms(): return empty.at[:, flat_slots].add(flat_terms)  143 us
    reshape x2, local copies, waits for them, and re-layouts, place_terms(): flat_terms = term_block.reshape(row_count, -1, block_width)  73.9 us
    transpose x1, local copies, waits for them, and re-layouts, shards(): jnp.einsum('tcn,sckn->tsck', pre_grad, w_up, preferred_element_type=jnp.f...  28.5 us
    transpose x1, local copies, waits for them, and re-layouts, shards(): jnp.einsum('tcn,scnk->tsck', activated, w_down, preferred_element_type=jn...  28.5 us
    dot_general x1, matrix products, shards(): jnp.einsum('tsck,scnk->tcn', grad_blocks, w_down, preferred_element_type=...  25.2 us
    select_n x2, other arithmetic, shards(): chosen = jnp.take(candidates, slot_index, axis=2)  22.9 us
    unnamed x10, local copies, waits for them, and re-layouts  22.3 us
  transfers between devices with their start and end apart: 11, of which 4 were waited for; matrix products, arithmetic and copies ran while one was open for 50% of the time, Pallas kernels for 0%

commit v1 on v0

v1 whole, which is shorter than its diff:
```python
import functools

import jax
import jax.numpy as jnp
from jax import lax
from jax.experimental import pallas as pl
from jax.experimental.pallas import tpu as pltpu
from jax.sharding import PartitionSpec as P


GROUPS = 2


def partner(value, axis, distance):
    mask = 2**distance
    pairs = [(source, source ^ mask) for source in range(lax.axis_size(axis))]
    return lax.ppermute(value, axis, pairs)


def gelu_pair(hidden):
    erf_part = lax.erf(hidden * 0.7071067811865476)
    value = 0.5 * hidden * (1.0 + erf_part)
    slope = 0.5 * (1.0 + erf_part) + hidden * jnp.exp(-0.5 * hidden * hidden) * 0.3989422804014327
    return value, slope


def dot_nn(left, right):
    return lax.dot_general(left, right, (((1,), (0,)), ((), ())), preferred_element_type=jnp.float32)


def dot_nt(left, right):
    return lax.dot_general(left, right, (((1,), (1,)), ((), ())), preferred_element_type=jnp.float32)


def dot_tn(left, right):
    return lax.dot_general(left, right, (((0,), (0,)), ((), ())), preferred_element_type=jnp.float32)


def main_body(dims, slots_ref, parity_ref, *refs):
    local, bits, rows, width, _, halves, _, has_prior = dims
    x_hbm, g_hbm = refs[0], refs[1]
    arrived = refs[2 : 2 + bits]
    at = 2 + bits
    prior = refs[at] if has_prior else None
    at += int(has_prior)
    up_ref, down_ref = refs[at], refs[at + 1]
    acc_hbm = refs[at + 2]
    sent = refs[at + 3 : at + 3 + bits]
    keep_ref, send_ref = refs[at + 3 + bits], refs[at + 4 + bits]
    cand, acc, stage, square, in_sems, acc_sems, out_sems = refs[at + 5 + bits :]
    step = pl.program_id(0)
    last = pl.num_programs(0) - 1

    def loads():
        copies = []
        for kind, source in enumerate((x_hbm, g_hbm)):
            for block in range(local):
                view = source.at[:, pl.ds(block * width, width)]
                copies.append((view, cand.at[kind, block]))
        for kind in range(2):
            for bit in range(bits):
                for row in range(rows):
                    view = arrived[bit].at[kind, :, pl.ds(row * width, width)]
                    copies.append((view, cand.at[kind, local + bit * rows + row]))
        return [pltpu.make_async_copy(a, b, in_sems.at[i]) for i, (a, b) in enumerate(copies)]

    def acc_copy(store):
        copies = []
        for kind in range(2):
            for block in range(local):
                index = kind * local + block
                far = acc_hbm if store else prior
                ends = (acc.at[kind, block], far.at[kind, block])
                ends = ends if store else ends[::-1]
                copies.append(pltpu.make_async_copy(*ends, acc_sems.at[index]))
        return copies

    @pl.when(step == 0)
    def _():
        for copy in loads():
            copy.start()
        if has_prior:
            for copy in acc_copy(False):
                copy.start()
        start = local if has_prior else 0
        tokens = acc.shape[2]
        for kind in range(2):

            @pl.loop(start, acc.shape[1])
            def _(slot):
                acc[kind, slot] = jnp.zeros((tokens, width), jnp.float32)

        if has_prior:
            for copy in acc_copy(False):
                copy.wait()
        for copy in loads():
            copy.wait()

    first_slot = slots_ref[step]
    second_slot = slots_ref[pl.num_programs(0) + step]
    slots = (first_slot, second_slot)
    pre_act = dot_nn(cand[0, first_slot], up_ref[0, 0]) + dot_nn(cand[0, second_slot], up_ref[1, 0])
    value, slope = gelu_pair(pre_act)
    activated = value.astype(jnp.bfloat16)
    hidden_grad = dot_nt(cand[1, first_slot], down_ref[0, 0])
    hidden_grad = hidden_grad + dot_nt(cand[1, second_slot], down_ref[1, 0])
    pre_grad = (hidden_grad * slope).astype(jnp.bfloat16)
    parity = parity_ref[0]
    piece = width // (2 * halves)
    for index, slot in enumerate(slots):
        acc[0, slot] += dot_nn(activated, down_ref[index, 0])
        acc[1, slot] += dot_nt(pre_grad, up_ref[index, 0])
        for which, grad in enumerate(
            (dot_tn(cand[0, slot], pre_grad), dot_tn(activated, cand[1, slot]))
        ):
            square[which] = grad
            for half in range(halves):
                own = pl.multiple_of((2 * half + parity) * piece, piece)
                other = pl.multiple_of((2 * half + 1 - parity) * piece, piece)
                keep_ref[0, half, which, index] = square[which, pl.ds(own, piece), :]
                send_ref[0, half, which, index] = square[which, pl.ds(other, piece), :]

    @pl.when(step == last)
    def _():
        for copy in acc_copy(True):
            copy.start()
        for bit in range(bits):
            for kind in range(2):
                for row in range(rows):
                    total = acc[kind, local + bit * rows + row]
                    stage[bit, kind, :, pl.ds(row * width, width)] = total.astype(jnp.bfloat16)
            pltpu.make_async_copy(stage.at[bit], sent[bit], out_sems.at[bit]).start()
        for bit in range(bits):
            pltpu.make_async_copy(stage.at[bit], sent[bit], out_sems.at[bit]).wait()
        for copy in acc_copy(True):
            copy.wait()


def main_call(group, rows, slots, parity, inputs, out_grad, arrived, prior, w_up, w_down, halves):
    tokens, features = inputs.shape
    slot_kinds, columns, width, _ = w_up.shape
    local = features // width
    bits = len(arrived)
    cols = columns * rows // local
    slot_count = local + bits * rows
    first = group * cols
    has_prior = prior is not None
    piece = width // (2 * halves)
    dims = (local, bits, rows, width, slot_count, halves, first, has_prior)
    anywhere = pl.BlockSpec(memory_space=pl.ANY)
    weight = pl.BlockSpec((slot_kinds, 1, width, width), lambda i, *_: (0, first + i, 0, 0))
    grad_block = pl.BlockSpec((1, halves, 2, slot_kinds, piece, width), lambda i, *_: (i, 0, 0, 0, 0, 0))
    grad_shape = jax.ShapeDtypeStruct((cols, halves, 2, slot_kinds, piece, width), jnp.float32)
    operands = [inputs, out_grad, *arrived] + ([prior] if has_prior else []) + [w_up, w_down]
    pair_flops = 2 * tokens * width * width * 6
    moved = 2 * cols * slot_kinds * width * width * 6 + 12 * tokens * width * slot_count
    return pl.pallas_call(
        functools.partial(main_body, dims),
        grid_spec=pltpu.PrefetchScalarGridSpec(
            num_scalar_prefetch=2,
            grid=(cols,),
            in_specs=[anywhere] * (len(operands) - 2) + [weight, weight],
            out_specs=[anywhere] * (1 + bits) + [grad_block, grad_block],
            scratch_shapes=[
                pltpu.VMEM((2, slot_count, tokens, width), jnp.bfloat16),
                pltpu.VMEM((2, slot_count, tokens, width), jnp.float32),
                pltpu.VMEM((bits, 2, tokens, rows * width), jnp.bfloat16),
                pltpu.VMEM((2, width, width), jnp.float32),
                pltpu.SemaphoreType.DMA((2 * slot_count,)),
                pltpu.SemaphoreType.DMA((2 * local,)),
                pltpu.SemaphoreType.DMA((bits,)),
            ],
        ),
        out_shape=[
            jax.ShapeDtypeStruct((2, local, tokens, width), jnp.float32),
            *[jax.ShapeDtypeStruct((2, tokens, rows * width), jnp.bfloat16)] * bits,
            grad_shape,
            grad_shape,
        ],
        cost_estimate=pl.CostEstimate(
            flops=pair_flops * cols * slot_kinds,
            bytes_accessed=moved,
            transcendentals=2 * cols * tokens * width,
        ),
        compiler_params=pltpu.CompilerParams(
            dimension_semantics=("arbitrary",), vmem_limit_bytes=60 << 20
        ),
        name="columns",
    )(slots, parity, *operands)


def halve_body(parity_ref, keep_ref, recv_ref, kept_ref, send_ref):
    parity = parity_ref[0]
    for half in range(kept_ref.shape[1]):
        own = 2 * half + parity
        other = 2 * half + 1 - parity
        kept_ref[:, half] = keep_ref[:, own] + recv_ref[:, own]
        send_ref[:, half] = keep_ref[:, other] + recv_ref[:, other]


def halve_call(parity, keep, recv):
    cols, halves, pair, slot_kinds, piece, width = keep.shape
    block = cols // 4 if cols % 4 == 0 else cols
    spec = pl.BlockSpec((block, halves, pair, slot_kinds, piece, width), lambda i, *_: (i, 0, 0, 0, 0, 0))
    half_shape = (cols, halves // 2, pair, slot_kinds, piece, width)
    half_spec = pl.BlockSpec((block,) + half_shape[1:], lambda i, *_: (i, 0, 0, 0, 0, 0))
    return pl.pallas_call(
        halve_body,
        grid_spec=pltpu.PrefetchScalarGridSpec(
            num_scalar_prefetch=1,
            grid=(cols // block,),
            in_specs=[spec, spec],
            out_specs=[half_spec, half_spec],
        ),
        out_shape=[jax.ShapeDtypeStruct(half_shape, jnp.float32)] * 2,
        cost_estimate=pl.CostEstimate(flops=keep.size, bytes_accessed=12 * keep.size, transcendentals=0),
        name="halve",
    )(parity, keep, recv)


def grads_body(keep_ref, recv_ref, *refs):
    up_ref, down_ref = refs[-2], refs[-1]
    for which, ref in enumerate((up_ref, down_ref)):
        for slot in range(ref.shape[0]):
            ref[slot] = keep_ref[:, 0, which, slot] + recv_ref[:, 0, which, slot]


def grads_call(group, columns, keep, recv, prior):
    cols, _, pair, slot_kinds, piece, width = keep.shape
    block = cols // 4 if cols % 4 == 0 else cols
    first = group * (cols // block)
    spec = pl.BlockSpec((block, 1, pair, slot_kinds, piece, width), lambda i: (i, 0, 0, 0, 0, 0))
    out_spec = pl.BlockSpec((slot_kinds, block, piece, width), lambda i: (0, first + i, 0, 0))
    out_shape = jax.ShapeDtypeStruct((slot_kinds, columns, piece, width), jnp.float32)
    return pl.pallas_call(
        grads_body,
        grid=(cols // block,),
        in_specs=[spec, spec] + [pl.BlockSpec(memory_space=pl.ANY)] * len(prior),
        out_specs=[out_spec, out_spec],
        out_shape=[out_shape, out_shape],
        input_output_aliases={2 + i: i for i in range(len(prior))},
        cost_estimate=pl.CostEstimate(flops=keep.size, bytes_accessed=12 * keep.size, transcendentals=0),
        name="grads",
    )(keep, recv, *prior)


def total_body(bits, acc_ref, *refs):
    out_refs = refs[-2:]
    for kind in range(2):
        total = acc_ref[kind, 0]
        for bit in range(bits):
            total = total + refs[bit][kind].astype(jnp.float32)
        out_refs[kind][...] = total.astype(jnp.bfloat16)


def total_call(group, rows, acc, arrived, prior):
    _, local, tokens, width = acc.shape
    bits = len(arrived)
    first = group * rows
    acc_spec = pl.BlockSpec((2, 1, tokens, width), lambda i: (0, first + i, 0, 0))
    recv_spec = pl.BlockSpec((2, tokens, width), lambda i: (0, 0, i))
    out_spec = pl.BlockSpec((tokens, width), lambda i: (0, first + i))
    out_shape = jax.ShapeDtypeStruct((tokens, local * width), jnp.bfloat16)
    size = 2 * rows * tokens * width
    return pl.pallas_call(
        functools.partial(total_body, bits),
        grid=(rows,),
        in_specs=[acc_spec] + [recv_spec] * bits + [pl.BlockSpec(memory_space=pl.ANY)] * len(prior),
        out_specs=[out_spec, out_spec],
        out_shape=[out_shape, out_shape],
        input_output_aliases={1 + bits + i: i for i in range(len(prior))},
        cost_estimate=pl.CostEstimate(flops=size * bits, bytes_accessed=(6 + 2 * bits) * size, transcendentals=0),
        name="totals",
    )(acc, *arrived, *prior)


def shards(inputs, out_grad, w_up, w_down, partners):
    _, features = inputs.shape
    _, columns, width, _ = w_up.shape
    local = features // width
    bits = lax.axis_size("mp").bit_length() - 1
    dp_bits = lax.axis_size("dp").bit_length() - 1
    group_count = min(GROUPS, local)
    rows = local // group_count
    cols = columns // group_count
    device = lax.axis_index("mp")
    dp_index = lax.axis_index("dp")

    distance = jnp.bitwise_xor(partners // local, device)
    within = partners % local
    level = jnp.zeros_like(distance)
    for bit in range(1, bits):
        level = level + (distance >= 1 << bit).astype(jnp.int32)
    slot = jnp.where(distance == 0, within, local + level * rows + within % rows)
    parities = [(dp_index // 2**bit % 2).reshape(1).astype(jnp.int32) for bit in range(dp_bits)]

    arrived = []
    for group in range(group_count):
        lanes = slice(group * rows * width, (group + 1) * rows * width)
        pair = jnp.stack([inputs[:, lanes], out_grad[:, lanes]])
        arrived.append([partner(pair, "mp", bit) for bit in range(bits)])

    acc = None
    returned = []
    kept = []
    for group in range(group_count):
        slots = slot[:, group * cols : (group + 1) * cols].reshape(-1)
        acc, *rest = main_call(
            group, rows, slots, parities[0], inputs, out_grad, arrived[group], acc, w_up, w_down,
            2 ** (dp_bits - 1),
        )
        returned.append([partner(rest[bit], "mp", bit) for bit in range(bits)])
        keep, send = rest[bits:]
        for bit in range(1, dp_bits):
            recv = partner(send, "dp", bit - 1)
            keep, send = halve_call(parities[bit], keep, recv)
        kept.append((keep, partner(send, "dp", dp_bits - 1)))

    grads = []
    for group in range(group_count):
        grads = grads_call(group, columns, *kept[group], grads)
    totals = []
    for group in range(group_count):
        totals = total_call(group, rows, acc, returned[group], totals)
    return (*totals, *grads)


def solution(mesh):
    in_specs = (
        P("dp", "mp"),
        P("dp", "mp"),
        P(None, "mp", None, None),
        P(None, "mp", None, None),
        P(None, "mp"),
    )
    out_specs = (P("dp", "mp"), P("dp", "mp"), P(None, "mp", "dp", None), P(None, "mp", "dp", None))

    return jax.shard_map(shards, mesh=mesh, in_specs=in_specs, out_specs=out_specs, check_vma=False)
```

time: 859 us -> 433 us (0.50)
  local copies, waits for them, and re-layouts: 243 us -> 3.95 us
  other arithmetic: 214 us -> 1.71 us
  Pallas kernels: 0 us -> 111 us
  matrix products: 104 us -> 0 us
  waiting for transfers between devices: 261 us -> 294 us
  between operations: 14.6 us -> 0.72 us
    scatter-add x2 -> x0, other arithmetic: 143 us -> none  [place_terms(): return empty.at[:, flat_slots].add(flat_terms)]
    pallas_call x0 -> x8, Pallas kernels: none -> 111 us  [the longest x2 70.1 us: main_call(): pl.pallas_call(functools.partial(main_body, dims), grid_spec=pltpu.Prefet...]
    dot_general x6 -> x0, matrix products: 104 us -> none  [the longest x1 25.2 us: shards(): jnp.einsum('tsck,scnk->tcn', grad_blocks, w_down, preferred_element_type=...]
    transpose x4 -> x0, local copies, waits for them, and re-layouts: 97.7 us -> none  [the longest x1 28.5 us: shards(): jnp.einsum('tcn,sckn->tsck', pre_grad, w_up, preferred_element_type=jnp.f...]
    reshape x3 -> x2, local copies, waits for them, and re-layouts: 74 us -> 1.25 us  [shards(): slots = slot[:, group * cols:(group + 1) * cols].reshape(-1)]
    ppermute x9 -> x16, waiting for transfers between devices: 261 us -> 294 us  [partner(): return lax.ppermute(value, axis, pairs)]
    select_n x3 -> x1, other arithmetic: 22.9 us -> 0.02 us  [shards(): jnp.where(distance == 0, within, local + level * rows + within % rows)]
    unnamed x10 -> x6, local copies, waits for them, and re-layouts: 22.3 us -> 0.01 us
  transfers between devices with their start and end apart: 11 -> 16, of which waited for: 4 -> 8; matrix products, arithmetic and copies ran while one was open for 50% -> 0% of each run, Pallas kernels for 0% -> 24%
where the time goes in v1:
time: 433 us; the launch traced here: 431 us
  waiting for transfers between devices  294 us (68%)
  Pallas kernels  111 us (26%)
  starting transfers between devices  19.9 us (5%)
    ppermute x16, waiting for transfers between devices, partner(): return lax.ppermute(value, axis, pairs)  294 us
    pallas_call x2, Pallas kernels, main_call(): pl.pallas_call(functools.partial(main_body, dims), grid_spec=pltpu.Prefet...  70.1 us
    ppermute x16, starting transfers between devices, partner(): return lax.ppermute(value, axis, pairs)  19.9 us
    pallas_call x2, Pallas kernels, halve_call(): pl.pallas_call(halve_body, grid_spec=pltpu.PrefetchScalarGridSpec(num_sca...  17.9 us
    pallas_call x2, Pallas kernels, total_call(): pl.pallas_call(functools.partial(total_body, bits), grid=(rows,), in_spec...  11.6 us
    pallas_call x2, Pallas kernels, grads_call(): pl.pallas_call(grads_body, grid=(cols // block,), in_specs=[spec, spec] +...  11.6 us
  transfers between devices with their start and end apart: 16, of which 8 were waited for; matrix products, arithmetic and copies ran while one was open for 0% of the time, Pallas kernels for 24%

profile of v1, /device:TPU:0, one launch (start us, length us, event | category | flops | bytes accessed | tf_op | source)
XLA Modules:
  0.0 431.3 jit_solution(7831072730471700850)
XLA Ops:
  0.6 2.6 slice_bitcast_fusion
  3.3 1.5 pad_maximum_fusion.1
  4.8 4.1 collective-permute-start.5
  8.8 1.6 collective-permute-start.4
  10.4 1.5 collective-permute-start.3
  11.9 0.0 copy-start.1
  11.9 0.2 pad_maximum_fusion
  12.1 0.4 collective-permute-start.2
  12.5 0.4 collective-permute-start.1
  12.9 88.4 %collective-permute-done.5.refs_4_ = bf16[2,512,1024]{2,1,0:T(8,128)(2,1)S(1)} collective-permute-done((bf16[2,512,1024]{2,1,0:T(8,128)(2,1)}, bf16[2,512,1024]{2,1,0:T(8,128)(2,1)S(1)}, u32[]{:S(2)}, u32[]{:S(2)}) %collective-permute-start.5) | collective-permute-done | bytes 2097184 | tf_op jit(solution)/shard_map/ppermute | solution.py:17
  101.4 0.0 copy-start.2
  101.4 2.0 collective-permute-start
  103.4 0.0 copy-done.2
  103.4 0.0 copy-done.1
  103.4 0.1 fusion.5
  103.5 0.7 reshape.22.slots_ref
  104.2 0.6 reshape.20.slots_ref
  104.7 0.0 collective-permute-done.4.refs_3_
  104.7 0.0 collective-permute-done.3.refs_2_
  104.7 33.9 %columns.2 = (f32[2,8,512,256]{3,2,1,0:T(8,128)}, bf16[2,512,1024]{2,1,0:T(8,128)(2,1)}, bf16[2,512,1024]{2,1,0:T(8,128)(2,1)}, bf16[2,512,1024]{2,1,0:T(8,128)(...) custom-call(s32[32]{0:T(128)} %reshape.22.slots_ref, s32[1]{0:T(128)} %bitcast.parity_ref, ...), custom_call_target="tpu_custom_call" | custom-call | flops 12884901888 | bytes 56623104 | tf_op jit(solution)/shard_map/columns/pallas_call | solution.py:157
  138.6 0.1 collective-permute-start.14
  138.7 51.0 %collective-permute-done.2.refs_4_ = bf16[2,512,1024]{2,1,0:T(8,128)(2,1)} collective-permute-done((bf16[2,512,1024]{2,1,0:T(8,128)(2,1)S(1)}, bf16[2,512,1024]{2,1,0:T(8,128)(2,1)}, u32[]{:S(2)}, u32[]{:S(2)}) %collective-permute-start.2) | collective-permute-done | bytes 2097184 | tf_op jit(solution)/shard_map/ppermute | solution.py:17
  189.7 0.1 collective-permute-done.1.refs_3_
  189.9 0.0 collective-permute-done.refs_2_
  189.9 36.3 %columns.3 = (f32[2,8,512,256]{3,2,1,0:T(8,128)}, bf16[2,512,1024]{2,1,0:T(8,128)(2,1)}, bf16[2,512,1024]{2,1,0:T(8,128)(2,1)}, bf16[2,512,1024]{2,1,0:T(8,128)(...) custom-call(s32[32]{0:T(128)} %reshape.20.slots_ref, s32[1]{0:T(128)} %bitcast.parity_ref, ...), custom_call_target="tpu_custom_call" | custom-call | flops 12884901888 | bytes 56623104 | tf_op jit(solution)/shard_map/columns/pallas_call | solution.py:157
  226.2 0.1 collective-permute-start.12
  226.3 1.6 collective-permute-start.9
  227.9 1.5 collective-permute-start.10
  229.4 2.3 collective-permute-start.11
  231.7 0.0 collective-permute-done.14.recv_ref
  231.7 8.9 %halve.3 = (f32[16,1,2,2,64,256]{5,4,3,2,1,0:T(8,128)}, f32[16,1,2,2,64,256]{5,4,3,2,1,0:T(8,128)}) custom-call(s32[1]{0:T(128)} %bitcast.5.parity_ref, f32[16,2,2,2,64,256]{5,4,3,2,1,0:T(8,128)} %get-tuple-element.44.keep_ref, f32[16,2,2,2,64,256]{5,4,3,2,1,0:T(8,128)} %collective-permute-done.14.recv_ref), custom_call_target="tpu_custom_call" | custom-call | flops 2097152 | bytes 25165824 | tf_op jit(solution)/shard_map/halve/pallas_call | solution.py:207
  240.6 1.5 collective-permute-start.15
  242.2 0.0 collective-permute-done.12.recv_ref
  242.2 9.0 %halve.2 = (f32[16,1,2,2,64,256]{5,4,3,2,1,0:T(8,128)}, f32[16,1,2,2,64,256]{5,4,3,2,1,0:T(8,128)}) custom-call(s32[1]{0:T(128)} %bitcast.5.parity_ref, f32[16,2,2,2,64,256]{5,4,3,2,1,0:T(8,128)} %get-tuple-element.40.keep_ref, f32[16,2,2,2,64,256]{5,4,3,2,1,0:T(8,128)} %collective-permute-done.12.recv_ref), custom_call_target="tpu_custom_call" | custom-call | flops 2097152 | bytes 25165824 | tf_op jit(solution)/shard_map/halve/pallas_call | solution.py:207
  251.1 0.5 collective-permute-start.13
  251.6 22.8 %collective-permute-done.9.refs_0_ = bf16[2,512,1024]{2,1,0:T(8,128)(2,1)S(1)} collective-permute-done((bf16[2,512,1024]{2,1,0:T(8,128)(2,1)}, bf16[2,512,1024]{2,1,0:T(8,128)(2,1)S(1)}, u32[]{:S(2)}, u32[]{:S(2)}) %collective-permute-start.9) | collective-permute-done | bytes 2097184 | tf_op jit(solution)/shard_map/ppermute | solution.py:17
  274.5 0.0 copy-start
  274.5 1.5 collective-permute-start.6
  276.0 44.2 %collective-permute-done.10.refs_1_ = bf16[2,512,1024]{2,1,0:T(8,128)(2,1)} collective-permute-done((bf16[2,512,1024]{2,1,0:T(8,128)(2,1)}, bf16[2,512,1024]{2,1,0:T(8,128)(2,1)}, u32[]{:S(2)}, u32[]{:S(2)}) %collective-permute-start.10) | collective-permute-done | bytes 2097184 | tf_op jit(solution)/shard_map/ppermute | solution.py:17
  320.2 0.0 collective-permute-start.7
  320.2 2.8 collective-permute-done.11.refs_2_
  323.0 0.8 collective-permute-start.8
  323.8 0.0 copy-done
  323.8 5.8 %totals.2 = (bf16[512,2048]{1,0:T(8,128)(2,1)}, bf16[512,2048]{1,0:T(8,128)(2,1)}) custom-call(f32[2,8,512,256]{3,2,1,0:T(8,128)} %get-tuple-element.29.acc_ref, bf16[2,512,1024]{2,1,0:T(8,128)(2,1)} %copy-done, bf16[2,512,1024]{2,1,0:T(8,128)(2,1)} %collective-permute-done.10.refs_1_, bf16[2,512,1024]{2,1,0:T(8,128)(2,1)} %collective-permute-done.11.refs_2_), custom_call_target="tpu_custom_call" | custom-call | flops 3145728 | bytes 12582912 | tf_op jit(solution)/shard_map/totals/pallas_call | solution.py:265
  329.6 0.0 collective-permute-done.6.refs_0_
  329.6 83.0 %collective-permute-done.7.refs_1_ = bf16[2,512,1024]{2,1,0:T(8,128)(2,1)} collective-permute-done((bf16[2,512,1024]{2,1,0:T(8,128)(2,1)}, bf16[2,512,1024]{2,1,0:T(8,128)(2,1)}, u32[]{:S(2)}, u32[]{:S(2)}) %collective-permute-start.7) | collective-permute-done | bytes 2097184 | tf_op jit(solution)/shard_map/ppermute | solution.py:17
  412.6 1.3 collective-permute-done.8.refs_2_
  413.9 5.8 %totals.3 = (bf16[512,2048]{1,0:T(8,128)(2,1)}, bf16[512,2048]{1,0:T(8,128)(2,1)}) custom-call(f32[2,8,512,256]{3,2,1,0:T(8,128)} %get-tuple-element.29.acc_ref, bf16[2,512,1024]{2,1,0:T(8,128)(2,1)} %collective-permute-done.6.refs_0_, bf16[2,512,1024]{2,1,0:T(8,128)(2,1)} %collective-permute-done.7.refs_1_, ...), custom_call_target="tpu_custom_call", output_to_operand_aliasing={{0}: (4, {}), {1}: (5, {})} | custom-call | flops 3145728 | bytes 12582912 | tf_op jit(solution)/shard_map/totals/pallas_call | solution.py:265
  419.7 0.0 collective-permute-done.15.recv_ref
  419.7 5.7 %grads.2 = (f32[2,32,64,256]{3,2,1,0:T(8,128)}, f32[2,32,64,256]{3,2,1,0:T(8,128)}) custom-call(f32[16,1,2,2,64,256]{5,4,3,2,1,0:T(8,128)} %get-tuple-element.46.keep_ref, f32[16,1,2,2,64,256]{5,4,3,2,1,0:T(8,128)} %collective-permute-done.15.recv_ref), custom_call_target="tpu_custom_call" | custom-call | flops 1048576 | bytes 12582912 | tf_op jit(solution)/shard_map/grads/pallas_call | solution.py:235
  425.4 0.0 collective-permute-done.13.recv_ref
  425.5 5.8 %grads.3 = (f32[2,32,64,256]{3,2,1,0:T(8,128)}, f32[2,32,64,256]{3,2,1,0:T(8,128)}) custom-call(f32[16,1,2,2,64,256]{5,4,3,2,1,0:T(8,128)} %get-tuple-element.42.keep_ref, f32[16,1,2,2,64,256]{5,4,3,2,1,0:T(8,128)} %collective-permute-done.13.recv_ref, f32[2,32,64,256]{3,2,1,0:T(8,128)} %get-tuple-element.48.refs_0_, ...), custom_call_target="tpu_custom_call", output_to_operand_aliasing={{0}: (2, {}), {1}: (3, {})} | custom-call | flops 1048576 | bytes 12582912 | tf_op jit(solution)/shard_map/grads/pallas_call | solution.py:235
  (1 shorter events, 0.0 us)
Async XLA Ops:
  4.8 96.6 %collective-permute-start.5 = (bf16[2,512,1024]{2,1,0:T(8,128)(2,1)}, bf16[2,512,1024]{2,1,0:T(8,128)(2,1)S(1)}, u32[]{:S(2)}, u32[]{:S(2)}) collective-permute-start(bf16[2,512,1024]{2,1,0:T(8,128)(2,1)} %pad_maximum_fusion.1), channel_id=1, source_target_pairs={{0,4},{1,5},{2,6},{3,7},{4,0},{5,1},{6,2},{7,3},{8,12},{9,13},{10,... | collective-permute-start | bytes 6291464 | tf_op jit(solution)/shard_map/ppermute | solution.py:17
  8.8 95.9 %collective-permute-start.4 = (bf16[2,512,1024]{2,1,0:T(8,128)(2,1)}, bf16[2,512,1024]{2,1,0:T(8,128)(2,1)}, u32[]{:S(2)}, u32[]{:S(2)}) collective-permute-start(bf16[2,512,1024]{2,1,0:T(8,128)(2,1)} %pad_maximum_fusion.1), channel_id=1, source_target_pairs={{0,2},{1,3},{2,0},{3,1},{4,6},{5,7},{6,4},{7,5},{8,10},{9,11},{10,... | collective-permute-start | bytes 6291464 | tf_op jit(solution)/shard_map/ppermute | solution.py:17
  10.4 94.4 %collective-permute-start.3 = (bf16[2,512,1024]{2,1,0:T(8,128)(2,1)}, bf16[2,512,1024]{2,1,0:T(8,128)(2,1)}, u32[]{:S(2)}, u32[]{:S(2)}) collective-permute-start(bf16[2,512,1024]{2,1,0:T(8,128)(2,1)} %pad_maximum_fusion.1), channel_id=1, source_target_pairs={{0,1},{1,0},{2,3},{3,2},{4,5},{5,4},{6,7},{7,6},{8,9},{9,8},{10,11... | collective-permute-start | bytes 6291464 | tf_op jit(solution)/shard_map/ppermute | solution.py:17
  11.9 91.5 %copy-start.1 = (s32[2,32]{1,0:T(2,128)S(1)}, s32[2,32]{1,0:T(2,128)}, u32[]{:S(2)}) copy-start(s32[2,32]{1,0:T(2,128)} %param.9) | copy-start | bytes 772
  12.1 177.6 %collective-permute-start.2 = (bf16[2,512,1024]{2,1,0:T(8,128)(2,1)S(1)}, bf16[2,512,1024]{2,1,0:T(8,128)(2,1)}, u32[]{:S(2)}, u32[]{:S(2)}) collective-permute-start(bf16[2,512,1024]{2,1,0:T(8,128)(2,1)S(1)} %pad_maximum_fusion), channel_id=1, source_target_pairs={{0,4},{1,5},{2,6},{3,7},{4,0},{5,1},{6,2},{7,3},{8,12},{9,13},{10,... | collective-permute-start | bytes 6291464 | tf_op jit(solution)/shard_map/ppermute | solution.py:17
  12.5 177.4 %collective-permute-start.1 = (bf16[2,512,1024]{2,1,0:T(8,128)(2,1)S(1)}, bf16[2,512,1024]{2,1,0:T(8,128)(2,1)}, u32[]{:S(2)}, u32[]{:S(2)}) collective-permute-start(bf16[2,512,1024]{2,1,0:T(8,128)(2,1)S(1)} %pad_maximum_fusion), channel_id=1, source_target_pairs={{0,2},{1,3},{2,0},{3,1},{4,6},{5,7},{6,4},{7,5},{8,10},{9,11},{10,... | collective-permute-start | bytes 6291464 | tf_op jit(solution)/shard_map/ppermute | solution.py:17
  101.4 2.0 copy-start.2
  101.4 88.5 %collective-permute-start = (bf16[2,512,1024]{2,1,0:T(8,128)(2,1)S(1)}, bf16[2,512,1024]{2,1,0:T(8,128)(2,1)}, u32[]{:S(2)}, u32[]{:S(2)}) collective-permute-start(bf16[2,512,1024]{2,1,0:T(8,128)(2,1)S(1)} %pad_maximum_fusion), channel_id=1, source_target_pairs={{0,1},{1,0},{2,3},{3,2},{4,5},{5,4},{6,7},{7,6},{8,9},{9,8},{10,11... | collective-permute-start | bytes 6291464 | tf_op jit(solution)/shard_map/ppermute | solution.py:17
  138.6 93.1 %collective-permute-start.14 = (f32[16,2,2,2,64,256]{5,4,3,2,1,0:T(8,128)}, f32[16,2,2,2,64,256]{5,4,3,2,1,0:T(8,128)}, u32[]{:S(2)}, u32[]{:S(2)}) collective-permute-start(f32[16,2,2,2,64,256]{5,4,3,2,1,0:T(8,128)} %get-tuple-element.45), channel_id=1, source_target_pairs={{0,8},{8,0},{16,24},{24,16},{1,9},{9,1},{17,25},{25,17},{2,10},{10... | collective-permute-start | bytes 25165832 | tf_op jit(solution)/shard_map/ppermute | solution.py:17
  226.2 16.0 %collective-permute-start.12 = (f32[16,2,2,2,64,256]{5,4,3,2,1,0:T(8,128)}, f32[16,2,2,2,64,256]{5,4,3,2,1,0:T(8,128)}, u32[]{:S(2)}, u32[]{:S(2)}) collective-permute-start(f32[16,2,2,2,64,256]{5,4,3,2,1,0:T(8,128)} %get-tuple-element.41), channel_id=1, source_target_pairs={{0,8},{8,0},{16,24},{24,16},{1,9},{9,1},{17,25},{25,17},{2,10},{10... | collective-permute-start | bytes 25165832 | tf_op jit(solution)/shard_map/ppermute | solution.py:17
  226.3 48.2 %collective-permute-start.9 = (bf16[2,512,1024]{2,1,0:T(8,128)(2,1)}, bf16[2,512,1024]{2,1,0:T(8,128)(2,1)S(1)}, u32[]{:S(2)}, u32[]{:S(2)}) collective-permute-start(bf16[2,512,1024]{2,1,0:T(8,128)(2,1)} %get-tuple-element.33), channel_id=1, source_target_pairs={{0,1},{1,0},{2,3},{3,2},{4,5},{5,4},{6,7},{7,6},{8,9},{9,8},{10,11... | collective-permute-start | bytes 6291464 | tf_op jit(solution)/shard_map/ppermute | solution.py:17
  227.9 92.4 %collective-permute-start.10 = (bf16[2,512,1024]{2,1,0:T(8,128)(2,1)}, bf16[2,512,1024]{2,1,0:T(8,128)(2,1)}, u32[]{:S(2)}, u32[]{:S(2)}) collective-permute-start(bf16[2,512,1024]{2,1,0:T(8,128)(2,1)} %get-tuple-element.34), channel_id=1, source_target_pairs={{0,2},{1,3},{2,0},{3,1},{4,6},{5,7},{6,4},{7,5},{8,10},{9,11},{10,... | collective-permute-start | bytes 6291464 | tf_op jit(solution)/shard_map/ppermute | solution.py:17
  229.4 93.6 %collective-permute-start.11 = (bf16[2,512,1024]{2,1,0:T(8,128)(2,1)}, bf16[2,512,1024]{2,1,0:T(8,128)(2,1)}, u32[]{:S(2)}, u32[]{:S(2)}) collective-permute-start(bf16[2,512,1024]{2,1,0:T(8,128)(2,1)} %get-tuple-element.35), channel_id=1, source_target_pairs={{0,4},{1,5},{2,6},{3,7},{4,0},{5,1},{6,2},{7,3},{8,12},{9,13},{10,... | collective-permute-start | bytes 6291464 | tf_op jit(solution)/shard_map/ppermute | solution.py:17
  240.6 179.1 %collective-permute-start.15 = (f32[16,1,2,2,64,256]{5,4,3,2,1,0:T(8,128)}, f32[16,1,2,2,64,256]{5,4,3,2,1,0:T(8,128)}, u32[]{:S(2)}, u32[]{:S(2)}) collective-permute-start(f32[16,1,2,2,64,256]{5,4,3,2,1,0:T(8,128)} %get-tuple-element.47), channel_id=1, source_target_pairs={{0,16},{8,24},{16,0},{24,8},{1,17},{9,25},{17,1},{25,9},{2,18},{10... | collective-permute-start | bytes 12582920 | tf_op jit(solution)/shard_map/ppermute | solution.py:17
  251.1 174.3 %collective-permute-start.13 = (f32[16,1,2,2,64,256]{5,4,3,2,1,0:T(8,128)}, f32[16,1,2,2,64,256]{5,4,3,2,1,0:T(8,128)}, u32[]{:S(2)}, u32[]{:S(2)}) collective-permute-start(f32[16,1,2,2,64,256]{5,4,3,2,1,0:T(8,128)} %get-tuple-element.43), channel_id=1, source_target_pairs={{0,16},{8,24},{16,0},{24,8},{1,17},{9,25},{17,1},{25,9},{2,18},{10... | collective-permute-start | bytes 12582920 | tf_op jit(solution)/shard_map/ppermute | solution.py:17
  274.5 49.3 %copy-start = (bf16[2,512,1024]{2,1,0:T(8,128)(2,1)}, bf16[2,512,1024]{2,1,0:T(8,128)(2,1)S(1)}, u32[]{:S(2)}) copy-start(bf16[2,512,1024]{2,1,0:T(8,128)(2,1)S(1)} %collective-permute-done.9.refs_0_) | copy-start | bytes 6291460
  274.5 55.1 %collective-permute-start.6 = (bf16[2,512,1024]{2,1,0:T(8,128)(2,1)}, bf16[2,512,1024]{2,1,0:T(8,128)(2,1)}, u32[]{:S(2)}, u32[]{:S(2)}) collective-permute-start(bf16[2,512,1024]{2,1,0:T(8,128)(2,1)} %get-tuple-element.30), channel_id=1, source_target_pairs={{0,1},{1,0},{2,3},{3,2},{4,5},{5,4},{6,7},{7,6},{8,9},{9,8},{10,11... | collective-permute-start | bytes 6291464 | tf_op jit(solution)/shard_map/ppermute | solution.py:17
  320.2 92.4 %collective-permute-start.7 = (bf16[2,512,1024]{2,1,0:T(8,128)(2,1)}, bf16[2,512,1024]{2,1,0:T(8,128)(2,1)}, u32[]{:S(2)}, u32[]{:S(2)}) collective-permute-start(bf16[2,512,1024]{2,1,0:T(8,128)(2,1)} %get-tuple-element.31), channel_id=1, source_target_pairs={{0,2},{1,3},{2,0},{3,1},{4,6},{5,7},{6,4},{7,5},{8,10},{9,11},{10,... | collective-permute-start | bytes 6291464 | tf_op jit(solution)/shard_map/ppermute | solution.py:17
  323.0 90.9 %collective-permute-start.8 = (bf16[2,512,1024]{2,1,0:T(8,128)(2,1)}, bf16[2,512,1024]{2,1,0:T(8,128)(2,1)}, u32[]{:S(2)}, u32[]{:S(2)}) collective-permute-start(bf16[2,512,1024]{2,1,0:T(8,128)(2,1)} %get-tuple-element.32), channel_id=1, source_target_pairs={{0,4},{1,5},{2,6},{3,7},{4,0},{5,1},{6,2},{7,3},{8,12},{9,13},{10,... | collective-permute-start | bytes 6291464 | tf_op jit(solution)/shard_map/ppermute | solution.py:17

commit v2 on v1

--- a/solution.py
+++ b/solution.py
@@ -8,7 +8,15 @@
 from jax.sharding import PartitionSpec as P
 
 
-GROUPS = 2
+PIECES = 8
+
+
+def row_groups(local):
+    if local < PIECES:
+        return [1] * local
+    unit = local // PIECES
+    sizes = [unit] + [2 * unit] * (PIECES // 2 - 1)
+    return sizes + [local - sum(sizes)]
 
 
 def partner(value, axis, distance):
@@ -34,6 +42,26 @@
 
 def dot_tn(left, right):
     return lax.dot_general(left, right, (((0,), (0,)), ((), ())), preferred_element_type=jnp.float32)
+
+
+def pack_body(x_ref, g_ref, pair_ref):
+    pair_ref[0] = x_ref[...]
+    pair_ref[1] = g_ref[...]
+
+
+def pack_call(start, rows, width, inputs, out_grad):
+    tokens = inputs.shape[0]
+    column = pl.BlockSpec((tokens, width), lambda i: (0, start + i))
+    size = 2 * tokens * rows * width
+    return pl.pallas_call(
+        pack_body,
+        grid=(rows,),
+        in_specs=[column, column],
+        out_specs=pl.BlockSpec((2, tokens, width), lambda i: (0, 0, i)),
+        out_shape=jax.ShapeDtypeStruct((2, tokens, rows * width), inputs.dtype),
+        cost_estimate=pl.CostEstimate(flops=0, bytes_accessed=4 * size, transcendentals=0),
+        name="pack",
+    )(inputs, out_grad)
 
 
 def main_body(dims, slots_ref, parity_ref, *refs):
@@ -136,14 +164,14 @@
             copy.wait()
 
 
-def main_call(group, rows, slots, parity, inputs, out_grad, arrived, prior, w_up, w_down, halves):
+def main_call(start, rows, slots, parity, inputs, out_grad, arrived, prior, w_up, w_down, halves):
     tokens, features = inputs.shape
     slot_kinds, columns, width, _ = w_up.shape
     local = features // width
     bits = len(arrived)
     cols = columns * rows // local
     slot_count = local + bits * rows
-    first = group * cols
+    first = start * columns // local
     has_prior = prior is not None
     piece = width // (2 * halves)
     dims = (local, bits, rows, width, slot_count, halves, first, has_prior)
@@ -200,7 +228,7 @@
 
 def halve_call(parity, keep, recv):
     cols, halves, pair, slot_kinds, piece, width = keep.shape
-    block = cols // 4 if cols % 4 == 0 else cols
+    block = min(4, cols)
     spec = pl.BlockSpec((block, halves, pair, slot_kinds, piece, width), lambda i, *_: (i, 0, 0, 0, 0, 0))
     half_shape = (cols, halves // 2, pair, slot_kinds, piece, width)
     half_spec = pl.BlockSpec((block,) + half_shape[1:], lambda i, *_: (i, 0, 0, 0, 0, 0))
@@ -225,10 +253,10 @@
             ref[slot] = keep_ref[:, 0, which, slot] + recv_ref[:, 0, which, slot]
 
 
-def grads_call(group, columns, keep, recv, prior):
+def grads_call(start, columns, keep, recv, prior):
     cols, _, pair, slot_kinds, piece, width = keep.shape
-    block = cols // 4 if cols % 4 == 0 else cols
-    first = group * (cols // block)
+    block = min(4, cols)
+    first = start // block
     spec = pl.BlockSpec((block, 1, pair, slot_kinds, piece, width), lambda i: (i, 0, 0, 0, 0, 0))
     out_spec = pl.BlockSpec((slot_kinds, block, piece, width), lambda i: (0, first + i, 0, 0))
     out_shape = jax.ShapeDtypeStruct((slot_kinds, columns, piece, width), jnp.float32)
@@ -253,18 +281,18 @@
         out_refs[kind][...] = total.astype(jnp.bfloat16)
 
 
-def total_call(group, rows, acc, arrived, prior):
+def total_call(start, rows, acc, arrived, prior):
     _, local, tokens, width = acc.shape
     bits = len(arrived)
-    first = group * rows
-    acc_spec = pl.BlockSpec((2, 1, tokens, width), lambda i: (0, first + i, 0, 0))
-    recv_spec = pl.BlockSpec((2, tokens, width), lambda i: (0, 0, i))
-    out_spec = pl.BlockSpec((tokens, width), lambda i: (0, first + i))
+    tile = tokens // 2
+    acc_spec = pl.BlockSpec((2, 1, tile, width), lambda i, t: (0, start + i, t, 0))
+    recv_spec = pl.BlockSpec((2, tile, width), lambda i, t: (0, t, i))
+    out_spec = pl.BlockSpec((tile, width), lambda i, t: (t, start + i))
     out_shape = jax.ShapeDtypeStruct((tokens, local * width), jnp.bfloat16)
     size = 2 * rows * tokens * width
     return pl.pallas_call(
         functools.partial(total_body, bits),
-        grid=(rows,),
+        grid=(rows, 2),
         in_specs=[acc_spec] + [recv_spec] * bits + [pl.BlockSpec(memory_space=pl.ANY)] * len(prior),
         out_specs=[out_spec, out_spec],
         out_shape=[out_shape, out_shape],
@@ -280,9 +308,9 @@
     local = features // width
     bits = lax.axis_size("mp").bit_length() - 1
     dp_bits = lax.axis_size("dp").bit_length() - 1
-    group_count = min(GROUPS, local)
-    rows = local // group_count
-    cols = columns // group_count
+    sizes = row_groups(local)
+    starts = [sum(sizes[:group]) for group in range(len(sizes))]
+    per_row = columns // local
     device = lax.axis_index("mp")
     dp_index = lax.axis_index("dp")
 
@@ -291,22 +319,22 @@
     level = jnp.zeros_like(distance)
     for bit in range(1, bits):
         level = level + (distance >= 1 << bit).astype(jnp.int32)
-    slot = jnp.where(distance == 0, within, local + level * rows + within % rows)
+    is_local = distance == 0
     parities = [(dp_index // 2**bit % 2).reshape(1).astype(jnp.int32) for bit in range(dp_bits)]
 
     arrived = []
-    for group in range(group_count):
-        lanes = slice(group * rows * width, (group + 1) * rows * width)
-        pair = jnp.stack([inputs[:, lanes], out_grad[:, lanes]])
+    for start, rows in zip(starts, sizes):
+        pair = pack_call(start, rows, width, inputs, out_grad)
         arrived.append([partner(pair, "mp", bit) for bit in range(bits)])
 
     acc = None
     returned = []
     kept = []
-    for group in range(group_count):
-        slots = slot[:, group * cols : (group + 1) * cols].reshape(-1)
+    for group, (start, rows) in enumerate(zip(starts, sizes)):
+        slot = jnp.where(is_local, within, local + level * rows + within - start)
+        slots = slot[:, start * per_row : (start + rows) * per_row].reshape(-1)
         acc, *rest = main_call(
-            group, rows, slots, parities[0], inputs, out_grad, arrived[group], acc, w_up, w_down,
+            start, rows, slots, parities[0], inputs, out_grad, arrived[group], acc, w_up, w_down,
             2 ** (dp_bits - 1),
         )
         returned.append([partner(rest[bit], "mp", bit) for bit in range(bits)])
@@ -317,11 +345,11 @@
         kept.append((keep, partner(send, "dp", dp_bits - 1)))
 
     grads = []
-    for group in range(group_count):
-        grads = grads_call(group, columns, *kept[group], grads)
+    for group, start in enumerate(starts):
+        grads = grads_call(start * per_row, columns, *kept[group], grads)
     totals = []
-    for group in range(group_count):
-        totals = total_call(group, rows, acc, returned[group], totals)
+    for group, (start, rows) in enumerate(zip(starts, sizes)):
+        totals = total_call(start, rows, acc, returned[group], totals)
     return (*totals, *grads)
 
 

time: 433 us -> 578 us (1.33)
  waiting for transfers between devices: 294 us -> 357 us
  Pallas kernels: 111 us -> 168 us
  starting transfers between devices: 19.9 us -> 41.9 us
    ppermute x16 -> x40, waiting for transfers between devices: 294 us -> 357 us  [partner(): return lax.ppermute(value, axis, pairs)]
    pallas_call x2 -> x5, Pallas kernels: 70.1 us -> 103 us  [main_call(): pl.pallas_call(functools.partial(main_body, dims), grid_spec=pltpu.Prefet...]
    ppermute x16 -> x40, starting transfers between devices: 19.9 us -> 41.9 us  [partner(): return lax.ppermute(value, axis, pairs)]
    pallas_call x2 -> x10, Pallas kernels: 11.6 us -> 27.5 us  [the longest x5 17.6 us: total_call(): pl.pallas_call(functools.partial(total_body, bits), grid=(rows, 2), in_sp...]
    pallas_call x2 -> x5, Pallas kernels: 17.9 us -> 22.9 us  [halve_call(): pl.pallas_call(halve_body, grid_spec=pltpu.PrefetchScalarGridSpec(num_sca...]
    pallas_call x2 -> x5, Pallas kernels: 11.6 us -> 15 us  [grads_call(): pl.pallas_call(grads_body, grid=(cols // block,), in_specs=[spec, spec] +...]
  transfers between devices with their start and end apart: 16 -> 40, of which waited for: 8 -> 16; matrix products, arithmetic and copies ran while one was open for 0% -> 1% of each run, Pallas kernels for 24% -> 28%
where the time goes in v2:
time: 578 us; the launch traced here: 577 us
  waiting for transfers between devices  357 us (62%)
  Pallas kernels  168 us (29%)
  starting transfers between devices  41.9 us (7%)
  local copies, waits for them, and re-layouts  8.92 us (2%)
    ppermute x40, waiting for transfers between devices, partner(): return lax.ppermute(value, axis, pairs)  357 us
    pallas_call x5, Pallas kernels, main_call(): pl.pallas_call(functools.partial(main_body, dims), grid_spec=pltpu.Prefet...  103 us
    ppermute x40, starting transfers between devices, partner(): return lax.ppermute(value, axis, pairs)  41.9 us
    pallas_call x5, Pallas kernels, halve_call(): pl.pallas_call(halve_body, grid_spec=pltpu.PrefetchScalarGridSpec(num_sca...  22.9 us
    pallas_call x5, Pallas kernels, total_call(): pl.pallas_call(functools.partial(total_body, bits), grid=(rows, 2), in_sp...  17.6 us
    pallas_call x5, Pallas kernels, grads_call(): pl.pallas_call(grads_body, grid=(cols // block,), in_specs=[spec, spec] +...  15 us
  transfers between devices with their start and end apart: 40, of which 16 were waited for; matrix products, arithmetic and copies ran while one was open for 1% of the time, Pallas kernels for 28%

profile of v2, /device:TPU:0, one launch (start us, length us, event | category | flops | bytes accessed | tf_op | source)
XLA Modules:
  0.0 576.5 jit_solution(1967913192024960826)
XLA Ops:
  0.6 2.1 pack.8
  2.7 3.1 collective-permute-start.10
  5.7 1.9 pack.9
  7.6 1.5 collective-permute-start.12
  9.5 2.6 collective-permute-start.14
  12.5 2.1 pack.7
  14.5 6.7 %collective-permute-done.12.refs_2_ = bf16[2,512,256]{2,1,0:T(8,128)(2,1)S(1)} collective-permute-done((bf16[2,512,256]{2,1,0:T(8,128)(2,1)}, bf16[2,512,256]{2,1,0:T(8,128)(2,1)S(1)}, u32[]{:S(2)}, u32[]{:S(2)}) %collective-permute-start.12) | collective-permute-done | bytes 524320 | tf_op jit(solution)/shard_map/ppermute | solution.py:25
  21.2 1.5 collective-permute-start.9
  22.7 48.1 %collective-permute-done.13.refs_3_ = bf16[2,512,256]{2,1,0:T(8,128)(2,1)} collective-permute-done((bf16[2,512,256]{2,1,0:T(8,128)(2,1)}, bf16[2,512,256]{2,1,0:T(8,128)(2,1)}, u32[]{:S(2)}, u32[]{:S(2)}) %collective-permute-start.13) | collective-permute-done | bytes 524320 | tf_op jit(solution)/shard_map/ppermute | solution.py:25
  70.8 2.7 collective-permute-start.6
  73.4 2.0 pack.6
  75.5 1.9 pack.5
  78.0 1.9 collective-permute-start.8
  82.7 14.8 %columns.5 = (f32[2,8,512,256]{3,2,1,0:T(8,128)}, bf16[2,512,256]{2,1,0:T(8,128)(2,1)}, bf16[2,512,256]{2,1,0:T(8,128)(2,1)}, bf16[2,512,256]{2,1,0:T(8,128)(2,1...) custom-call(s32[8]{0:T(128)} %reshape.34.slots_ref, s32[1]{0:T(128)} %bitcast.parity_ref, ...), custom_call_target="tpu_custom_call" | custom-call | flops 3221225472 | bytes 23592960 | tf_op jit(solution)/shard_map/columns/pallas_call | solution.py:185
  98.0 2.8 collective-permute-start.5
  100.8 23.4 %columns.6 = (f32[2,8,512,256]{3,2,1,0:T(8,128)}, bf16[2,512,512]{2,1,0:T(8,128)(2,1)}, bf16[2,512,512]{2,1,0:T(8,128)(2,1)}, bf16[2,512,512]{2,1,0:T(8,128)(2,1...) custom-call(s32[16]{0:T(128)} %reshape.33.slots_ref, s32[1]{0:T(128)} %bitcast.parity_ref, ...), custom_call_target="tpu_custom_call" | custom-call | flops 6442450944 | bytes 34603008 | tf_op jit(solution)/shard_map/columns/pallas_call | solution.py:185
  124.2 2.0 collective-permute-done.7.refs_3_
  126.2 1.7 collective-permute-done.8.refs_4_
  127.9 23.5 %columns.7 = (f32[2,8,512,256]{3,2,1,0:T(8,128)}, bf16[2,512,512]{2,1,0:T(8,128)(2,1)}, bf16[2,512,512]{2,1,0:T(8,128)(2,1)}, bf16[2,512,512]{2,1,0:T(8,128)(2,1...) custom-call(s32[16]{0:T(128)} %reshape.32.slots_ref, s32[1]{0:T(128)} %bitcast.parity_ref, ...), custom_call_target="tpu_custom_call" | custom-call | flops 6442450944 | bytes 34603008 | tf_op jit(solution)/shard_map/columns/pallas_call | solution.py:185
  151.4 2.7 collective-permute-start.2
  154.0 17.1 %collective-permute-done.4.refs_3_ = bf16[2,512,512]{2,1,0:T(8,128)(2,1)} collective-permute-done((bf16[2,512,512]{2,1,0:T(8,128)(2,1)S(1)}, bf16[2,512,512]{2,1,0:T(8,128)(2,1)}, u32[]{:S(2)}, u32[]{:S(2)}) %collective-permute-start.4) | collective-permute-done | bytes 1048608 | tf_op jit(solution)/shard_map/ppermute | solution.py:25
  171.1 0.8 collective-permute-done.5.refs_4_
  172.0 23.8 %columns.8 = (f32[2,8,512,256]{3,2,1,0:T(8,128)}, bf16[2,512,512]{2,1,0:T(8,128)(2,1)}, bf16[2,512,512]{2,1,0:T(8,128)(2,1)}, bf16[2,512,512]{2,1,0:T(8,128)(2,1...) custom-call(s32[16]{0:T(128)} %reshape.31.slots_ref, s32[1]{0:T(128)} %bitcast.parity_ref, ...), custom_call_target="tpu_custom_call" | custom-call | flops 6442450944 | bytes 34603008 | tf_op jit(solution)/shard_map/columns/pallas_call | solution.py:185
  195.9 3.5 collective-permute-start.29
  199.4 0.8 copy-done.16
  200.4 17.1 %columns.9 = (f32[2,8,512,256]{3,2,1,0:T(8,128)}, bf16[2,512,256]{2,1,0:T(8,128)(2,1)}, bf16[2,512,256]{2,1,0:T(8,128)(2,1)}, bf16[2,512,256]{2,1,0:T(8,128)(2,1...) custom-call(s32[8]{0:T(128)} %reshape.29.slots_ref, s32[1]{0:T(128)} %bitcast.parity_ref, ...), custom_call_target="tpu_custom_call" | custom-call | flops 3221225472 | bytes 23592960 | tf_op jit(solution)/shard_map/columns/pallas_call | solution.py:185
  217.5 0.8 collective-permute-start.15
  218.3 1.3 collective-permute-start.24
  219.7 1.4 collective-permute-done.29.refs_2_
  221.7 10.9 %collective-permute-done.15.refs_0_ = bf16[2,512,256]{2,1,0:T(8,128)(2,1)S(1)} collective-permute-done((bf16[2,512,256]{2,1,0:T(8,128)(2,1)}, bf16[2,512,256]{2,1,0:T(8,128)(2,1)S(1)}, u32[]{:S(2)}, u32[]{:S(2)}) %collective-permute-start.15) | collective-permute-done | bytes 524320 | tf_op jit(solution)/shard_map/ppermute | solution.py:25
  232.6 33.3 %collective-permute-done.16.refs_1_ = bf16[2,512,256]{2,1,0:T(8,128)(2,1)S(1)} collective-permute-done((bf16[2,512,256]{2,1,0:T(8,128)(2,1)}, bf16[2,512,256]{2,1,0:T(8,128)(2,1)S(1)}, u32[]{:S(2)}, u32[]{:S(2)}) %collective-permute-start.16) | collective-permute-done | bytes 524320 | tf_op jit(solution)/shard_map/ppermute | solution.py:25
  265.9 0.8 copy-done.19
  268.1 1.7 collective-permute-start.21
  269.8 43.2 %collective-permute-done.26.refs_2_ = bf16[2,512,512]{2,1,0:T(8,128)(2,1)S(1)} collective-permute-done((bf16[2,512,512]{2,1,0:T(8,128)(2,1)}, bf16[2,512,512]{2,1,0:T(8,128)(2,1)S(1)}, u32[]{:S(2)}, u32[]{:S(2)}) %collective-permute-start.26) | collective-permute-done | bytes 1048608 | tf_op jit(solution)/shard_map/ppermute | solution.py:25
  313.3 3.3 collective-permute-start.23
  316.6 42.8 %collective-permute-done.22.refs_1_ = bf16[2,512,512]{2,1,0:T(8,128)(2,1)S(1)} collective-permute-done((bf16[2,512,512]{2,1,0:T(8,128)(2,1)}, bf16[2,512,512]{2,1,0:T(8,128)(2,1)S(1)}, u32[]{:S(2)}, u32[]{:S(2)}) %collective-permute-start.22) | collective-permute-done | bytes 1048608 | tf_op jit(solution)/shard_map/ppermute | solution.py:25
  359.3 3.1 collective-permute-start.18
  362.5 21.9 %collective-permute-done.18.refs_0_ = bf16[2,512,512]{2,1,0:T(8,128)(2,1)S(1)} collective-permute-done((bf16[2,512,512]{2,1,0:T(8,128)(2,1)}, bf16[2,512,512]{2,1,0:T(8,128)(2,1)S(1)}, u32[]{:S(2)}, u32[]{:S(2)}) %collective-permute-start.18) | collective-permute-done | bytes 1048608 | tf_op jit(solution)/shard_map/ppermute | solution.py:25
  384.5 0.8 copy-done.13
  385.3 5.1 halve.8
  390.4 1.4 collective-permute-start.37
  391.8 5.1 halve.7
  397.5 5.2 halve.6
  402.7 7.6 %collective-permute-done.19.refs_1_ = bf16[2,512,512]{2,1,0:T(8,128)(2,1)S(1)} collective-permute-done((bf16[2,512,512]{2,1,0:T(8,128)(2,1)}, bf16[2,512,512]{2,1,0:T(8,128)(2,1)S(1)}, u32[]{:S(2)}, u32[]{:S(2)}) %collective-permute-start.19) | collective-permute-done | bytes 1048608 | tf_op jit(solution)/shard_map/ppermute | solution.py:25
  410.3 1.4 collective-permute-start.33
  411.8 1.4 collective-permute-start.20
  413.1 3.7 halve.9
  416.9 0.7 collective-permute-start.39
  418.2 3.8 halve.5
  422.0 37.2 %collective-permute-done.20.refs_2_ = bf16[2,512,512]{2,1,0:T(8,128)(2,1)} collective-permute-done((bf16[2,512,512]{2,1,0:T(8,128)(2,1)}, bf16[2,512,512]{2,1,0:T(8,128)(2,1)}, u32[]{:S(2)}, u32[]{:S(2)}) %collective-permute-start.20) | collective-permute-done | bytes 1048608 | tf_op jit(solution)/shard_map/ppermute | solution.py:25
  459.8 2.4 totals.5
  462.2 4.2 totals.6
  466.5 4.2 totals.7
  470.7 4.2 totals.8
  474.9 2.5 totals.9
  477.4 74.1 %collective-permute-done.39.recv_ref = f32[4,1,2,2,64,256]{5,4,3,2,1,0:T(8,128)S(1)} collective-permute-done((f32[4,1,2,2,64,256]{5,4,3,2,1,0:T(8,128)}, f32[4,1,2,2,64,256]{5,4,3,2,1,0:T(8,128)S(1)}, u32[]{:S(2)}, u32[]{:S(2)}) %collective-permute-start.39) | collective-permute-done | bytes 1048608 | tf_op jit(solution)/shard_map/ppermute | solution.py:25
  551.5 1.0 copy-done.6
  552.4 2.6 grads.5
  555.1 3.3 grads.6
  558.3 3.3 grads.7
  561.6 3.3 grads.8
  564.9 8.1 %collective-permute-done.31.recv_ref = f32[4,1,2,2,64,256]{5,4,3,2,1,0:T(8,128)S(1)} collective-permute-done((f32[4,1,2,2,64,256]{5,4,3,2,1,0:T(8,128)}, f32[4,1,2,2,64,256]{5,4,3,2,1,0:T(8,128)S(1)}, u32[]{:S(2)}, u32[]{:S(2)}) %collective-permute-start.31) | collective-permute-done | bytes 1048608 | tf_op jit(solution)/shard_map/ppermute | solution.py:25
  572.9 1.0 copy-done.4
  573.9 2.6 grads.9
  (106 shorter events, 9.3 us)
Async XLA Ops:
  2.7 75.3 %collective-permute-start.10 = (bf16[2,512,512]{2,1,0:T(8,128)(2,1)}, bf16[2,512,512]{2,1,0:T(8,128)(2,1)S(1)}, u32[]{:S(2)}, u32[]{:S(2)}) collective-permute-start(bf16[2,512,512]{2,1,0:T(8,128)(2,1)} %pack.8), channel_id=1, source_target_pairs={{0,2},{1,3},{2,0},{3,1},{4,6},{5,7},{6,4},{7,5},{8,10},{9,11},{10,... | collective-permute-start | bytes 3145736 | tf_op jit(solution)/shard_map/ppermute | solution.py:25
  7.6 13.6 %collective-permute-start.12 = (bf16[2,512,256]{2,1,0:T(8,128)(2,1)}, bf16[2,512,256]{2,1,0:T(8,128)(2,1)S(1)}, u32[]{:S(2)}, u32[]{:S(2)}) collective-permute-start(bf16[2,512,256]{2,1,0:T(8,128)(2,1)} %pack.9), channel_id=1, source_target_pairs={{0,1},{1,0},{2,3},{3,2},{4,5},{5,4},{6,7},{7,6},{8,9},{9,8},{10,11... | collective-permute-start | bytes 1572872 | tf_op jit(solution)/shard_map/ppermute | solution.py:25
  9.1 61.7 %collective-permute-start.13 = (bf16[2,512,256]{2,1,0:T(8,128)(2,1)}, bf16[2,512,256]{2,1,0:T(8,128)(2,1)}, u32[]{:S(2)}, u32[]{:S(2)}) collective-permute-start(bf16[2,512,256]{2,1,0:T(8,128)(2,1)} %pack.9), channel_id=1, source_target_pairs={{0,2},{1,3},{2,0},{3,1},{4,6},{5,7},{6,4},{7,5},{8,10},{9,11},{10,... | collective-permute-start | bytes 1572872 | tf_op jit(solution)/shard_map/ppermute | solution.py:25
  9.5 68.4 %collective-permute-start.14 = (bf16[2,512,256]{2,1,0:T(8,128)(2,1)}, bf16[2,512,256]{2,1,0:T(8,128)(2,1)S(1)}, u32[]{:S(2)}, u32[]{:S(2)}) collective-permute-start(bf16[2,512,256]{2,1,0:T(8,128)(2,1)} %pack.9), channel_id=1, source_target_pairs={{0,4},{1,5},{2,6},{3,7},{4,0},{5,1},{6,2},{7,3},{8,12},{9,13},{10,... | collective-permute-start | bytes 1572872 | tf_op jit(solution)/shard_map/ppermute | solution.py:25
  12.1 85.4 %collective-permute-start.11 = (bf16[2,512,512]{2,1,0:T(8,128)(2,1)}, bf16[2,512,512]{2,1,0:T(8,128)(2,1)}, u32[]{:S(2)}, u32[]{:S(2)}) collective-permute-start(bf16[2,512,512]{2,1,0:T(8,128)(2,1)} %pack.8), channel_id=1, source_target_pairs={{0,4},{1,5},{2,6},{3,7},{4,0},{5,1},{6,2},{7,3},{8,12},{9,13},{10,... | collective-permute-start | bytes 3145736 | tf_op jit(solution)/shard_map/ppermute | solution.py:25
  21.2 1.5 copy-start.23
  21.2 76.5 %collective-permute-start.9 = (bf16[2,512,512]{2,1,0:T(8,128)(2,1)}, bf16[2,512,512]{2,1,0:T(8,128)(2,1)}, u32[]{:S(2)}, u32[]{:S(2)}) collective-permute-start(bf16[2,512,512]{2,1,0:T(8,128)(2,1)} %pack.8), channel_id=1, source_target_pairs={{0,1},{1,0},{2,3},{3,2},{4,5},{5,4},{6,7},{7,6},{8,9},{9,8},{10,11... | collective-permute-start | bytes 3145736 | tf_op jit(solution)/shard_map/ppermute | solution.py:25
  70.8 27.2 %collective-permute-start.6 = (bf16[2,512,512]{2,1,0:T(8,128)(2,1)}, bf16[2,512,512]{2,1,0:T(8,128)(2,1)S(1)}, u32[]{:S(2)}, u32[]{:S(2)}) collective-permute-start(bf16[2,512,512]{2,1,0:T(8,128)(2,1)} %pack.7), channel_id=1, source_target_pairs={{0,1},{1,0},{2,3},{3,2},{4,5},{5,4},{6,7},{7,6},{8,9},{9,8},{10,11... | collective-permute-start | bytes 3145736 | tf_op jit(solution)/shard_map/ppermute | solution.py:25
  75.5 1.9 copy-start.25
  78.0 4.7 copy-start.24
  78.0 48.2 %collective-permute-start.7 = (bf16[2,512,512]{2,1,0:T(8,128)(2,1)}, bf16[2,512,512]{2,1,0:T(8,128)(2,1)}, u32[]{:S(2)}, u32[]{:S(2)}) collective-permute-start(bf16[2,512,512]{2,1,0:T(8,128)(2,1)} %pack.7), channel_id=1, source_target_pairs={{0,2},{1,3},{2,0},{3,1},{4,6},{5,7},{6,4},{7,5},{8,10},{9,11},{10,... | collective-permute-start | bytes 3145736 | tf_op jit(solution)/shard_map/ppermute | solution.py:25
  78.0 19.6 %copy-start.1 = (bf16[2,512,512]{2,1,0:T(8,128)(2,1)}, bf16[2,512,512]{2,1,0:T(8,128)(2,1)S(1)}, u32[]{:S(2)}) copy-start(bf16[2,512,512]{2,1,0:T(8,128)(2,1)S(1)} %collective-permute-done.10.refs_3_) | copy-start | bytes 3145732
  78.0 49.9 %collective-permute-start.8 = (bf16[2,512,512]{2,1,0:T(8,128)(2,1)}, bf16[2,512,512]{2,1,0:T(8,128)(2,1)}, u32[]{:S(2)}, u32[]{:S(2)}) collective-permute-start(bf16[2,512,512]{2,1,0:T(8,128)(2,1)} %pack.7), channel_id=1, source_target_pairs={{0,4},{1,5},{2,6},{3,7},{4,0},{5,1},{6,2},{7,3},{8,12},{9,13},{10,... | collective-permute-start | bytes 3145736 | tf_op jit(solution)/shard_map/ppermute | solution.py:25
  82.7 14.9 %copy-start.3 = (bf16[2,512,512]{2,1,0:T(8,128)(2,1)S(1)}, bf16[2,512,512]{2,1,0:T(8,128)(2,1)}, u32[]{:S(2)}) copy-start(bf16[2,512,512]{2,1,0:T(8,128)(2,1)} %pack.6) | copy-start | bytes 3145732
  97.6 53.8 %collective-permute-start.3 = (bf16[2,512,512]{2,1,0:T(8,128)(2,1)S(1)}, bf16[2,512,512]{2,1,0:T(8,128)(2,1)S(1)}, u32[]{:S(2)}, u32[]{:S(2)}) collective-permute-start(bf16[2,512,512]{2,1,0:T(8,128)(2,1)S(1)} %copy-done.3), channel_id=1, source_target_pairs={{0,1},{1,0},{2,3},{3,2},{4,5},{5,4},{6,7},{7,6},{8,9},{9,8},{10,11... | collective-permute-start | bytes 3145736 | tf_op jit(solution)/shard_map/ppermute | solution.py:25
  97.7 73.5 %collective-permute-start.4 = (bf16[2,512,512]{2,1,0:T(8,128)(2,1)S(1)}, bf16[2,512,512]{2,1,0:T(8,128)(2,1)}, u32[]{:S(2)}, u32[]{:S(2)}) collective-permute-start(bf16[2,512,512]{2,1,0:T(8,128)(2,1)S(1)} %copy-done.3), channel_id=1, source_target_pairs={{0,2},{1,3},{2,0},{3,1},{4,6},{5,7},{6,4},{7,5},{8,10},{9,11},{10,... | collective-permute-start | bytes 3145736 | tf_op jit(solution)/shard_map/ppermute | solution.py:25
  98.0 26.1 %copy-start.2 = (bf16[2,512,512]{2,1,0:T(8,128)(2,1)}, bf16[2,512,512]{2,1,0:T(8,128)(2,1)S(1)}, u32[]{:S(2)}) copy-start(bf16[2,512,512]{2,1,0:T(8,128)(2,1)S(1)} %collective-permute-done.6.refs_2_) | copy-start | bytes 3145732
  98.0 74.0 %collective-permute-start.5 = (bf16[2,512,512]{2,1,0:T(8,128)(2,1)S(1)}, bf16[2,512,512]{2,1,0:T(8,128)(2,1)}, u32[]{:S(2)}, u32[]{:S(2)}) collective-permute-start(bf16[2,512,512]{2,1,0:T(8,128)(2,1)S(1)} %copy-done.3), channel_id=1, source_target_pairs={{0,4},{1,5},{2,6},{3,7},{4,0},{5,1},{6,2},{7,3},{8,12},{9,13},{10,... | collective-permute-start | bytes 3145736 | tf_op jit(solution)/shard_map/ppermute | solution.py:25
  126.2 69.6 %collective-permute-start = (bf16[2,512,256]{2,1,0:T(8,128)(2,1)}, bf16[2,512,256]{2,1,0:T(8,128)(2,1)S(1)}, u32[]{:S(2)}, u32[]{:S(2)}) collective-permute-start(bf16[2,512,256]{2,1,0:T(8,128)(2,1)} %pack.5), channel_id=1, source_target_pairs={{0,1},{1,0},{2,3},{3,2},{4,5},{5,4},{6,7},{7,6},{8,9},{9,8},{10,11... | collective-permute-start | bytes 1572872 | tf_op jit(solution)/shard_map/ppermute | solution.py:25
  127.9 71.5 %collective-permute-start.1 = (bf16[2,512,256]{2,1,0:T(8,128)(2,1)}, bf16[2,512,256]{2,1,0:T(8,128)(2,1)S(1)}, u32[]{:S(2)}, u32[]{:S(2)}) collective-permute-start(bf16[2,512,256]{2,1,0:T(8,128)(2,1)} %pack.5), channel_id=1, source_target_pairs={{0,2},{1,3},{2,0},{3,1},{4,6},{5,7},{6,4},{7,5},{8,10},{9,11},{10,... | collective-permute-start | bytes 1572872 | tf_op jit(solution)/shard_map/ppermute | solution.py:25
  151.4 20.6 %copy-start.5 = (bf16[2,512,512]{2,1,0:T(8,128)(2,1)}, bf16[2,512,512]{2,1,0:T(8,128)(2,1)S(1)}, u32[]{:S(2)}) copy-start(bf16[2,512,512]{2,1,0:T(8,128)(2,1)S(1)} %collective-permute-done.3.refs_2_) | copy-start | bytes 3145732
  151.4 48.0 %collective-permute-start.2 = (bf16[2,512,256]{2,1,0:T(8,128)(2,1)}, bf16[2,512,256]{2,1,0:T(8,128)(2,1)S(1)}, u32[]{:S(2)}, u32[]{:S(2)}) collective-permute-start(bf16[2,512,256]{2,1,0:T(8,128)(2,1)} %pack.5), channel_id=1, source_target_pairs={{0,4},{1,5},{2,6},{3,7},{4,0},{5,1},{6,2},{7,3},{8,12},{9,13},{10,... | collective-permute-start | bytes 1572872 | tf_op jit(solution)/shard_map/ppermute | solution.py:25
  171.1 48.4 %collective-permute-start.27 = (bf16[2,512,256]{2,1,0:T(8,128)(2,1)}, bf16[2,512,256]{2,1,0:T(8,128)(2,1)}, u32[]{:S(2)}, u32[]{:S(2)}) collective-permute-start(bf16[2,512,256]{2,1,0:T(8,128)(2,1)} %get-tuple-element.81), channel_id=1, source_target_pairs={{0,1},{1,0},{2,3},{3,2},{4,5},{5,4},{6,7},{7,6},{8,9},{9,8},{10,11... | collective-permute-start | bytes 1572872 | tf_op jit(solution)/shard_map/ppermute | solution.py:25
  172.0 47.6 %collective-permute-start.28 = (bf16[2,512,256]{2,1,0:T(8,128)(2,1)}, bf16[2,512,256]{2,1,0:T(8,128)(2,1)S(1)}, u32[]{:S(2)}, u32[]{:S(2)}) collective-permute-start(bf16[2,512,256]{2,1,0:T(8,128)(2,1)} %get-tuple-element.82), channel_id=1, source_target_pairs={{0,2},{1,3},{2,0},{3,1},{4,6},{5,7},{6,4},{7,5},{8,10},{9,11},{10,... | collective-permute-start | bytes 1572872 | tf_op jit(solution)/shard_map/ppermute | solution.py:25
  172.0 23.9 %copy-start.26 = (bf16[2,512,256]{2,1,0:T(8,128)(2,1)S(1)}, bf16[2,512,256]{2,1,0:T(8,128)(2,1)}, u32[]{:S(2)}) copy-start(bf16[2,512,256]{2,1,0:T(8,128)(2,1)} %get-tuple-element.83) | copy-start | bytes 1572868
  195.8 3.6 copy-start.15
  195.9 25.2 %collective-permute-start.29 = (bf16[2,512,256]{2,1,0:T(8,128)(2,1)S(1)}, bf16[2,512,256]{2,1,0:T(8,128)(2,1)S(1)}, u32[]{:S(2)}, u32[]{:S(2)}) collective-permute-start(bf16[2,512,256]{2,1,0:T(8,128)(2,1)S(1)} %copy-done.26), channel_id=1, source_target_pairs={{0,4},{1,5},{2,6},{3,7},{4,0},{5,1},{6,2},{7,3},{8,12},{9,13},{10,... | collective-permute-start | bytes 1572872 | tf_op jit(solution)/shard_map/ppermute | solution.py:25
  199.4 1.0 copy-start.17
  217.5 15.1 %collective-permute-start.15 = (bf16[2,512,256]{2,1,0:T(8,128)(2,1)}, bf16[2,512,256]{2,1,0:T(8,128)(2,1)S(1)}, u32[]{:S(2)}, u32[]{:S(2)}) collective-permute-start(bf16[2,512,256]{2,1,0:T(8,128)(2,1)} %get-tuple-element.69), channel_id=1, source_target_pairs={{0,1},{1,0},{2,3},{3,2},{4,5},{5,4},{6,7},{7,6},{8,9},{9,8},{10,11... | collective-permute-start | bytes 1572872 | tf_op jit(solution)/shard_map/ppermute | solution.py:25
  218.3 49.0 %collective-permute-start.24 = (bf16[2,512,512]{2,1,0:T(8,128)(2,1)}, bf16[2,512,512]{2,1,0:T(8,128)(2,1)S(1)}, u32[]{:S(2)}, u32[]{:S(2)}) collective-permute-start(bf16[2,512,512]{2,1,0:T(8,128)(2,1)} %get-tuple-element.78), channel_id=1, source_target_pairs={{0,1},{1,0},{2,3},{3,2},{4,5},{5,4},{6,7},{7,6},{8,9},{9,8},{10,11... | collective-permute-start | bytes 3145736 | tf_op jit(solution)/shard_map/ppermute | solution.py:25
  219.6 48.2 %collective-permute-start.25 = (bf16[2,512,512]{2,1,0:T(8,128)(2,1)}, bf16[2,512,512]{2,1,0:T(8,128)(2,1)S(1)}, u32[]{:S(2)}, u32[]{:S(2)}) collective-permute-start(bf16[2,512,512]{2,1,0:T(8,128)(2,1)} %get-tuple-element.79), channel_id=1, source_target_pairs={{0,2},{1,3},{2,0},{3,1},{4,6},{5,7},{6,4},{7,5},{8,10},{9,11},{10,... | collective-permute-start | bytes 3145736 | tf_op jit(solution)/shard_map/ppermute | solution.py:25
  219.6 164.8 %copy-start.21 = (bf16[2,512,256]{2,1,0:T(8,128)(2,1)}, bf16[2,512,256]{2,1,0:T(8,128)(2,1)S(1)}, u32[]{:S(2)}) copy-start(bf16[2,512,256]{2,1,0:T(8,128)(2,1)S(1)} %collective-permute-done.28.refs_1_) | copy-start | bytes 1572868
  219.6 164.9 %collective-permute-start.36 = (f32[8,2,2,2,64,256]{5,4,3,2,1,0:T(8,128)}, f32[8,2,2,2,64,256]{5,4,3,2,1,0:T(8,128)}, u32[]{:S(2)}, u32[]{:S(2)}) collective-permute-start(f32[8,2,2,2,64,256]{5,4,3,2,1,0:T(8,128)} %get-tuple-element.107), channel_id=1, source_target_pairs={{0,8},{8,0},{16,24},{24,16},{1,9},{9,1},{17,25},{25,17},{2,10},{10... | collective-permute-start | bytes 12582920 | tf_op jit(solution)/shard_map/ppermute | solution.py:25
  221.0 163.4 %copy-start.22 = (bf16[2,512,256]{2,1,0:T(8,128)(2,1)}, bf16[2,512,256]{2,1,0:T(8,128)(2,1)S(1)}, u32[]{:S(2)}) copy-start(bf16[2,512,256]{2,1,0:T(8,128)(2,1)S(1)} %collective-permute-done.29.refs_2_) | copy-start | bytes 1572868
  221.0 44.8 %collective-permute-start.16 = (bf16[2,512,256]{2,1,0:T(8,128)(2,1)}, bf16[2,512,256]{2,1,0:T(8,128)(2,1)S(1)}, u32[]{:S(2)}, u32[]{:S(2)}) collective-permute-start(bf16[2,512,256]{2,1,0:T(8,128)(2,1)} %get-tuple-element.70), channel_id=1, source_target_pairs={{0,2},{1,3},{2,0},{3,1},{4,6},{5,7},{6,4},{7,5},{8,10},{9,11},{10,... | collective-permute-start | bytes 1572872 | tf_op jit(solution)/shard_map/ppermute | solution.py:25
  232.5 33.3 %copy-start.18 = (bf16[2,512,256]{2,1,0:T(8,128)(2,1)}, bf16[2,512,256]{2,1,0:T(8,128)(2,1)S(1)}, u32[]{:S(2)}) copy-start(bf16[2,512,256]{2,1,0:T(8,128)(2,1)S(1)} %collective-permute-done.15.refs_0_) | copy-start | bytes 1572868
  232.5 34.7 %collective-permute-start.17 = (bf16[2,512,256]{2,1,0:T(8,128)(2,1)}, bf16[2,512,256]{2,1,0:T(8,128)(2,1)S(1)}, u32[]{:S(2)}, u32[]{:S(2)}) collective-permute-start(bf16[2,512,256]{2,1,0:T(8,128)(2,1)} %get-tuple-element.71), channel_id=1, source_target_pairs={{0,4},{1,5},{2,6},{3,7},{4,0},{5,1},{6,2},{7,3},{8,12},{9,13},{10,... | collective-permute-start | bytes 1572872 | tf_op jit(solution)/shard_map/ppermute | solution.py:25
  266.7 46.4 %collective-permute-start.26 = (bf16[2,512,512]{2,1,0:T(8,128)(2,1)}, bf16[2,512,512]{2,1,0:T(8,128)(2,1)S(1)}, u32[]{:S(2)}, u32[]{:S(2)}) collective-permute-start(bf16[2,512,512]{2,1,0:T(8,128)(2,1)} %get-tuple-element.80), channel_id=1, source_target_pairs={{0,4},{1,5},{2,6},{3,7},{4,0},{5,1},{6,2},{7,3},{8,12},{9,13},{10,... | collective-permute-start | bytes 3145736 | tf_op jit(solution)/shard_map/ppermute | solution.py:25
  267.3 123.1 %collective-permute-start.34 = (f32[8,2,2,2,64,256]{5,4,3,2,1,0:T(8,128)}, f32[8,2,2,2,64,256]{5,4,3,2,1,0:T(8,128)}, u32[]{:S(2)}, u32[]{:S(2)}) collective-permute-start(f32[8,2,2,2,64,256]{5,4,3,2,1,0:T(8,128)} %get-tuple-element.103), channel_id=1, source_target_pairs={{0,8},{8,0},{16,24},{24,16},{1,9},{9,1},{17,25},{25,17},{2,10},{10... | collective-permute-start | bytes 12582920 | tf_op jit(solution)/shard_map/ppermute | solution.py:25
  267.3 117.1 %copy-start.7 = (bf16[2,512,512]{2,1,0:T(8,128)(2,1)}, bf16[2,512,512]{2,1,0:T(8,128)(2,1)S(1)}, u32[]{:S(2)}) copy-start(bf16[2,512,512]{2,1,0:T(8,128)(2,1)S(1)} %collective-permute-done.24.refs_0_) | copy-start | bytes 3145732
  267.3 129.6 %collective-permute-start.32 = (f32[8,2,2,2,64,256]{5,4,3,2,1,0:T(8,128)}, f32[8,2,2,2,64,256]{5,4,3,2,1,0:T(8,128)}, u32[]{:S(2)}, u32[]{:S(2)}) collective-permute-start(f32[8,2,2,2,64,256]{5,4,3,2,1,0:T(8,128)} %get-tuple-element.99), channel_id=1, source_target_pairs={{0,8},{8,0},{16,24},{24,16},{1,9},{9,1},{17,25},{25,17},{2,10},{10... | collective-permute-start | bytes 12582920 | tf_op jit(solution)/shard_map/ppermute | solution.py:25
  268.1 116.3 %copy-start.8 = (bf16[2,512,512]{2,1,0:T(8,128)(2,1)}, bf16[2,512,512]{2,1,0:T(8,128)(2,1)S(1)}, u32[]{:S(2)}) copy-start(bf16[2,512,512]{2,1,0:T(8,128)(2,1)S(1)} %collective-permute-done.25.refs_1_) | copy-start | bytes 3145732
  268.1 45.2 %collective-permute-start.21 = (bf16[2,512,512]{2,1,0:T(8,128)(2,1)}, bf16[2,512,512]{2,1,0:T(8,128)(2,1)S(1)}, u32[]{:S(2)}, u32[]{:S(2)}) collective-permute-start(bf16[2,512,512]{2,1,0:T(8,128)(2,1)} %get-tuple-element.75), channel_id=1, source_target_pairs={{0,1},{1,0},{2,3},{3,2},{4,5},{5,4},{6,7},{7,6},{8,9},{9,8},{10,11... | collective-permute-start | bytes 3145736 | tf_op jit(solution)/shard_map/ppermute | solution.py:25
  313.0 71.4 %copy-start.9 = (bf16[2,512,512]{2,1,0:T(8,128)(2,1)}, bf16[2,512,512]{2,1,0:T(8,128)(2,1)S(1)}, u32[]{:S(2)}) copy-start(bf16[2,512,512]{2,1,0:T(8,128)(2,1)S(1)} %collective-permute-done.26.refs_2_) | copy-start | bytes 3145732
  313.0 46.3 %collective-permute-start.22 = (bf16[2,512,512]{2,1,0:T(8,128)(2,1)}, bf16[2,512,512]{2,1,0:T(8,128)(2,1)S(1)}, u32[]{:S(2)}, u32[]{:S(2)}) collective-permute-start(bf16[2,512,512]{2,1,0:T(8,128)(2,1)} %get-tuple-element.76), channel_id=1, source_target_pairs={{0,2},{1,3},{2,0},{3,1},{4,6},{5,7},{6,4},{7,5},{8,10},{9,11},{10,... | collective-permute-start | bytes 3145736 | tf_op jit(solution)/shard_map/ppermute | solution.py:25
  313.3 71.2 %copy-start.10 = (bf16[2,512,512]{2,1,0:T(8,128)(2,1)}, bf16[2,512,512]{2,1,0:T(8,128)(2,1)S(1)}, u32[]{:S(2)}) copy-start(bf16[2,512,512]{2,1,0:T(8,128)(2,1)S(1)} %collective-permute-done.21.refs_0_) | copy-start | bytes 3145732
  313.3 49.2 %collective-permute-start.23 = (bf16[2,512,512]{2,1,0:T(8,128)(2,1)}, bf16[2,512,512]{2,1,0:T(8,128)(2,1)S(1)}, u32[]{:S(2)}, u32[]{:S(2)}) collective-permute-start(bf16[2,512,512]{2,1,0:T(8,128)(2,1)} %get-tuple-element.77), channel_id=1, source_target_pairs={{0,4},{1,5},{2,6},{3,7},{4,0},{5,1},{6,2},{7,3},{8,12},{9,13},{10,... | collective-permute-start | bytes 3145736 | tf_op jit(solution)/shard_map/ppermute | solution.py:25
  359.3 25.1 %copy-start.11 = (bf16[2,512,512]{2,1,0:T(8,128)(2,1)}, bf16[2,512,512]{2,1,0:T(8,128)(2,1)S(1)}, u32[]{:S(2)}) copy-start(bf16[2,512,512]{2,1,0:T(8,128)(2,1)S(1)} %collective-permute-done.22.refs_1_) | copy-start | bytes 3145732
  359.3 25.0 %collective-permute-start.18 = (bf16[2,512,512]{2,1,0:T(8,128)(2,1)}, bf16[2,512,512]{2,1,0:T(8,128)(2,1)S(1)}, u32[]{:S(2)}, u32[]{:S(2)}) collective-permute-start(bf16[2,512,512]{2,1,0:T(8,128)(2,1)} %get-tuple-element.72), channel_id=1, source_target_pairs={{0,1},{1,0},{2,3},{3,2},{4,5},{5,4},{6,7},{7,6},{8,9},{9,8},{10,11... | collective-permute-start | bytes 3145736 | tf_op jit(solution)/shard_map/ppermute | solution.py:25
  362.5 22.0 %copy-start.12 = (bf16[2,512,512]{2,1,0:T(8,128)(2,1)}, bf16[2,512,512]{2,1,0:T(8,128)(2,1)S(1)}, u32[]{:S(2)}) copy-start(bf16[2,512,512]{2,1,0:T(8,128)(2,1)S(1)} %collective-permute-done.23.refs_2_) | copy-start | bytes 3145732
  362.5 49.3 %collective-permute-start.38 = (f32[4,2,2,2,64,256]{5,4,3,2,1,0:T(8,128)}, f32[4,2,2,2,64,256]{5,4,3,2,1,0:T(8,128)}, u32[]{:S(2)}, u32[]{:S(2)}) collective-permute-start(f32[4,2,2,2,64,256]{5,4,3,2,1,0:T(8,128)} %get-tuple-element.111), channel_id=1, source_target_pairs={{0,8},{8,0},{16,24},{24,16},{1,9},{9,1},{17,25},{25,17},{2,10},{10... | collective-permute-start | bytes 6291464 | tf_op jit(solution)/shard_map/ppermute | solution.py:25
  384.3 1.0 copy-start.13
  384.4 32.5 %collective-permute-start.30 = (f32[4,2,2,2,64,256]{5,4,3,2,1,0:T(8,128)}, f32[4,2,2,2,64,256]{5,4,3,2,1,0:T(8,128)S(1)}, u32[]{:S(2)}, u32[]{:S(2)}) collective-permute-start(f32[4,2,2,2,64,256]{5,4,3,2,1,0:T(8,128)} %get-tuple-element.95), channel_id=1, source_target_pairs={{0,8},{8,0},{16,24},{24,16},{1,9},{9,1},{17,25},{25,17},{2,10},{10... | collective-permute-start | bytes 6291464 | tf_op jit(solution)/shard_map/ppermute | solution.py:25
  385.3 25.0 %collective-permute-start.19 = (bf16[2,512,512]{2,1,0:T(8,128)(2,1)}, bf16[2,512,512]{2,1,0:T(8,128)(2,1)S(1)}, u32[]{:S(2)}, u32[]{:S(2)}) collective-permute-start(bf16[2,512,512]{2,1,0:T(8,128)(2,1)} %get-tuple-element.73), channel_id=1, source_target_pairs={{0,2},{1,3},{2,0},{3,1},{4,6},{5,7},{6,4},{7,5},{8,10},{9,11},{10,... | collective-permute-start | bytes 3145736 | tf_op jit(solution)/shard_map/ppermute | solution.py:25
  390.4 164.7 %collective-permute-start.37 = (f32[8,1,2,2,64,256]{5,4,3,2,1,0:T(8,128)}, f32[8,1,2,2,64,256]{5,4,3,2,1,0:T(8,128)}, u32[]{:S(2)}, u32[]{:S(2)}) collective-permute-start(f32[8,1,2,2,64,256]{5,4,3,2,1,0:T(8,128)} %get-tuple-element.109), channel_id=1, source_target_pairs={{0,16},{8,24},{16,0},{24,8},{1,17},{9,25},{17,1},{25,9},{2,18},{10... | collective-permute-start | bytes 6291464 | tf_op jit(solution)/shard_map/ppermute | solution.py:25
  396.9 161.4 %collective-permute-start.35 = (f32[8,1,2,2,64,256]{5,4,3,2,1,0:T(8,128)}, f32[8,1,2,2,64,256]{5,4,3,2,1,0:T(8,128)}, u32[]{:S(2)}, u32[]{:S(2)}) collective-permute-start(f32[8,1,2,2,64,256]{5,4,3,2,1,0:T(8,128)} %get-tuple-element.105), channel_id=1, source_target_pairs={{0,16},{8,24},{16,0},{24,8},{1,17},{9,25},{17,1},{25,9},{2,18},{10... | collective-permute-start | bytes 6291464 | tf_op jit(solution)/shard_map/ppermute | solution.py:25
  410.3 6.5 %copy-start.14 = (bf16[2,512,512]{2,1,0:T(8,128)(2,1)}, bf16[2,512,512]{2,1,0:T(8,128)(2,1)S(1)}, u32[]{:S(2)}) copy-start(bf16[2,512,512]{2,1,0:T(8,128)(2,1)S(1)} %collective-permute-done.19.refs_1_) | copy-start | bytes 3145732
  410.3 151.3 %collective-permute-start.33 = (f32[8,1,2,2,64,256]{5,4,3,2,1,0:T(8,128)}, f32[8,1,2,2,64,256]{5,4,3,2,1,0:T(8,128)}, u32[]{:S(2)}, u32[]{:S(2)}) collective-permute-start(f32[8,1,2,2,64,256]{5,4,3,2,1,0:T(8,128)} %get-tuple-element.101), channel_id=1, source_target_pairs={{0,16},{8,24},{16,0},{24,8},{1,17},{9,25},{17,1},{25,9},{2,18},{10... | collective-permute-start | bytes 6291464 | tf_op jit(solution)/shard_map/ppermute | solution.py:25
  411.8 47.4 %collective-permute-start.20 = (bf16[2,512,512]{2,1,0:T(8,128)(2,1)}, bf16[2,512,512]{2,1,0:T(8,128)(2,1)}, u32[]{:S(2)}, u32[]{:S(2)}) collective-permute-start(bf16[2,512,512]{2,1,0:T(8,128)(2,1)} %get-tuple-element.74), channel_id=1, source_target_pairs={{0,4},{1,5},{2,6},{3,7},{4,0},{5,1},{6,2},{7,3},{8,12},{9,13},{10,... | collective-permute-start | bytes 3145736 | tf_op jit(solution)/shard_map/ppermute | solution.py:25
  416.9 1.3 copy-start
  416.9 134.6 %collective-permute-start.39 = (f32[4,1,2,2,64,256]{5,4,3,2,1,0:T(8,128)}, f32[4,1,2,2,64,256]{5,4,3,2,1,0:T(8,128)S(1)}, u32[]{:S(2)}, u32[]{:S(2)}) collective-permute-start(f32[4,1,2,2,64,256]{5,4,3,2,1,0:T(8,128)} %get-tuple-element.113), channel_id=1, source_target_pairs={{0,16},{8,24},{16,0},{24,8},{1,17},{9,25},{17,1},{25,9},{2,18},{10... | collective-permute-start | bytes 3145736 | tf_op jit(solution)/shard_map/ppermute | solution.py:25
  459.2 113.7 %collective-permute-start.31 = (f32[4,1,2,2,64,256]{5,4,3,2,1,0:T(8,128)}, f32[4,1,2,2,64,256]{5,4,3,2,1,0:T(8,128)S(1)}, u32[]{:S(2)}, u32[]{:S(2)}) collective-permute-start(f32[4,1,2,2,64,256]{5,4,3,2,1,0:T(8,128)} %get-tuple-element.97), channel_id=1, source_target_pairs={{0,16},{8,24},{16,0},{24,8},{1,17},{9,25},{17,1},{25,9},{2,18},{10... | collective-permute-start | bytes 3145736 | tf_op jit(solution)/shard_map/ppermute | solution.py:25
  551.5 1.0 copy-start.6
  572.9 1.0 copy-start.4
  (3 other events, 2.4 us)

commit v3 on v2

--- a/solution.py
+++ b/solution.py
@@ -8,15 +8,11 @@
 from jax.sharding import PartitionSpec as P
 
 
-PIECES = 8
-
-
 def row_groups(local):
-    if local < PIECES:
-        return [1] * local
-    unit = local // PIECES
-    sizes = [unit] + [2 * unit] * (PIECES // 2 - 1)
-    return sizes + [local - sum(sizes)]
+    edge = max(1, local // 8)
+    middle = local - 2 * edge
+    sizes = [edge, middle - middle // 2, middle // 2, edge] if middle >= 0 else [local]
+    return [size for size in sizes if size > 0]
 
 
 def partner(value, axis, distance):
@@ -226,9 +222,9 @@
         send_ref[:, half] = keep_ref[:, other] + recv_ref[:, other]
 
 
-def halve_call(parity, keep, recv):
+def halve_call(per_row, parity, keep, recv):
     cols, halves, pair, slot_kinds, piece, width = keep.shape
-    block = min(4, cols)
+    block = per_row
     spec = pl.BlockSpec((block, halves, pair, slot_kinds, piece, width), lambda i, *_: (i, 0, 0, 0, 0, 0))
     half_shape = (cols, halves // 2, pair, slot_kinds, piece, width)
     half_spec = pl.BlockSpec((block,) + half_shape[1:], lambda i, *_: (i, 0, 0, 0, 0, 0))
@@ -253,10 +249,10 @@
             ref[slot] = keep_ref[:, 0, which, slot] + recv_ref[:, 0, which, slot]
 
 
-def grads_call(start, columns, keep, recv, prior):
+def grads_call(start, per_row, columns, keep, recv, prior):
     cols, _, pair, slot_kinds, piece, width = keep.shape
-    block = min(4, cols)
-    first = start // block
+    block = per_row
+    first = start
     spec = pl.BlockSpec((block, 1, pair, slot_kinds, piece, width), lambda i: (i, 0, 0, 0, 0, 0))
     out_spec = pl.BlockSpec((slot_kinds, block, piece, width), lambda i: (0, first + i, 0, 0))
     out_shape = jax.ShapeDtypeStruct((slot_kinds, columns, piece, width), jnp.float32)
@@ -341,12 +337,12 @@
         keep, send = rest[bits:]
         for bit in range(1, dp_bits):
             recv = partner(send, "dp", bit - 1)
-            keep, send = halve_call(parities[bit], keep, recv)
+            keep, send = halve_call(per_row, parities[bit], keep, recv)
         kept.append((keep, partner(send, "dp", dp_bits - 1)))
 
     grads = []
     for group, start in enumerate(starts):
-        grads = grads_call(start * per_row, columns, *kept[group], grads)
+        grads = grads_call(start, per_row, columns, *kept[group], grads)
     totals = []
     for group, (start, rows) in enumerate(zip(starts, sizes)):
         totals = total_call(start, rows, acc, returned[group], totals)

time: 578 us -> 498 us (0.86)
  waiting for transfers between devices: 357 us -> 299 us
  Pallas kernels: 168 us -> 157 us
  starting transfers between devices: 41.9 us -> 33.8 us
    ppermute x40 -> x32, waiting for transfers between devices: 357 us -> 299 us  [partner(): return lax.ppermute(value, axis, pairs)]
    pallas_call x5 -> x4, Pallas kernels: 103 us -> 91.3 us  [main_call(): pl.pallas_call(functools.partial(main_body, dims), grid_spec=pltpu.Prefet...]
    ppermute x40 -> x32, starting transfers between devices: 41.9 us -> 33.8 us  [partner(): return lax.ppermute(value, axis, pairs)]
    pallas_call x5 -> x4, Pallas kernels: 17.6 us -> 16.6 us  [total_call(): pl.pallas_call(functools.partial(total_body, bits), grid=(rows, 2), in_sp...]
    pallas_call x5 -> x4, Pallas kernels: 22.9 us -> 23.5 us  [halve_call(): pl.pallas_call(halve_body, grid_spec=pltpu.PrefetchScalarGridSpec(num_sca...]
    pallas_call x5 -> x4, Pallas kernels: 15 us -> 15.6 us  [grads_call(): pl.pallas_call(grads_body, grid=(cols // block,), in_specs=[spec, spec] +...]
  transfers between devices with their start and end apart: 40 -> 32, of which waited for: 16 -> 18; matrix products, arithmetic and copies ran while one was open for 1% -> 1% of each run, Pallas kernels for 28% -> 31%
where the time goes in v3:
time: 498 us; the launch traced here: 496 us
  waiting for transfers between devices  299 us (60%)
  Pallas kernels  157 us (32%)
  starting transfers between devices  33.8 us (7%)
  local copies, waits for them, and re-layouts  5.37 us (1%)
    ppermute x32, waiting for transfers between devices, partner(): return lax.ppermute(value, axis, pairs)  299 us
    pallas_call x4, Pallas kernels, main_call(): pl.pallas_call(functools.partial(main_body, dims), grid_spec=pltpu.Prefet...  91.3 us
    ppermute x32, starting transfers between devices, partner(): return lax.ppermute(value, axis, pairs)  33.8 us
    pallas_call x4, Pallas kernels, halve_call(): pl.pallas_call(halve_body, grid_spec=pltpu.PrefetchScalarGridSpec(num_sca...  23.5 us
    pallas_call x4, Pallas kernels, total_call(): pl.pallas_call(functools.partial(total_body, bits), grid=(rows, 2), in_sp...  16.6 us
    pallas_call x4, Pallas kernels, grads_call(): pl.pallas_call(grads_body, grid=(cols // block,), in_specs=[spec, spec] +...  15.6 us
    pallas_call x4, Pallas kernels, pack_call(): pl.pallas_call(pack_body, grid=(rows,), in_specs=[column, column], out_sp...  10.5 us
  transfers between devices with their start and end apart: 32, of which 18 were waited for; matrix products, arithmetic and copies ran while one was open for 1% of the time, Pallas kernels for 31%

profile of v3, /device:TPU:0, one launch (start us, length us, event | category | flops | bytes accessed | tf_op | source)
XLA Modules:
  0.0 496.3 jit_solution(15446646368189591592)
XLA Ops:
  0.6 3.4 pack.6
  4.0 3.0 collective-permute-start.6
  7.0 1.9 pack.7
  8.8 1.6 collective-permute-start.10
  10.4 0.4 collective-permute-start.7
  10.9 2.6 collective-permute-start.8
  13.8 54.9 %collective-permute-done.10.refs_3_ = bf16[2,512,256]{2,1,0:T(8,128)(2,1)S(1)} collective-permute-done((bf16[2,512,256]{2,1,0:T(8,128)(2,1)}, bf16[2,512,256]{2,1,0:T(8,128)(2,1)S(1)}, u32[]{:S(2)}, u32[]{:S(2)}) %collective-permute-start.10) | collective-permute-done | bytes 524320 | tf_op jit(solution)/shard_map/ppermute | solution.py:21
  68.9 3.4 pack.5
  72.3 31.0 %collective-permute-done.11.refs_4_ = bf16[2,512,256]{2,1,0:T(8,128)(2,1)S(1)} collective-permute-done((bf16[2,512,256]{2,1,0:T(8,128)(2,1)}, bf16[2,512,256]{2,1,0:T(8,128)(2,1)S(1)}, u32[]{:S(2)}, u32[]{:S(2)}) %collective-permute-start.11) | collective-permute-done | bytes 524320 | tf_op jit(solution)/shard_map/ppermute | solution.py:21
  103.3 0.6 collective-permute-start.3
  103.9 0.9 collective-permute-start.4
  104.8 3.3 collective-permute-start.5
  108.1 0.7 reshape.30.slots_ref
  108.9 0.6 reshape.29.slots_ref
  109.6 0.6 reshape.28.slots_ref
  110.2 14.6 %columns.4 = (f32[2,8,512,256]{3,2,1,0:T(8,128)}, bf16[2,512,256]{2,1,0:T(8,128)(2,1)}, bf16[2,512,256]{2,1,0:T(8,128)(2,1)}, bf16[2,512,256]{2,1,0:T(8,128)(2,1...) custom-call(s32[8]{0:T(128)} %reshape.30.slots_ref, s32[1]{0:T(128)} %bitcast.parity_ref, ...), custom_call_target="tpu_custom_call" | custom-call | flops 3221225472 | bytes 23592960 | tf_op jit(solution)/shard_map/columns/pallas_call | solution.py:181
  124.8 29.9 %columns.5 = (f32[2,8,512,256]{3,2,1,0:T(8,128)}, bf16[2,512,768]{2,1,0:T(8,128)(2,1)}, bf16[2,512,768]{2,1,0:T(8,128)(2,1)}, bf16[2,512,768]{2,1,0:T(8,128)(2,1...) custom-call(s32[24]{0:T(128)} %reshape.29.slots_ref, s32[1]{0:T(128)} %bitcast.parity_ref, ...), custom_call_target="tpu_custom_call" | custom-call | flops 9663676416 | bytes 45613056 | tf_op jit(solution)/shard_map/columns/pallas_call | solution.py:181
  154.8 16.5 %collective-permute-done.4.refs_3_ = bf16[2,512,768]{2,1,0:T(8,128)(2,1)} collective-permute-done((bf16[2,512,768]{2,1,0:T(8,128)(2,1)}, bf16[2,512,768]{2,1,0:T(8,128)(2,1)}, u32[]{:S(2)}, u32[]{:S(2)}) %collective-permute-start.4) | collective-permute-done | bytes 1572896 | tf_op jit(solution)/shard_map/ppermute | solution.py:21
  171.3 3.2 collective-permute-done.5.refs_4_
  174.5 29.8 %columns.6 = (f32[2,8,512,256]{3,2,1,0:T(8,128)}, bf16[2,512,768]{2,1,0:T(8,128)(2,1)}, bf16[2,512,768]{2,1,0:T(8,128)(2,1)}, bf16[2,512,768]{2,1,0:T(8,128)(2,1...) custom-call(s32[24]{0:T(128)} %reshape.28.slots_ref, s32[1]{0:T(128)} %bitcast.parity_ref, ...), custom_call_target="tpu_custom_call" | custom-call | flops 9663676416 | bytes 45613056 | tf_op jit(solution)/shard_map/columns/pallas_call | solution.py:181
  204.5 1.9 pack.4
  206.3 1.2 collective-permute-start
  207.9 2.6 collective-permute-start.2
  210.5 10.3 %collective-permute-done.refs_2_ = bf16[2,512,256]{2,1,0:T(8,128)(2,1)S(1)} collective-permute-done((bf16[2,512,256]{2,1,0:T(8,128)(2,1)}, bf16[2,512,256]{2,1,0:T(8,128)(2,1)S(1)}, u32[]{:S(2)}, u32[]{:S(2)}) %collective-permute-start) | collective-permute-done | bytes 524320 | tf_op jit(solution)/shard_map/ppermute | solution.py:21
  220.9 1.2 collective-permute-start.21
  222.1 10.7 %collective-permute-done.1.refs_3_ = bf16[2,512,256]{2,1,0:T(8,128)(2,1)S(1)} collective-permute-done((bf16[2,512,256]{2,1,0:T(8,128)(2,1)}, bf16[2,512,256]{2,1,0:T(8,128)(2,1)S(1)}, u32[]{:S(2)}, u32[]{:S(2)}) %collective-permute-start.1) | collective-permute-done | bytes 524320 | tf_op jit(solution)/shard_map/ppermute | solution.py:21
  232.8 1.2 collective-permute-done.2.refs_4_
  234.1 0.8 copy-done.5
  235.0 0.6 reshape.26.slots_ref
  235.6 0.8 collective-permute-start.23
  236.4 17.0 %columns.7 = (f32[2,8,512,256]{3,2,1,0:T(8,128)}, bf16[2,512,256]{2,1,0:T(8,128)(2,1)}, bf16[2,512,256]{2,1,0:T(8,128)(2,1)}, bf16[2,512,256]{2,1,0:T(8,128)(2,1...) custom-call(s32[8]{0:T(128)} %reshape.26.slots_ref, s32[1]{0:T(128)} %bitcast.parity_ref, ...), custom_call_target="tpu_custom_call" | custom-call | flops 3221225472 | bytes 23592960 | tf_op jit(solution)/shard_map/columns/pallas_call | solution.py:181
  253.5 0.9 collective-permute-start.12
  254.3 8.0 %collective-permute-done.23.refs_2_ = bf16[2,512,256]{2,1,0:T(8,128)(2,1)S(1)} collective-permute-done((bf16[2,512,256]{2,1,0:T(8,128)(2,1)}, bf16[2,512,256]{2,1,0:T(8,128)(2,1)S(1)}, u32[]{:S(2)}, u32[]{:S(2)}) %collective-permute-start.23) | collective-permute-done | bytes 524320 | tf_op jit(solution)/shard_map/ppermute | solution.py:21
  262.3 0.8 collective-permute-start.18
  263.1 5.5 %collective-permute-done.12.refs_0_ = bf16[2,512,256]{2,1,0:T(8,128)(2,1)S(1)} collective-permute-done((bf16[2,512,256]{2,1,0:T(8,128)(2,1)}, bf16[2,512,256]{2,1,0:T(8,128)(2,1)S(1)}, u32[]{:S(2)}, u32[]{:S(2)}) %collective-permute-start.12) | collective-permute-done | bytes 524320 | tf_op jit(solution)/shard_map/ppermute | solution.py:21
  268.6 2.0 collective-permute-start.13
  270.6 10.9 %collective-permute-done.13.refs_1_ = bf16[2,512,256]{2,1,0:T(8,128)(2,1)S(1)} collective-permute-done((bf16[2,512,256]{2,1,0:T(8,128)(2,1)}, bf16[2,512,256]{2,1,0:T(8,128)(2,1)S(1)}, u32[]{:S(2)}, u32[]{:S(2)}) %collective-permute-start.13) | collective-permute-done | bytes 524320 | tf_op jit(solution)/shard_map/ppermute | solution.py:21
  281.5 1.7 collective-permute-start.19
  283.3 0.9 collective-permute-start.20
  284.2 17.4 %collective-permute-done.18.refs_0_ = bf16[2,512,768]{2,1,0:T(8,128)(2,1)} collective-permute-done((bf16[2,512,768]{2,1,0:T(8,128)(2,1)}, bf16[2,512,768]{2,1,0:T(8,128)(2,1)}, u32[]{:S(2)}, u32[]{:S(2)}) %collective-permute-start.18) | collective-permute-done | bytes 1572896 | tf_op jit(solution)/shard_map/ppermute | solution.py:21
  301.6 0.8 collective-permute-start.15
  302.4 8.0 %halve.6 = (f32[12,1,2,2,64,256]{5,4,3,2,1,0:T(8,128)}, f32[12,1,2,2,64,256]{5,4,3,2,1,0:T(8,128)}) custom-call(s32[1]{0:T(128)} %bitcast.1.parity_ref, f32[12,2,2,2,64,256]{5,4,3,2,1,0:T(8,128)} %get-tuple-element.84.keep_ref, f32[12,2,2,2,64,256]{5,4,3,2,1,0:T(8,128)} %collective-permute-done.28.recv_ref), custom_call_target="tpu_custom_call" | custom-call | flops 1572864 | bytes 18874368 | tf_op jit(solution)/shard_map/halve/pallas_call | solution.py:231
  310.4 1.6 collective-permute-start.29
  312.0 8.0 %halve.5 = (f32[12,1,2,2,64,256]{5,4,3,2,1,0:T(8,128)}, f32[12,1,2,2,64,256]{5,4,3,2,1,0:T(8,128)}) custom-call(s32[1]{0:T(128)} %bitcast.1.parity_ref, f32[12,2,2,2,64,256]{5,4,3,2,1,0:T(8,128)} %get-tuple-element.80.keep_ref, f32[12,2,2,2,64,256]{5,4,3,2,1,0:T(8,128)} %collective-permute-done.26.recv_ref), custom_call_target="tpu_custom_call" | custom-call | flops 1572864 | bytes 18874368 | tf_op jit(solution)/shard_map/halve/pallas_call | solution.py:231
  320.0 28.9 %collective-permute-done.19.refs_1_ = bf16[2,512,768]{2,1,0:T(8,128)(2,1)} collective-permute-done((bf16[2,512,768]{2,1,0:T(8,128)(2,1)}, bf16[2,512,768]{2,1,0:T(8,128)(2,1)}, u32[]{:S(2)}, u32[]{:S(2)}) %collective-permute-start.19) | collective-permute-done | bytes 1572896 | tf_op jit(solution)/shard_map/ppermute | solution.py:21
  348.9 1.5 collective-permute-start.27
  350.3 2.0 collective-permute-done.20.refs_2_
  352.4 1.9 collective-permute-start.17
  354.3 3.7 halve.7
  358.0 1.6 collective-permute-start.31
  359.6 3.8 halve.4
  363.4 55.7 %collective-permute-done.16.refs_1_ = bf16[2,512,768]{2,1,0:T(8,128)(2,1)} collective-permute-done((bf16[2,512,768]{2,1,0:T(8,128)(2,1)}, bf16[2,512,768]{2,1,0:T(8,128)(2,1)}, u32[]{:S(2)}, u32[]{:S(2)}) %collective-permute-start.16) | collective-permute-done | bytes 1572896 | tf_op jit(solution)/shard_map/ppermute | solution.py:21
  419.9 2.4 totals.4
  422.4 5.8 %totals.5 = (bf16[512,2048]{1,0:T(8,128)(2,1)}, bf16[512,2048]{1,0:T(8,128)(2,1)}) custom-call(f32[2,8,512,256]{3,2,1,0:T(8,128)} %get-tuple-element.55.acc_ref, bf16[2,512,768]{2,1,0:T(8,128)(2,1)} %collective-permute-done.18.refs_0_, bf16[2,512,768]{2,1,0:T(8,128)(2,1)} %collective-permute-done.19.refs_1_, ...), custom_call_target="tpu_custom_call", output_to_operand_aliasing={{0}: (4, {}), {1}: (5, {})} | custom-call | flops 2359296 | bytes 9437184 | tf_op jit(solution)/shard_map/totals/pallas_call | solution.py:289
  428.2 5.8 %totals.6 = (bf16[512,2048]{1,0:T(8,128)(2,1)}, bf16[512,2048]{1,0:T(8,128)(2,1)}) custom-call(f32[2,8,512,256]{3,2,1,0:T(8,128)} %get-tuple-element.55.acc_ref, bf16[2,512,768]{2,1,0:T(8,128)(2,1)} %collective-permute-done.15.refs_0_, bf16[2,512,768]{2,1,0:T(8,128)(2,1)} %collective-permute-done.16.refs_1_, ...), custom_call_target="tpu_custom_call", output_to_operand_aliasing={{0}: (4, {}), {1}: (5, {})} | custom-call | flops 2359296 | bytes 9437184 | tf_op jit(solution)/shard_map/totals/pallas_call | solution.py:289
  434.1 10.1 %collective-permute-done.14.refs_2_ = bf16[2,512,256]{2,1,0:T(8,128)(2,1)} collective-permute-done((bf16[2,512,256]{2,1,0:T(8,128)(2,1)}, bf16[2,512,256]{2,1,0:T(8,128)(2,1)}, u32[]{:S(2)}, u32[]{:S(2)}) %collective-permute-start.14) | collective-permute-done | bytes 524320 | tf_op jit(solution)/shard_map/ppermute | solution.py:21
  444.2 2.5 totals.7
  446.7 25.0 %collective-permute-done.31.recv_ref = f32[4,1,2,2,64,256]{5,4,3,2,1,0:T(8,128)} collective-permute-done((f32[4,1,2,2,64,256]{5,4,3,2,1,0:T(8,128)}, f32[4,1,2,2,64,256]{5,4,3,2,1,0:T(8,128)}, u32[]{:S(2)}, u32[]{:S(2)}) %collective-permute-start.31) | collective-permute-done | bytes 1048608 | tf_op jit(solution)/shard_map/ppermute | solution.py:21
  471.7 2.6 grads.4
  474.3 1.8 copy-done
  476.1 5.2 %grads.5 = (f32[2,32,64,256]{3,2,1,0:T(8,128)}, f32[2,32,64,256]{3,2,1,0:T(8,128)}) custom-call(f32[12,1,2,2,64,256]{5,4,3,2,1,0:T(8,128)} %get-tuple-element.86.keep_ref, f32[12,1,2,2,64,256]{5,4,3,2,1,0:T(8,128)} %copy-done, f32[2,32,64,256]{3,2,1,0:T(8,128)} %get-tuple-element.92.refs_0_, ...), custom_call_target="tpu_custom_call", output_to_operand_aliasing={{0}: (2, {}), {1}: (3, {})} | custom-call | flops 786432 | bytes 9437184 | tf_op jit(solution)/shard_map/grads/pallas_call | solution.py:259
  481.2 5.2 %grads.6 = (f32[2,32,64,256]{3,2,1,0:T(8,128)}, f32[2,32,64,256]{3,2,1,0:T(8,128)}) custom-call(f32[12,1,2,2,64,256]{5,4,3,2,1,0:T(8,128)} %get-tuple-element.82.keep_ref, f32[12,1,2,2,64,256]{5,4,3,2,1,0:T(8,128)} %collective-permute-done.27.recv_ref, f32[2,32,64,256]{3,2,1,0:T(8,128)} %get-tuple-element.94.refs_0_, ...), custom_call_target="tpu_custom_call", output_to_operand_aliasing={{0}: (2, {}), {1}: (3, {})} | custom-call | flops 786432 | bytes 9437184 | tf_op jit(solution)/shard_map/grads/pallas_call | solution.py:259
  486.4 7.3 %collective-permute-done.25.recv_ref = f32[4,1,2,2,64,256]{5,4,3,2,1,0:T(8,128)} collective-permute-done((f32[4,1,2,2,64,256]{5,4,3,2,1,0:T(8,128)}, f32[4,1,2,2,64,256]{5,4,3,2,1,0:T(8,128)}, u32[]{:S(2)}, u32[]{:S(2)}) %collective-permute-start.25) | collective-permute-done | bytes 1048608 | tf_op jit(solution)/shard_map/ppermute | solution.py:21
  493.7 2.6 grads.7
  (55 shorter events, 2.1 us)
Async XLA Ops:
  4.0 6.4 %copy-start.2 = (bf16[2,512,768]{2,1,0:T(8,128)(2,1)S(1)}, bf16[2,512,768]{2,1,0:T(8,128)(2,1)}, u32[]{:S(2)}) copy-start(bf16[2,512,768]{2,1,0:T(8,128)(2,1)} %pack.6) | copy-start | bytes 4718596
  4.0 100.8 %collective-permute-start.6 = (bf16[2,512,768]{2,1,0:T(8,128)(2,1)}, bf16[2,512,768]{2,1,0:T(8,128)(2,1)}, u32[]{:S(2)}, u32[]{:S(2)}) collective-permute-start(bf16[2,512,768]{2,1,0:T(8,128)(2,1)} %pack.6), channel_id=1, source_target_pairs={{0,1},{1,0},{2,3},{3,2},{4,5},{5,4},{6,7},{7,6},{8,9},{9,8},{10,11... | collective-permute-start | bytes 4718600 | tf_op jit(solution)/shard_map/ppermute | solution.py:21
  8.8 59.9 %collective-permute-start.10 = (bf16[2,512,256]{2,1,0:T(8,128)(2,1)}, bf16[2,512,256]{2,1,0:T(8,128)(2,1)S(1)}, u32[]{:S(2)}, u32[]{:S(2)}) collective-permute-start(bf16[2,512,256]{2,1,0:T(8,128)(2,1)} %pack.7), channel_id=1, source_target_pairs={{0,2},{1,3},{2,0},{3,1},{4,6},{5,7},{6,4},{7,5},{8,10},{9,11},{10,... | collective-permute-start | bytes 1572872 | tf_op jit(solution)/shard_map/ppermute | solution.py:21
  10.4 114.4 %collective-permute-start.7 = (bf16[2,512,768]{2,1,0:T(8,128)(2,1)S(1)}, bf16[2,512,768]{2,1,0:T(8,128)(2,1)}, u32[]{:S(2)}, u32[]{:S(2)}) collective-permute-start(bf16[2,512,768]{2,1,0:T(8,128)(2,1)S(1)} %copy-done.2), channel_id=1, source_target_pairs={{0,2},{1,3},{2,0},{3,1},{4,6},{5,7},{6,4},{7,5},{8,10},{9,11},{10,... | collective-permute-start | bytes 4718600 | tf_op jit(solution)/shard_map/ppermute | solution.py:21
  10.9 114.0 %collective-permute-start.8 = (bf16[2,512,768]{2,1,0:T(8,128)(2,1)S(1)}, bf16[2,512,768]{2,1,0:T(8,128)(2,1)}, u32[]{:S(2)}, u32[]{:S(2)}) collective-permute-start(bf16[2,512,768]{2,1,0:T(8,128)(2,1)S(1)} %copy-done.2), channel_id=1, source_target_pairs={{0,4},{1,5},{2,6},{3,7},{4,0},{5,1},{6,2},{7,3},{8,12},{9,13},{10,... | collective-permute-start | bytes 4718600 | tf_op jit(solution)/shard_map/ppermute | solution.py:21
  13.4 89.8 %collective-permute-start.11 = (bf16[2,512,256]{2,1,0:T(8,128)(2,1)}, bf16[2,512,256]{2,1,0:T(8,128)(2,1)S(1)}, u32[]{:S(2)}, u32[]{:S(2)}) collective-permute-start(bf16[2,512,256]{2,1,0:T(8,128)(2,1)} %pack.7), channel_id=1, source_target_pairs={{0,4},{1,5},{2,6},{3,7},{4,0},{5,1},{6,2},{7,3},{8,12},{9,13},{10,... | collective-permute-start | bytes 1572872 | tf_op jit(solution)/shard_map/ppermute | solution.py:21
  68.7 3.6 copy-start.9
  68.7 35.2 %collective-permute-start.9 = (bf16[2,512,256]{2,1,0:T(8,128)(2,1)}, bf16[2,512,256]{2,1,0:T(8,128)(2,1)S(1)}, u32[]{:S(2)}, u32[]{:S(2)}) collective-permute-start(bf16[2,512,256]{2,1,0:T(8,128)(2,1)} %pack.7), channel_id=1, source_target_pairs={{0,1},{1,0},{2,3},{3,2},{4,5},{5,4},{6,7},{7,6},{8,9},{9,8},{10,11... | collective-permute-start | bytes 1572872 | tf_op jit(solution)/shard_map/ppermute | solution.py:21
  68.9 39.2 %copy-start.12 = (s32[2,32]{1,0:T(2,128)S(1)}, s32[2,32]{1,0:T(2,128)}, u32[]{:S(2)}) copy-start(s32[2,32]{1,0:T(2,128)} %param.9) | copy-start | bytes 772
  103.3 6.9 %copy-start.10 = (bf16[2,512,256]{2,1,0:T(8,128)(2,1)}, bf16[2,512,256]{2,1,0:T(8,128)(2,1)S(1)}, u32[]{:S(2)}) copy-start(bf16[2,512,256]{2,1,0:T(8,128)(2,1)S(1)} %collective-permute-done.11.refs_4_) | copy-start | bytes 1572868
  103.3 51.5 %collective-permute-start.3 = (bf16[2,512,768]{2,1,0:T(8,128)(2,1)}, bf16[2,512,768]{2,1,0:T(8,128)(2,1)}, u32[]{:S(2)}, u32[]{:S(2)}) collective-permute-start(bf16[2,512,768]{2,1,0:T(8,128)(2,1)} %pack.5), channel_id=1, source_target_pairs={{0,1},{1,0},{2,3},{3,2},{4,5},{5,4},{6,7},{7,6},{8,9},{9,8},{10,11... | collective-permute-start | bytes 4718600 | tf_op jit(solution)/shard_map/ppermute | solution.py:21
  103.9 6.3 %copy-start.11 = (bf16[2,512,256]{2,1,0:T(8,128)(2,1)}, bf16[2,512,256]{2,1,0:T(8,128)(2,1)S(1)}, u32[]{:S(2)}) copy-start(bf16[2,512,256]{2,1,0:T(8,128)(2,1)S(1)} %collective-permute-done.9.refs_2_) | copy-start | bytes 1572868
  103.9 67.4 %collective-permute-start.4 = (bf16[2,512,768]{2,1,0:T(8,128)(2,1)}, bf16[2,512,768]{2,1,0:T(8,128)(2,1)}, u32[]{:S(2)}, u32[]{:S(2)}) collective-permute-start(bf16[2,512,768]{2,1,0:T(8,128)(2,1)} %pack.5), channel_id=1, source_target_pairs={{0,2},{1,3},{2,0},{3,1},{4,6},{5,7},{6,4},{7,5},{8,10},{9,11},{10,... | collective-permute-start | bytes 4718600 | tf_op jit(solution)/shard_map/ppermute | solution.py:21
  104.8 69.7 %collective-permute-start.5 = (bf16[2,512,768]{2,1,0:T(8,128)(2,1)}, bf16[2,512,768]{2,1,0:T(8,128)(2,1)}, u32[]{:S(2)}, u32[]{:S(2)}) collective-permute-start(bf16[2,512,768]{2,1,0:T(8,128)(2,1)} %pack.5), channel_id=1, source_target_pairs={{0,4},{1,5},{2,6},{3,7},{4,0},{5,1},{6,2},{7,3},{8,12},{9,13},{10,... | collective-permute-start | bytes 4718600 | tf_op jit(solution)/shard_map/ppermute | solution.py:21
  154.7 147.7 %collective-permute-start.28 = (f32[12,2,2,2,64,256]{5,4,3,2,1,0:T(8,128)}, f32[12,2,2,2,64,256]{5,4,3,2,1,0:T(8,128)}, u32[]{:S(2)}, u32[]{:S(2)}) collective-permute-start(f32[12,2,2,2,64,256]{5,4,3,2,1,0:T(8,128)} %get-tuple-element.85), channel_id=1, source_target_pairs={{0,8},{8,0},{16,24},{24,16},{1,9},{9,1},{17,25},{25,17},{2,10},{10... | collective-permute-start | bytes 18874376 | tf_op jit(solution)/shard_map/ppermute | solution.py:21
  204.4 106.1 %collective-permute-start.26 = (f32[12,2,2,2,64,256]{5,4,3,2,1,0:T(8,128)}, f32[12,2,2,2,64,256]{5,4,3,2,1,0:T(8,128)}, u32[]{:S(2)}, u32[]{:S(2)}) collective-permute-start(f32[12,2,2,2,64,256]{5,4,3,2,1,0:T(8,128)} %get-tuple-element.81), channel_id=1, source_target_pairs={{0,8},{8,0},{16,24},{24,16},{1,9},{9,1},{17,25},{25,17},{2,10},{10... | collective-permute-start | bytes 18874376 | tf_op jit(solution)/shard_map/ppermute | solution.py:21
  206.3 14.5 %collective-permute-start = (bf16[2,512,256]{2,1,0:T(8,128)(2,1)}, bf16[2,512,256]{2,1,0:T(8,128)(2,1)S(1)}, u32[]{:S(2)}, u32[]{:S(2)}) collective-permute-start(bf16[2,512,256]{2,1,0:T(8,128)(2,1)} %pack.4), channel_id=1, source_target_pairs={{0,1},{1,0},{2,3},{3,2},{4,5},{5,4},{6,7},{7,6},{8,9},{9,8},{10,11... | collective-permute-start | bytes 1572872 | tf_op jit(solution)/shard_map/ppermute | solution.py:21
  207.6 25.3 %collective-permute-start.1 = (bf16[2,512,256]{2,1,0:T(8,128)(2,1)}, bf16[2,512,256]{2,1,0:T(8,128)(2,1)S(1)}, u32[]{:S(2)}, u32[]{:S(2)}) collective-permute-start(bf16[2,512,256]{2,1,0:T(8,128)(2,1)} %pack.4), channel_id=1, source_target_pairs={{0,2},{1,3},{2,0},{3,1},{4,6},{5,7},{6,4},{7,5},{8,10},{9,11},{10,... | collective-permute-start | bytes 1572872 | tf_op jit(solution)/shard_map/ppermute | solution.py:21
  207.9 26.2 %collective-permute-start.2 = (bf16[2,512,256]{2,1,0:T(8,128)(2,1)}, bf16[2,512,256]{2,1,0:T(8,128)(2,1)S(1)}, u32[]{:S(2)}, u32[]{:S(2)}) collective-permute-start(bf16[2,512,256]{2,1,0:T(8,128)(2,1)} %pack.4), channel_id=1, source_target_pairs={{0,4},{1,5},{2,6},{3,7},{4,0},{5,1},{6,2},{7,3},{8,12},{9,13},{10,... | collective-permute-start | bytes 1572872 | tf_op jit(solution)/shard_map/ppermute | solution.py:21
  220.9 15.6 %copy-start.3 = (bf16[2,512,256]{2,1,0:T(8,128)(2,1)}, bf16[2,512,256]{2,1,0:T(8,128)(2,1)S(1)}, u32[]{:S(2)}) copy-start(bf16[2,512,256]{2,1,0:T(8,128)(2,1)S(1)} %collective-permute-done.refs_2_) | copy-start | bytes 1572868
  220.9 14.7 %collective-permute-start.21 = (bf16[2,512,256]{2,1,0:T(8,128)(2,1)}, bf16[2,512,256]{2,1,0:T(8,128)(2,1)}, u32[]{:S(2)}, u32[]{:S(2)}) collective-permute-start(bf16[2,512,256]{2,1,0:T(8,128)(2,1)} %get-tuple-element.65), channel_id=1, source_target_pairs={{0,1},{1,0},{2,3},{3,2},{4,5},{5,4},{6,7},{7,6},{8,9},{9,8},{10,11... | collective-permute-start | bytes 1572872 | tf_op jit(solution)/shard_map/ppermute | solution.py:21
  232.8 3.6 copy-start.4
  232.8 20.7 %collective-permute-start.22 = (bf16[2,512,256]{2,1,0:T(8,128)(2,1)}, bf16[2,512,256]{2,1,0:T(8,128)(2,1)}, u32[]{:S(2)}, u32[]{:S(2)}) collective-permute-start(bf16[2,512,256]{2,1,0:T(8,128)(2,1)} %get-tuple-element.66), channel_id=1, source_target_pairs={{0,2},{1,3},{2,0},{3,1},{4,6},{5,7},{6,4},{7,5},{8,10},{9,11},{10,... | collective-permute-start | bytes 1572872 | tf_op jit(solution)/shard_map/ppermute | solution.py:21
  234.1 0.8 copy-start.5
  234.9 48.4 %collective-permute-start.30 = (f32[4,2,2,2,64,256]{5,4,3,2,1,0:T(8,128)}, f32[4,2,2,2,64,256]{5,4,3,2,1,0:T(8,128)S(1)}, u32[]{:S(2)}, u32[]{:S(2)}) collective-permute-start(f32[4,2,2,2,64,256]{5,4,3,2,1,0:T(8,128)} %get-tuple-element.89), channel_id=1, source_target_pairs={{0,8},{8,0},{16,24},{24,16},{1,9},{9,1},{17,25},{25,17},{2,10},{10... | collective-permute-start | bytes 6291464 | tf_op jit(solution)/shard_map/ppermute | solution.py:21
  235.6 26.7 %collective-permute-start.23 = (bf16[2,512,256]{2,1,0:T(8,128)(2,1)}, bf16[2,512,256]{2,1,0:T(8,128)(2,1)S(1)}, u32[]{:S(2)}, u32[]{:S(2)}) collective-permute-start(bf16[2,512,256]{2,1,0:T(8,128)(2,1)} %get-tuple-element.67), channel_id=1, source_target_pairs={{0,4},{1,5},{2,6},{3,7},{4,0},{5,1},{6,2},{7,3},{8,12},{9,13},{10,... | collective-permute-start | bytes 1572872 | tf_op jit(solution)/shard_map/ppermute | solution.py:21
  253.5 15.1 %collective-permute-start.12 = (bf16[2,512,256]{2,1,0:T(8,128)(2,1)}, bf16[2,512,256]{2,1,0:T(8,128)(2,1)S(1)}, u32[]{:S(2)}, u32[]{:S(2)}) collective-permute-start(bf16[2,512,256]{2,1,0:T(8,128)(2,1)} %get-tuple-element.56), channel_id=1, source_target_pairs={{0,1},{1,0},{2,3},{3,2},{4,5},{5,4},{6,7},{7,6},{8,9},{9,8},{10,11... | collective-permute-start | bytes 1572872 | tf_op jit(solution)/shard_map/ppermute | solution.py:21
  262.3 21.9 %copy-start.8 = (bf16[2,512,256]{2,1,0:T(8,128)(2,1)}, bf16[2,512,256]{2,1,0:T(8,128)(2,1)S(1)}, u32[]{:S(2)}) copy-start(bf16[2,512,256]{2,1,0:T(8,128)(2,1)S(1)} %collective-permute-done.23.refs_2_) | copy-start | bytes 1572868
  262.3 39.3 %collective-permute-start.18 = (bf16[2,512,768]{2,1,0:T(8,128)(2,1)}, bf16[2,512,768]{2,1,0:T(8,128)(2,1)}, u32[]{:S(2)}, u32[]{:S(2)}) collective-permute-start(bf16[2,512,768]{2,1,0:T(8,128)(2,1)} %get-tuple-element.62), channel_id=1, source_target_pairs={{0,1},{1,0},{2,3},{3,2},{4,5},{5,4},{6,7},{7,6},{8,9},{9,8},{10,11... | collective-permute-start | bytes 4718600 | tf_op jit(solution)/shard_map/ppermute | solution.py:21
  268.6 14.7 %copy-start.6 = (bf16[2,512,256]{2,1,0:T(8,128)(2,1)}, bf16[2,512,256]{2,1,0:T(8,128)(2,1)S(1)}, u32[]{:S(2)}) copy-start(bf16[2,512,256]{2,1,0:T(8,128)(2,1)S(1)} %collective-permute-done.12.refs_0_) | copy-start | bytes 1572868
  268.6 13.0 %collective-permute-start.13 = (bf16[2,512,256]{2,1,0:T(8,128)(2,1)}, bf16[2,512,256]{2,1,0:T(8,128)(2,1)S(1)}, u32[]{:S(2)}, u32[]{:S(2)}) collective-permute-start(bf16[2,512,256]{2,1,0:T(8,128)(2,1)} %get-tuple-element.57), channel_id=1, source_target_pairs={{0,2},{1,3},{2,0},{3,1},{4,6},{5,7},{6,4},{7,5},{8,10},{9,11},{10,... | collective-permute-start | bytes 1572872 | tf_op jit(solution)/shard_map/ppermute | solution.py:21
  281.5 1.8 copy-start.7
  281.5 67.3 %collective-permute-start.19 = (bf16[2,512,768]{2,1,0:T(8,128)(2,1)}, bf16[2,512,768]{2,1,0:T(8,128)(2,1)}, u32[]{:S(2)}, u32[]{:S(2)}) collective-permute-start(bf16[2,512,768]{2,1,0:T(8,128)(2,1)} %get-tuple-element.63), channel_id=1, source_target_pairs={{0,2},{1,3},{2,0},{3,1},{4,6},{5,7},{6,4},{7,5},{8,10},{9,11},{10,... | collective-permute-start | bytes 4718600 | tf_op jit(solution)/shard_map/ppermute | solution.py:21
  283.3 27.2 %copy-start.1 = (f32[4,2,2,2,64,256]{5,4,3,2,1,0:T(8,128)}, f32[4,2,2,2,64,256]{5,4,3,2,1,0:T(8,128)S(1)}, u32[]{:S(2)}) copy-start(f32[4,2,2,2,64,256]{5,4,3,2,1,0:T(8,128)S(1)} %collective-permute-done.30.recv_ref) | copy-start | bytes 6291460
  283.3 69.1 %collective-permute-start.20 = (bf16[2,512,768]{2,1,0:T(8,128)(2,1)}, bf16[2,512,768]{2,1,0:T(8,128)(2,1)}, u32[]{:S(2)}, u32[]{:S(2)}) collective-permute-start(bf16[2,512,768]{2,1,0:T(8,128)(2,1)} %get-tuple-element.64), channel_id=1, source_target_pairs={{0,4},{1,5},{2,6},{3,7},{4,0},{5,1},{6,2},{7,3},{8,12},{9,13},{10,... | collective-permute-start | bytes 4718600 | tf_op jit(solution)/shard_map/ppermute | solution.py:21
  301.6 50.8 %collective-permute-start.15 = (bf16[2,512,768]{2,1,0:T(8,128)(2,1)}, bf16[2,512,768]{2,1,0:T(8,128)(2,1)}, u32[]{:S(2)}, u32[]{:S(2)}) collective-permute-start(bf16[2,512,768]{2,1,0:T(8,128)(2,1)} %get-tuple-element.59), channel_id=1, source_target_pairs={{0,1},{1,0},{2,3},{3,2},{4,5},{5,4},{6,7},{7,6},{8,9},{9,8},{10,11... | collective-permute-start | bytes 4718600 | tf_op jit(solution)/shard_map/ppermute | solution.py:21
  302.4 55.6 %collective-permute-start.24 = (f32[4,2,2,2,64,256]{5,4,3,2,1,0:T(8,128)}, f32[4,2,2,2,64,256]{5,4,3,2,1,0:T(8,128)}, u32[]{:S(2)}, u32[]{:S(2)}) collective-permute-start(f32[4,2,2,2,64,256]{5,4,3,2,1,0:T(8,128)} %get-tuple-element.77), channel_id=1, source_target_pairs={{0,8},{8,0},{16,24},{24,16},{1,9},{9,1},{17,25},{25,17},{2,10},{10... | collective-permute-start | bytes 6291464 | tf_op jit(solution)/shard_map/ppermute | solution.py:21
  310.4 163.9 %collective-permute-start.29 = (f32[12,1,2,2,64,256]{5,4,3,2,1,0:T(8,128)}, f32[12,1,2,2,64,256]{5,4,3,2,1,0:T(8,128)S(1)}, u32[]{:S(2)}, u32[]{:S(2)}) collective-permute-start(f32[12,1,2,2,64,256]{5,4,3,2,1,0:T(8,128)} %get-tuple-element.87), channel_id=1, source_target_pairs={{0,16},{8,24},{16,0},{24,8},{1,17},{9,25},{17,1},{25,9},{2,18},{10... | collective-permute-start | bytes 9437192 | tf_op jit(solution)/shard_map/ppermute | solution.py:21
  348.9 132.4 %collective-permute-start.27 = (f32[12,1,2,2,64,256]{5,4,3,2,1,0:T(8,128)}, f32[12,1,2,2,64,256]{5,4,3,2,1,0:T(8,128)}, u32[]{:S(2)}, u32[]{:S(2)}) collective-permute-start(f32[12,1,2,2,64,256]{5,4,3,2,1,0:T(8,128)} %get-tuple-element.83), channel_id=1, source_target_pairs={{0,16},{8,24},{16,0},{24,8},{1,17},{9,25},{17,1},{25,9},{2,18},{10... | collective-permute-start | bytes 9437192 | tf_op jit(solution)/shard_map/ppermute | solution.py:21
  352.4 66.8 %collective-permute-start.16 = (bf16[2,512,768]{2,1,0:T(8,128)(2,1)}, bf16[2,512,768]{2,1,0:T(8,128)(2,1)}, u32[]{:S(2)}, u32[]{:S(2)}) collective-permute-start(bf16[2,512,768]{2,1,0:T(8,128)(2,1)} %get-tuple-element.60), channel_id=1, source_target_pairs={{0,2},{1,3},{2,0},{3,1},{4,6},{5,7},{6,4},{7,5},{8,10},{9,11},{10,... | collective-permute-start | bytes 4718600 | tf_op jit(solution)/shard_map/ppermute | solution.py:21
  352.4 67.3 %collective-permute-start.17 = (bf16[2,512,768]{2,1,0:T(8,128)(2,1)}, bf16[2,512,768]{2,1,0:T(8,128)(2,1)}, u32[]{:S(2)}, u32[]{:S(2)}) collective-permute-start(bf16[2,512,768]{2,1,0:T(8,128)(2,1)} %get-tuple-element.61), channel_id=1, source_target_pairs={{0,4},{1,5},{2,6},{3,7},{4,0},{5,1},{6,2},{7,3},{8,12},{9,13},{10,... | collective-permute-start | bytes 4718600 | tf_op jit(solution)/shard_map/ppermute | solution.py:21
  358.0 113.6 %collective-permute-start.31 = (f32[4,1,2,2,64,256]{5,4,3,2,1,0:T(8,128)}, f32[4,1,2,2,64,256]{5,4,3,2,1,0:T(8,128)}, u32[]{:S(2)}, u32[]{:S(2)}) collective-permute-start(f32[4,1,2,2,64,256]{5,4,3,2,1,0:T(8,128)} %get-tuple-element.91), channel_id=1, source_target_pairs={{0,16},{8,24},{16,0},{24,8},{1,17},{9,25},{17,1},{25,9},{2,18},{10... | collective-permute-start | bytes 3145736 | tf_op jit(solution)/shard_map/ppermute | solution.py:21
  419.1 74.5 %collective-permute-start.25 = (f32[4,1,2,2,64,256]{5,4,3,2,1,0:T(8,128)}, f32[4,1,2,2,64,256]{5,4,3,2,1,0:T(8,128)}, u32[]{:S(2)}, u32[]{:S(2)}) collective-permute-start(f32[4,1,2,2,64,256]{5,4,3,2,1,0:T(8,128)} %get-tuple-element.79), channel_id=1, source_target_pairs={{0,16},{8,24},{16,0},{24,8},{1,17},{9,25},{17,1},{25,9},{2,18},{10... | collective-permute-start | bytes 3145736 | tf_op jit(solution)/shard_map/ppermute | solution.py:21
  419.7 24.5 %collective-permute-start.14 = (bf16[2,512,256]{2,1,0:T(8,128)(2,1)}, bf16[2,512,256]{2,1,0:T(8,128)(2,1)}, u32[]{:S(2)}, u32[]{:S(2)}) collective-permute-start(bf16[2,512,256]{2,1,0:T(8,128)(2,1)} %get-tuple-element.58), channel_id=1, source_target_pairs={{0,4},{1,5},{2,6},{3,7},{4,0},{5,1},{6,2},{7,3},{8,12},{9,13},{10,... | collective-permute-start | bytes 1572872 | tf_op jit(solution)/shard_map/ppermute | solution.py:21
  474.3 1.8 copy-start

commit v4 on v3

--- a/solution.py
+++ b/solution.py
@@ -40,38 +40,41 @@
     return lax.dot_general(left, right, (((0,), (0,)), ((), ())), preferred_element_type=jnp.float32)
 
 
-def pack_body(x_ref, g_ref, pair_ref):
-    pair_ref[0] = x_ref[...]
-    pair_ref[1] = g_ref[...]
-
-
-def pack_call(start, rows, width, inputs, out_grad):
-    tokens = inputs.shape[0]
+def pack_body(*refs):
+    pair_ref = refs[-1]
+    for kind, ref in enumerate(refs[:-1]):
+        pair_ref[kind] = ref[...]
+
+
+def pack_call(start, rows, width, *arrays):
+    tokens = arrays[0].shape[0]
+    kinds = len(arrays)
     column = pl.BlockSpec((tokens, width), lambda i: (0, start + i))
-    size = 2 * tokens * rows * width
+    size = kinds * tokens * rows * width
     return pl.pallas_call(
         pack_body,
         grid=(rows,),
-        in_specs=[column, column],
-        out_specs=pl.BlockSpec((2, tokens, width), lambda i: (0, 0, i)),
-        out_shape=jax.ShapeDtypeStruct((2, tokens, rows * width), inputs.dtype),
+        in_specs=[column] * kinds,
+        out_specs=pl.BlockSpec((kinds, tokens, width), lambda i: (0, 0, i)),
+        out_shape=jax.ShapeDtypeStruct((kinds, tokens, rows * width), arrays[0].dtype),
         cost_estimate=pl.CostEstimate(flops=0, bytes_accessed=4 * size, transcendentals=0),
         name="pack",
-    )(inputs, out_grad)
+    )(*arrays)
 
 
 def main_body(dims, slots_ref, parity_ref, *refs):
-    local, bits, rows, width, _, halves, _, has_prior = dims
+    local, bits, rows, width, _, halves, _, has_prior, apart, came_apart = dims
     x_hbm, g_hbm = refs[0], refs[1]
-    arrived = refs[2 : 2 + bits]
-    at = 2 + bits
+    arrived = refs[2 : 2 + bits * (1 + int(came_apart))]
+    at = 2 + len(arrived)
     prior = refs[at] if has_prior else None
     at += int(has_prior)
     up_ref, down_ref = refs[at], refs[at + 1]
     acc_hbm = refs[at + 2]
-    sent = refs[at + 3 : at + 3 + bits]
-    keep_ref, send_ref = refs[at + 3 + bits], refs[at + 4 + bits]
-    cand, acc, stage, square, in_sems, acc_sems, out_sems = refs[at + 5 + bits :]
+    outs = refs[at + 3 : at + 3 + bits * (1 + int(apart))]
+    at += 3 + len(outs)
+    keep_ref, send_ref = refs[at], refs[at + 1]
+    cand, acc, stage, square, in_sems, acc_sems, out_sems = refs[at + 2 :]
     step = pl.program_id(0)
     last = pl.num_programs(0) - 1
 
@@ -84,7 +87,8 @@
         for kind in range(2):
             for bit in range(bits):
                 for row in range(rows):
-                    view = arrived[bit].at[kind, :, pl.ds(row * width, width)]
+                    whole = arrived[2 * bit + kind].at[0] if came_apart else arrived[bit].at[kind]
+                    view = whole.at[:, pl.ds(row * width, width)]
                     copies.append((view, cand.at[kind, local + bit * rows + row]))
         return [pltpu.make_async_copy(a, b, in_sems.at[i]) for i, (a, b) in enumerate(copies)]
 
@@ -98,6 +102,10 @@
                 ends = ends if store else ends[::-1]
                 copies.append(pltpu.make_async_copy(*ends, acc_sems.at[index]))
         return copies
+
+    def out_copy(bit, kind):
+        far = outs[2 * bit + kind].at[0] if apart else outs[bit].at[kind]
+        return pltpu.make_async_copy(stage.at[bit, kind], far, out_sems.at[2 * bit + kind])
 
     @pl.when(step == 0)
     def _():
@@ -148,29 +156,31 @@
     def _():
         for copy in acc_copy(True):
             copy.start()
-        for bit in range(bits):
-            for kind in range(2):
-                for row in range(rows):
-                    total = acc[kind, local + bit * rows + row]
-                    stage[bit, kind, :, pl.ds(row * width, width)] = total.astype(jnp.bfloat16)
-            pltpu.make_async_copy(stage.at[bit], sent[bit], out_sems.at[bit]).start()
-        for bit in range(bits):
-            pltpu.make_async_copy(stage.at[bit], sent[bit], out_sems.at[bit]).wait()
+        order = [(bit, kind) for bit in range(bits) for kind in range(2)]
+        for bit, kind in order:
+            for row in range(rows):
+                total = acc[kind, local + bit * rows + row]
+                stage[bit, kind, :, pl.ds(row * width, width)] = total.astype(jnp.bfloat16)
+            out_copy(bit, kind).start()
+        for bit, kind in order:
+            out_copy(bit, kind).wait()
         for copy in acc_copy(True):
             copy.wait()
 
 
-def main_call(start, rows, slots, parity, inputs, out_grad, arrived, prior, w_up, w_down, halves):
+def main_call(start, rows, slots, parity, inputs, out_grad, arrived, prior, w_up, w_down, halves, apart):
     tokens, features = inputs.shape
     slot_kinds, columns, width, _ = w_up.shape
     local = features // width
-    bits = len(arrived)
+    came_apart = arrived[0].shape[0] == 1
+    bits = len(arrived) // (1 + int(came_apart))
     cols = columns * rows // local
     slot_count = local + bits * rows
     first = start * columns // local
     has_prior = prior is not None
     piece = width // (2 * halves)
-    dims = (local, bits, rows, width, slot_count, halves, first, has_prior)
+    dims = (local, bits, rows, width, slot_count, halves, first, has_prior, apart, came_apart)
+    sends = bits * (1 + int(apart))
     anywhere = pl.BlockSpec(memory_space=pl.ANY)
     weight = pl.BlockSpec((slot_kinds, 1, width, width), lambda i, *_: (0, first + i, 0, 0))
     grad_block = pl.BlockSpec((1, halves, 2, slot_kinds, piece, width), lambda i, *_: (i, 0, 0, 0, 0, 0))
@@ -184,7 +194,7 @@
             num_scalar_prefetch=2,
             grid=(cols,),
             in_specs=[anywhere] * (len(operands) - 2) + [weight, weight],
-            out_specs=[anywhere] * (1 + bits) + [grad_block, grad_block],
+            out_specs=[anywhere] * (1 + sends) + [grad_block, grad_block],
             scratch_shapes=[
                 pltpu.VMEM((2, slot_count, tokens, width), jnp.bfloat16),
                 pltpu.VMEM((2, slot_count, tokens, width), jnp.float32),
@@ -192,12 +202,12 @@
                 pltpu.VMEM((2, width, width), jnp.float32),
                 pltpu.SemaphoreType.DMA((2 * slot_count,)),
                 pltpu.SemaphoreType.DMA((2 * local,)),
-                pltpu.SemaphoreType.DMA((bits,)),
+                pltpu.SemaphoreType.DMA((2 * bits,)),
             ],
         ),
         out_shape=[
             jax.ShapeDtypeStruct((2, local, tokens, width), jnp.float32),
-            *[jax.ShapeDtypeStruct((2, tokens, rows * width), jnp.bfloat16)] * bits,
+            *[jax.ShapeDtypeStruct((2 * bits // sends, tokens, rows * width), jnp.bfloat16)] * sends,
             grad_shape,
             grad_shape,
         ],
@@ -268,34 +278,46 @@
     )(keep, recv, *prior)
 
 
-def total_body(bits, acc_ref, *refs):
-    out_refs = refs[-2:]
-    for kind in range(2):
+def total_body(bits, kinds, acc_ref, *refs):
+    out_refs = refs[-kinds:]
+    for kind in range(kinds):
         total = acc_ref[kind, 0]
         for bit in range(bits):
             total = total + refs[bit][kind].astype(jnp.float32)
         out_refs[kind][...] = total.astype(jnp.bfloat16)
 
 
-def total_call(start, rows, acc, arrived, prior):
+def total_call(start, rows, first_kind, acc, arrived, prior):
     _, local, tokens, width = acc.shape
     bits = len(arrived)
+    kinds = arrived[0].shape[0]
     tile = tokens // 2
-    acc_spec = pl.BlockSpec((2, 1, tile, width), lambda i, t: (0, start + i, t, 0))
-    recv_spec = pl.BlockSpec((2, tile, width), lambda i, t: (0, t, i))
+    acc_spec = pl.BlockSpec((kinds, 1, tile, width), lambda i, t: (first_kind, start + i, t, 0))
+    recv_spec = pl.BlockSpec((kinds, tile, width), lambda i, t: (0, t, i))
     out_spec = pl.BlockSpec((tile, width), lambda i, t: (t, start + i))
     out_shape = jax.ShapeDtypeStruct((tokens, local * width), jnp.bfloat16)
-    size = 2 * rows * tokens * width
+    size = kinds * rows * tokens * width
     return pl.pallas_call(
-        functools.partial(total_body, bits),
+        functools.partial(total_body, bits, kinds),
         grid=(rows, 2),
         in_specs=[acc_spec] + [recv_spec] * bits + [pl.BlockSpec(memory_space=pl.ANY)] * len(prior),
-        out_specs=[out_spec, out_spec],
-        out_shape=[out_shape, out_shape],
+        out_specs=[out_spec] * kinds,
+        out_shape=[out_shape] * kinds,
         input_output_aliases={1 + bits + i: i for i in range(len(prior))},
         cost_estimate=pl.CostEstimate(flops=size * bits, bytes_accessed=(6 + 2 * bits) * size, transcendentals=0),
         name="totals",
     )(acc, *arrived, *prior)
+
+
+def last_total(start, rows, acc, arrived, whole):
+    _, _, width = acc.shape
+    for row in range(rows):
+        lanes = slice(row * width, (row + 1) * width)
+        total = acc[start + row]
+        for value in arrived:
+            total = total + value[0, :, lanes].astype(jnp.float32)
+        whole = lax.dynamic_update_slice(whole, total.astype(whole.dtype), (0, (start + row) * width))
+    return whole
 
 
 def shards(inputs, out_grad, w_up, w_down, partners):
@@ -307,6 +329,7 @@
     sizes = row_groups(local)
     starts = [sum(sizes[:group]) for group in range(len(sizes))]
     per_row = columns // local
+    last = len(sizes) - 1
     device = lax.axis_index("mp")
     dp_index = lax.axis_index("dp")
 
@@ -319,9 +342,19 @@
     parities = [(dp_index // 2**bit % 2).reshape(1).astype(jnp.int32) for bit in range(dp_bits)]
 
     arrived = []
-    for start, rows in zip(starts, sizes):
-        pair = pack_call(start, rows, width, inputs, out_grad)
-        arrived.append([partner(pair, "mp", bit) for bit in range(bits)])
+    for group, (start, rows) in enumerate(zip(starts, sizes)):
+        if group == 0:
+            parts = []
+            for kind, array in enumerate((inputs, out_grad)):
+                if kind == 0:
+                    block = array[None, :, start * width : (start + rows) * width]
+                else:
+                    block = pack_call(start, rows, width, array)
+                parts.append([partner(block, "mp", bit) for bit in range(bits)])
+            arrived.append([parts[kind][bit] for bit in range(bits) for kind in range(2)])
+        else:
+            pair = pack_call(start, rows, width, inputs, out_grad)
+            arrived.append([partner(pair, "mp", bit) for bit in range(bits)])
 
     acc = None
     returned = []
@@ -331,10 +364,17 @@
         slots = slot[:, start * per_row : (start + rows) * per_row].reshape(-1)
         acc, *rest = main_call(
             start, rows, slots, parities[0], inputs, out_grad, arrived[group], acc, w_up, w_down,
-            2 ** (dp_bits - 1),
+            2 ** (dp_bits - 1), group == last,
         )
-        returned.append([partner(rest[bit], "mp", bit) for bit in range(bits)])
-        keep, send = rest[bits:]
+        sends = rest[:-2]
+        keep, send = rest[-2:]
+        if group == last:
+            parts = []
+            for kind in range(2):
+                parts.append([partner(sends[2 * bit + kind], "mp", bit) for bit in range(bits)])
+            returned.append(parts)
+        else:
+            returned.append([partner(sends[bit], "mp", bit) for bit in range(bits)])
         for bit in range(1, dp_bits):
             recv = partner(send, "dp", bit - 1)
             keep, send = halve_call(per_row, parities[bit], keep, recv)
@@ -344,9 +384,12 @@
     for group, start in enumerate(starts):
         grads = grads_call(start, per_row, columns, *kept[group], grads)
     totals = []
-    for group, (start, rows) in enumerate(zip(starts, sizes)):
-        totals = total_call(start, rows, acc, returned[group], totals)
-    return (*totals, *grads)
+    for group, (start, rows) in enumerate(zip(starts[:-1], sizes[:-1])):
+        totals = total_call(start, rows, 0, acc, returned[group], totals)
+    ends = []
+    for kind in range(2):
+        ends.append(last_total(starts[-1], sizes[-1], acc[kind], returned[-1][kind], totals[kind]))
+    return (*ends, *grads)
 
 
 def solution(mesh):

time: 498 us -> 526 us (1.056)
  waiting for transfers between devices: 299 us -> 317 us
  starting transfers between devices: 33.8 us -> 42.7 us
    ppermute x32 -> x38, waiting for transfers between devices: 299 us -> 317 us  [partner(): return lax.ppermute(value, axis, pairs)]
    ppermute x32 -> x38, starting transfers between devices: 33.8 us -> 42.7 us  [partner(): return lax.ppermute(value, axis, pairs)]
    pallas_call x8 -> x7, Pallas kernels: 27.1 us -> 24.5 us  [the longest x3 14.1 us: total_call(): pl.pallas_call(functools.partial(total_body, bits, kinds), grid=(rows, 2)...]
  transfers between devices with their start and end apart: 32 -> 38, of which waited for: 18 -> 22; matrix products, arithmetic and copies ran while one was open for 1% -> 1% of each run, Pallas kernels for 31% -> 28%
where the time goes in v4:
time: 526 us; the launch traced here: 524 us
  waiting for transfers between devices  317 us (60%)
  Pallas kernels  155 us (29%)
  starting transfers between devices  42.7 us (8%)
  local copies, waits for them, and re-layouts  6.28 us (1%)
    ppermute x38, waiting for transfers between devices, partner(): return lax.ppermute(value, axis, pairs)  317 us
    pallas_call x4, Pallas kernels, main_call(): pl.pallas_call(functools.partial(main_body, dims), grid_spec=pltpu.Prefet...  91.3 us
    ppermute x38, starting transfers between devices, partner(): return lax.ppermute(value, axis, pairs)  42.7 us
    pallas_call x4, Pallas kernels, halve_call(): pl.pallas_call(halve_body, grid_spec=pltpu.PrefetchScalarGridSpec(num_sca...  23.4 us
    pallas_call x4, Pallas kernels, grads_call(): pl.pallas_call(grads_body, grid=(cols // block,), in_specs=[spec, spec] +...  15.6 us
    pallas_call x3, Pallas kernels, total_call(): pl.pallas_call(functools.partial(total_body, bits, kinds), grid=(rows, 2)...  14.1 us
  transfers between devices with their start and end apart: 38, of which 22 were waited for; matrix products, arithmetic and copies ran while one was open for 1% of the time, Pallas kernels for 28%

profile of v4, /device:TPU:0, one launch (start us, length us, event | category | flops | bytes accessed | tf_op | source)
XLA Modules:
  0.0 524.4 jit_solution(1686160218266608198)
XLA Ops:
  0.6 3.4 pack.6
  4.0 3.0 collective-permute-start.6
  7.0 1.6 collective-permute-start.7
  8.5 2.6 collective-permute-start.8
  11.1 1.7 pack.7
  13.3 1.0 slice_bitcast_fusion
  14.8 32.4 %collective-permute-done.10.refs_3_ = bf16[1,512,256]{2,1,0:T(8,128)(2,1)S(1)} collective-permute-done((bf16[1,512,256]{2,1,0:T(8,128)(2,1)}, bf16[1,512,256]{2,1,0:T(8,128)(2,1)S(1)}, u32[]{:S(2)}, u32[]{:S(2)}) %collective-permute-start.10) | collective-permute-done | bytes 262176 | tf_op jit(solution)/shard_map/ppermute | solution.py:21
  47.2 1.8 collective-permute-start.12
  49.0 34.7 %collective-permute-done.11.refs_4_ = bf16[1,512,256]{2,1,0:T(8,128)(2,1)S(1)} collective-permute-done((bf16[1,512,256]{2,1,0:T(8,128)(2,1)S(1)}, bf16[1,512,256]{2,1,0:T(8,128)(2,1)S(1)}, u32[]{:S(2)}, u32[]{:S(2)}) %collective-permute-start.11) | collective-permute-done | bytes 262176 | tf_op jit(solution)/shard_map/ppermute | solution.py:21
  83.8 2.6 collective-permute-start.13
  86.4 6.3 %collective-permute-done.12.refs_5_ = bf16[1,512,256]{2,1,0:T(8,128)(2,1)S(1)} collective-permute-done((bf16[1,512,256]{2,1,0:T(8,128)(2,1)}, bf16[1,512,256]{2,1,0:T(8,128)(2,1)S(1)}, u32[]{:S(2)}, u32[]{:S(2)}) %collective-permute-start.12) | collective-permute-done | bytes 262176 | tf_op jit(solution)/shard_map/ppermute | solution.py:21
  92.8 10.4 %collective-permute-done.13.refs_6_ = bf16[1,512,256]{2,1,0:T(8,128)(2,1)S(1)} collective-permute-done((bf16[1,512,256]{2,1,0:T(8,128)(2,1)S(1)}, bf16[1,512,256]{2,1,0:T(8,128)(2,1)S(1)}, u32[]{:S(2)}, u32[]{:S(2)}) %collective-permute-start.13) | collective-permute-done | bytes 262176 | tf_op jit(solution)/shard_map/ppermute | solution.py:21
  103.2 3.5 pack.5
  106.7 1.2 collective-permute-done.14.refs_7_
  107.9 0.8 collective-permute-start.3
  108.7 0.9 collective-permute-done.9.refs_2_
  109.5 4.0 collective-permute-start.4
  113.6 3.5 collective-permute-start.5
  117.8 0.6 reshape.45.slots_ref
  119.1 14.5 %columns.4 = (f32[2,8,512,256]{3,2,1,0:T(8,128)}, bf16[2,512,256]{2,1,0:T(8,128)(2,1)}, bf16[2,512,256]{2,1,0:T(8,128)(2,1)}, bf16[2,512,256]{2,1,0:T(8,128)(2,1...) custom-call(s32[8]{0:T(128)} %reshape.46.slots_ref, s32[1]{0:T(128)} %bitcast.parity_ref, ...), custom_call_target="tpu_custom_call" | custom-call | flops 3221225472 | bytes 23592960 | tf_op jit(solution)/shard_map/columns/pallas_call | solution.py:191
  133.7 29.9 %columns.5 = (f32[2,8,512,256]{3,2,1,0:T(8,128)}, bf16[2,512,768]{2,1,0:T(8,128)(2,1)}, bf16[2,512,768]{2,1,0:T(8,128)(2,1)}, bf16[2,512,768]{2,1,0:T(8,128)(2,1...) custom-call(s32[24]{0:T(128)} %reshape.45.slots_ref, s32[1]{0:T(128)} %bitcast.parity_ref, ...), custom_call_target="tpu_custom_call" | custom-call | flops 9663676416 | bytes 45613056 | tf_op jit(solution)/shard_map/columns/pallas_call | solution.py:191
  163.6 13.0 %collective-permute-done.4.refs_3_ = bf16[2,512,768]{2,1,0:T(8,128)(2,1)} collective-permute-done((bf16[2,512,768]{2,1,0:T(8,128)(2,1)}, bf16[2,512,768]{2,1,0:T(8,128)(2,1)}, u32[]{:S(2)}, u32[]{:S(2)}) %collective-permute-start.4) | collective-permute-done | bytes 1572896 | tf_op jit(solution)/shard_map/ppermute | solution.py:21
  176.6 2.1 collective-permute-done.5.refs_4_
  178.7 29.8 %columns.6 = (f32[2,8,512,256]{3,2,1,0:T(8,128)}, bf16[2,512,768]{2,1,0:T(8,128)(2,1)}, bf16[2,512,768]{2,1,0:T(8,128)(2,1)}, bf16[2,512,768]{2,1,0:T(8,128)(2,1...) custom-call(s32[24]{0:T(128)} %reshape.44.slots_ref, s32[1]{0:T(128)} %bitcast.parity_ref, ...), custom_call_target="tpu_custom_call" | custom-call | flops 9663676416 | bytes 45613056 | tf_op jit(solution)/shard_map/columns/pallas_call | solution.py:191
  208.6 1.9 pack.4
  210.5 1.5 collective-permute-start
  212.0 2.1 collective-permute-start.2
  214.1 10.9 %collective-permute-done.refs_2_ = bf16[2,512,256]{2,1,0:T(8,128)(2,1)S(1)} collective-permute-done((bf16[2,512,256]{2,1,0:T(8,128)(2,1)}, bf16[2,512,256]{2,1,0:T(8,128)(2,1)S(1)}, u32[]{:S(2)}, u32[]{:S(2)}) %collective-permute-start) | collective-permute-done | bytes 524320 | tf_op jit(solution)/shard_map/ppermute | solution.py:21
  225.0 1.5 collective-permute-start.21
  226.5 10.0 %collective-permute-done.1.refs_3_ = bf16[2,512,256]{2,1,0:T(8,128)(2,1)S(1)} collective-permute-done((bf16[2,512,256]{2,1,0:T(8,128)(2,1)}, bf16[2,512,256]{2,1,0:T(8,128)(2,1)S(1)}, u32[]{:S(2)}, u32[]{:S(2)}) %collective-permute-start.1) | collective-permute-done | bytes 524320 | tf_op jit(solution)/shard_map/ppermute | solution.py:21
  236.5 1.9 collective-permute-done.2.refs_4_
  238.4 0.8 copy-done.4
  239.2 0.7 reshape.42.slots_ref
  239.9 0.9 collective-permute-start.23
  240.8 17.1 %columns.7 = (f32[2,8,512,256]{3,2,1,0:T(8,128)}, bf16[1,512,256]{2,1,0:T(8,128)(2,1)}, bf16[1,512,256]{2,1,0:T(8,128)(2,1)}, bf16[1,512,256]{2,1,0:T(8,128)(2,1...) custom-call(s32[8]{0:T(128)} %reshape.42.slots_ref, ...), custom_call_target="tpu_custom_call" | custom-call | flops 3221225472 | bytes 23592960 | tf_op jit(solution)/shard_map/columns/pallas_call | solution.py:191
  258.5 8.1 %collective-permute-done.23.refs_2_ = bf16[2,512,256]{2,1,0:T(8,128)(2,1)S(1)} collective-permute-done((bf16[2,512,256]{2,1,0:T(8,128)(2,1)}, bf16[2,512,256]{2,1,0:T(8,128)(2,1)S(1)}, u32[]{:S(2)}, u32[]{:S(2)}) %collective-permute-start.23) | collective-permute-done | bytes 524320 | tf_op jit(solution)/shard_map/ppermute | solution.py:21
  266.7 2.1 collective-permute-start.26
  268.8 10.5 %collective-permute-done.25 = bf16[1,512,256]{2,1,0:T(8,128)(2,1)S(1)} collective-permute-done((bf16[1,512,256]{2,1,0:T(8,128)(2,1)}, bf16[1,512,256]{2,1,0:T(8,128)(2,1)S(1)}, u32[]{:S(2)}, u32[]{:S(2)}) %collective-permute-start.25) | collective-permute-done | bytes 262176 | tf_op jit(solution)/shard_map/ppermute | solution.py:21
  279.8 1.6 collective-permute-done.26
  281.9 38.5 %collective-permute-done.27 = bf16[1,512,256]{2,1,0:T(8,128)(2,1)S(1)} collective-permute-done((bf16[1,512,256]{2,1,0:T(8,128)(2,1)}, bf16[1,512,256]{2,1,0:T(8,128)(2,1)S(1)}, u32[]{:S(2)}, u32[]{:S(2)}) %collective-permute-start.27) | collective-permute-done | bytes 262176 | tf_op jit(solution)/shard_map/ppermute | solution.py:21
  320.4 6.6 %collective-permute-done.28 = bf16[1,512,256]{2,1,0:T(8,128)(2,1)S(1)} collective-permute-done((bf16[1,512,256]{2,1,0:T(8,128)(2,1)}, bf16[1,512,256]{2,1,0:T(8,128)(2,1)S(1)}, u32[]{:S(2)}, u32[]{:S(2)}) %collective-permute-start.28) | collective-permute-done | bytes 262176 | tf_op jit(solution)/shard_map/ppermute | solution.py:21
  327.3 2.6 collective-permute-start.20
  330.5 8.0 %halve.6 = (f32[12,1,2,2,64,256]{5,4,3,2,1,0:T(8,128)}, f32[12,1,2,2,64,256]{5,4,3,2,1,0:T(8,128)}) custom-call(s32[1]{0:T(128)} %bitcast.10.parity_ref, f32[12,2,2,2,64,256]{5,4,3,2,1,0:T(8,128)} %get-tuple-element.86.keep_ref, f32[12,2,2,2,64,256]{5,4,3,2,1,0:T(8,128)} %collective-permute-done.34.recv_ref), custom_call_target="tpu_custom_call" | custom-call | flops 1572864 | bytes 18874368 | tf_op jit(solution)/shard_map/halve/pallas_call | solution.py:241
  338.5 1.6 collective-permute-start.35
  340.1 7.9 %halve.5 = (f32[12,1,2,2,64,256]{5,4,3,2,1,0:T(8,128)}, f32[12,1,2,2,64,256]{5,4,3,2,1,0:T(8,128)}) custom-call(s32[1]{0:T(128)} %bitcast.10.parity_ref, f32[12,2,2,2,64,256]{5,4,3,2,1,0:T(8,128)} %get-tuple-element.82.keep_ref, f32[12,2,2,2,64,256]{5,4,3,2,1,0:T(8,128)} %collective-permute-done.32.recv_ref), custom_call_target="tpu_custom_call" | custom-call | flops 1572864 | bytes 18874368 | tf_op jit(solution)/shard_map/halve/pallas_call | solution.py:241
  348.0 46.2 %collective-permute-done.19.refs_1_ = bf16[2,512,768]{2,1,0:T(8,128)(2,1)} collective-permute-done((bf16[2,512,768]{2,1,0:T(8,128)(2,1)}, bf16[2,512,768]{2,1,0:T(8,128)(2,1)}, u32[]{:S(2)}, u32[]{:S(2)}) %collective-permute-start.19) | collective-permute-done | bytes 1572896 | tf_op jit(solution)/shard_map/ppermute | solution.py:21
  394.3 1.5 collective-permute-start.33
  396.1 2.7 collective-permute-start.17
  398.8 3.7 halve.7
  402.5 1.6 collective-permute-start.37
  404.1 3.8 halve.4
  407.9 55.6 %collective-permute-done.16.refs_1_ = bf16[2,512,768]{2,1,0:T(8,128)(2,1)} collective-permute-done((bf16[2,512,768]{2,1,0:T(8,128)(2,1)}, bf16[2,512,768]{2,1,0:T(8,128)(2,1)}, u32[]{:S(2)}, u32[]{:S(2)}) %collective-permute-start.16) | collective-permute-done | bytes 1572896 | tf_op jit(solution)/shard_map/ppermute | solution.py:21
  464.0 1.6 collective-permute-done.17.refs_2_
  465.9 2.4 totals.3
  468.3 5.8 %totals.4 = (bf16[512,2048]{1,0:T(8,128)(2,1)}, bf16[512,2048]{1,0:T(8,128)(2,1)}) custom-call(f32[2,8,512,256]{3,2,1,0:T(8,128)} %get-tuple-element.56.acc_ref, bf16[2,512,768]{2,1,0:T(8,128)(2,1)} %collective-permute-done.18.refs_0_, bf16[2,512,768]{2,1,0:T(8,128)(2,1)} %collective-permute-done.19.refs_1_, ...), custom_call_target="tpu_custom_call", output_to_operand_aliasing={{0}: (4, {}), {1}: (5, {})} | custom-call | flops 2359296 | bytes 9437184 | tf_op jit(solution)/shard_map/totals/pallas_call | solution.py:300
  474.1 5.8 %totals.5 = (bf16[512,2048]{1,0:T(8,128)(2,1)}, bf16[512,2048]{1,0:T(8,128)(2,1)}) custom-call(f32[2,8,512,256]{3,2,1,0:T(8,128)} %get-tuple-element.56.acc_ref, bf16[2,512,768]{2,1,0:T(8,128)(2,1)} %collective-permute-done.15.refs_0_, bf16[2,512,768]{2,1,0:T(8,128)(2,1)} %collective-permute-done.16.refs_1_, ...), custom_call_target="tpu_custom_call", output_to_operand_aliasing={{0}: (4, {}), {1}: (5, {})} | custom-call | flops 2359296 | bytes 9437184 | tf_op jit(solution)/shard_map/totals/pallas_call | solution.py:300
  480.0 2.6 fusion.3
  482.6 17.2 %collective-permute-done.37.recv_ref = f32[4,1,2,2,64,256]{5,4,3,2,1,0:T(8,128)} collective-permute-done((f32[4,1,2,2,64,256]{5,4,3,2,1,0:T(8,128)}, f32[4,1,2,2,64,256]{5,4,3,2,1,0:T(8,128)}, u32[]{:S(2)}, u32[]{:S(2)}) %collective-permute-start.37) | collective-permute-done | bytes 1048608 | tf_op jit(solution)/shard_map/ppermute | solution.py:21
  499.8 2.6 grads.4
  502.4 1.8 copy-done
  504.1 5.2 grads.5
  509.3 5.2 grads.6
  514.5 7.3 %collective-permute-done.31.recv_ref = f32[4,1,2,2,64,256]{5,4,3,2,1,0:T(8,128)} collective-permute-done((f32[4,1,2,2,64,256]{5,4,3,2,1,0:T(8,128)}, f32[4,1,2,2,64,256]{5,4,3,2,1,0:T(8,128)}, u32[]{:S(2)}, u32[]{:S(2)}) %collective-permute-start.31) | collective-permute-done | bytes 1048608 | tf_op jit(solution)/shard_map/ppermute | solution.py:21
  521.8 2.6 grads.7
  (78 shorter events, 6.5 us)
Async XLA Ops:
  4.0 109.6 %collective-permute-start.6 = (bf16[2,512,768]{2,1,0:T(8,128)(2,1)}, bf16[2,512,768]{2,1,0:T(8,128)(2,1)S(1)}, u32[]{:S(2)}, u32[]{:S(2)}) collective-permute-start(bf16[2,512,768]{2,1,0:T(8,128)(2,1)} %pack.6), channel_id=1, source_target_pairs={{0,1},{1,0},{2,3},{3,2},{4,5},{5,4},{6,7},{7,6},{8,9},{9,8},{10,11... | collective-permute-start | bytes 4718600 | tf_op jit(solution)/shard_map/ppermute | solution.py:21
  7.0 126.7 %collective-permute-start.7 = (bf16[2,512,768]{2,1,0:T(8,128)(2,1)}, bf16[2,512,768]{2,1,0:T(8,128)(2,1)}, u32[]{:S(2)}, u32[]{:S(2)}) collective-permute-start(bf16[2,512,768]{2,1,0:T(8,128)(2,1)} %pack.6), channel_id=1, source_target_pairs={{0,2},{1,3},{2,0},{3,1},{4,6},{5,7},{6,4},{7,5},{8,10},{9,11},{10,... | collective-permute-start | bytes 4718600 | tf_op jit(solution)/shard_map/ppermute | solution.py:21
  8.5 125.1 %collective-permute-start.8 = (bf16[2,512,768]{2,1,0:T(8,128)(2,1)}, bf16[2,512,768]{2,1,0:T(8,128)(2,1)}, u32[]{:S(2)}, u32[]{:S(2)}) collective-permute-start(bf16[2,512,768]{2,1,0:T(8,128)(2,1)} %pack.6), channel_id=1, source_target_pairs={{0,4},{1,5},{2,6},{3,7},{4,0},{5,1},{6,2},{7,3},{8,12},{9,13},{10,... | collective-permute-start | bytes 4718600 | tf_op jit(solution)/shard_map/ppermute | solution.py:21
  12.8 34.4 %collective-permute-start.10 = (bf16[1,512,256]{2,1,0:T(8,128)(2,1)}, bf16[1,512,256]{2,1,0:T(8,128)(2,1)S(1)}, u32[]{:S(2)}, u32[]{:S(2)}) collective-permute-start(bf16[1,512,256]{2,1,0:T(8,128)(2,1)} %pack.7), channel_id=1, source_target_pairs={{0,1},{1,0},{2,3},{3,2},{4,5},{5,4},{6,7},{7,6},{8,9},{9,8},{10,11... | collective-permute-start | bytes 786440 | tf_op jit(solution)/shard_map/ppermute | solution.py:21
  14.3 69.5 %collective-permute-start.11 = (bf16[1,512,256]{2,1,0:T(8,128)(2,1)S(1)}, bf16[1,512,256]{2,1,0:T(8,128)(2,1)S(1)}, u32[]{:S(2)}, u32[]{:S(2)}) collective-permute-start(bf16[1,512,256]{2,1,0:T(8,128)(2,1)S(1)} %slice_bitcast_fusion), channel_id=1, source_target_pairs={{0,2},{1,3},{2,0},{3,1},{4,6},{5,7},{6,4},{7,5},{8,10},{9,11},{10,... | collective-permute-start | bytes 786440 | tf_op jit(solution)/shard_map/ppermute | solution.py:21
  47.2 59.5 %copy-start.6 = (bf16[1,512,256]{2,1,0:T(8,128)(2,1)}, bf16[1,512,256]{2,1,0:T(8,128)(2,1)S(1)}, u32[]{:S(2)}) copy-start(bf16[1,512,256]{2,1,0:T(8,128)(2,1)S(1)} %collective-permute-done.10.refs_3_) | copy-start | bytes 786436
  47.2 45.5 %collective-permute-start.12 = (bf16[1,512,256]{2,1,0:T(8,128)(2,1)}, bf16[1,512,256]{2,1,0:T(8,128)(2,1)S(1)}, u32[]{:S(2)}, u32[]{:S(2)}) collective-permute-start(bf16[1,512,256]{2,1,0:T(8,128)(2,1)} %pack.7), channel_id=1, source_target_pairs={{0,2},{1,3},{2,0},{3,1},{4,6},{5,7},{6,4},{7,5},{8,10},{9,11},{10,... | collective-permute-start | bytes 786440 | tf_op jit(solution)/shard_map/ppermute | solution.py:21
  83.8 22.9 %copy-start.7 = (bf16[1,512,256]{2,1,0:T(8,128)(2,1)}, bf16[1,512,256]{2,1,0:T(8,128)(2,1)S(1)}, u32[]{:S(2)}) copy-start(bf16[1,512,256]{2,1,0:T(8,128)(2,1)S(1)} %collective-permute-done.11.refs_4_) | copy-start | bytes 786436
  83.8 19.4 %collective-permute-start.13 = (bf16[1,512,256]{2,1,0:T(8,128)(2,1)S(1)}, bf16[1,512,256]{2,1,0:T(8,128)(2,1)S(1)}, u32[]{:S(2)}, u32[]{:S(2)}) collective-permute-start(bf16[1,512,256]{2,1,0:T(8,128)(2,1)S(1)} %slice_bitcast_fusion), channel_id=1, source_target_pairs={{0,4},{1,5},{2,6},{3,7},{4,0},{5,1},{6,2},{7,3},{8,12},{9,13},{10,... | collective-permute-start | bytes 786440 | tf_op jit(solution)/shard_map/ppermute | solution.py:21
  92.7 13.9 %copy-start.8 = (bf16[1,512,256]{2,1,0:T(8,128)(2,1)}, bf16[1,512,256]{2,1,0:T(8,128)(2,1)S(1)}, u32[]{:S(2)}) copy-start(bf16[1,512,256]{2,1,0:T(8,128)(2,1)S(1)} %collective-permute-done.12.refs_5_) | copy-start | bytes 786436
  92.7 15.2 %collective-permute-start.14 = (bf16[1,512,256]{2,1,0:T(8,128)(2,1)}, bf16[1,512,256]{2,1,0:T(8,128)(2,1)S(1)}, u32[]{:S(2)}, u32[]{:S(2)}) collective-permute-start(bf16[1,512,256]{2,1,0:T(8,128)(2,1)} %pack.7), channel_id=1, source_target_pairs={{0,4},{1,5},{2,6},{3,7},{4,0},{5,1},{6,2},{7,3},{8,12},{9,13},{10,... | collective-permute-start | bytes 786440 | tf_op jit(solution)/shard_map/ppermute | solution.py:21
  103.2 3.5 copy-start.9
  103.2 6.4 %collective-permute-start.9 = (bf16[1,512,256]{2,1,0:T(8,128)(2,1)S(1)}, bf16[1,512,256]{2,1,0:T(8,128)(2,1)S(1)}, u32[]{:S(2)}, u32[]{:S(2)}) collective-permute-start(bf16[1,512,256]{2,1,0:T(8,128)(2,1)S(1)} %slice_bitcast_fusion), channel_id=1, source_target_pairs={{0,1},{1,0},{2,3},{3,2},{4,5},{5,4},{6,7},{7,6},{8,9},{9,8},{10,11... | collective-permute-start | bytes 786440 | tf_op jit(solution)/shard_map/ppermute | solution.py:21
  103.2 13.9 %copy-start.16 = (s32[2,32]{1,0:T(2,128)S(1)}, s32[2,32]{1,0:T(2,128)}, u32[]{:S(2)}) copy-start(s32[2,32]{1,0:T(2,128)} %param.9) | copy-start | bytes 772
  107.9 11.2 %copy-start.10 = (bf16[1,512,256]{2,1,0:T(8,128)(2,1)}, bf16[1,512,256]{2,1,0:T(8,128)(2,1)S(1)}, u32[]{:S(2)}) copy-start(bf16[1,512,256]{2,1,0:T(8,128)(2,1)S(1)} %collective-permute-done.14.refs_7_) | copy-start | bytes 786436
  107.9 55.7 %collective-permute-start.3 = (bf16[2,512,768]{2,1,0:T(8,128)(2,1)}, bf16[2,512,768]{2,1,0:T(8,128)(2,1)}, u32[]{:S(2)}, u32[]{:S(2)}) collective-permute-start(bf16[2,512,768]{2,1,0:T(8,128)(2,1)} %pack.5), channel_id=1, source_target_pairs={{0,1},{1,0},{2,3},{3,2},{4,5},{5,4},{6,7},{7,6},{8,9},{9,8},{10,11... | collective-permute-start | bytes 4718600 | tf_op jit(solution)/shard_map/ppermute | solution.py:21
  109.5 9.6 %copy-start.11 = (bf16[1,512,256]{2,1,0:T(8,128)(2,1)}, bf16[1,512,256]{2,1,0:T(8,128)(2,1)S(1)}, u32[]{:S(2)}) copy-start(bf16[1,512,256]{2,1,0:T(8,128)(2,1)S(1)} %collective-permute-done.9.refs_2_) | copy-start | bytes 786436
  109.5 67.1 %collective-permute-start.4 = (bf16[2,512,768]{2,1,0:T(8,128)(2,1)}, bf16[2,512,768]{2,1,0:T(8,128)(2,1)}, u32[]{:S(2)}, u32[]{:S(2)}) collective-permute-start(bf16[2,512,768]{2,1,0:T(8,128)(2,1)} %pack.5), channel_id=1, source_target_pairs={{0,2},{1,3},{2,0},{3,1},{4,6},{5,7},{6,4},{7,5},{8,10},{9,11},{10,... | collective-permute-start | bytes 4718600 | tf_op jit(solution)/shard_map/ppermute | solution.py:21
  113.6 4.1 copy-start.17
  113.6 65.1 %collective-permute-start.5 = (bf16[2,512,768]{2,1,0:T(8,128)(2,1)}, bf16[2,512,768]{2,1,0:T(8,128)(2,1)}, u32[]{:S(2)}, u32[]{:S(2)}) collective-permute-start(bf16[2,512,768]{2,1,0:T(8,128)(2,1)} %pack.5), channel_id=1, source_target_pairs={{0,4},{1,5},{2,6},{3,7},{4,0},{5,1},{6,2},{7,3},{8,12},{9,13},{10,... | collective-permute-start | bytes 4718600 | tf_op jit(solution)/shard_map/ppermute | solution.py:21
  163.5 167.0 %collective-permute-start.34 = (f32[12,2,2,2,64,256]{5,4,3,2,1,0:T(8,128)}, f32[12,2,2,2,64,256]{5,4,3,2,1,0:T(8,128)}, u32[]{:S(2)}, u32[]{:S(2)}) collective-permute-start(f32[12,2,2,2,64,256]{5,4,3,2,1,0:T(8,128)} %get-tuple-element.87), channel_id=1, source_target_pairs={{0,8},{8,0},{16,24},{24,16},{1,9},{9,1},{17,25},{25,17},{2,10},{10... | collective-permute-start | bytes 18874376 | tf_op jit(solution)/shard_map/ppermute | solution.py:21
  208.5 130.0 %collective-permute-start.32 = (f32[12,2,2,2,64,256]{5,4,3,2,1,0:T(8,128)}, f32[12,2,2,2,64,256]{5,4,3,2,1,0:T(8,128)}, u32[]{:S(2)}, u32[]{:S(2)}) collective-permute-start(f32[12,2,2,2,64,256]{5,4,3,2,1,0:T(8,128)} %get-tuple-element.83), channel_id=1, source_target_pairs={{0,8},{8,0},{16,24},{24,16},{1,9},{9,1},{17,25},{25,17},{2,10},{10... | collective-permute-start | bytes 18874376 | tf_op jit(solution)/shard_map/ppermute | solution.py:21
  210.5 14.5 %collective-permute-start = (bf16[2,512,256]{2,1,0:T(8,128)(2,1)}, bf16[2,512,256]{2,1,0:T(8,128)(2,1)S(1)}, u32[]{:S(2)}, u32[]{:S(2)}) collective-permute-start(bf16[2,512,256]{2,1,0:T(8,128)(2,1)} %pack.4), channel_id=1, source_target_pairs={{0,1},{1,0},{2,3},{3,2},{4,5},{5,4},{6,7},{7,6},{8,9},{9,8},{10,11... | collective-permute-start | bytes 1572872 | tf_op jit(solution)/shard_map/ppermute | solution.py:21
  212.0 24.5 %collective-permute-start.1 = (bf16[2,512,256]{2,1,0:T(8,128)(2,1)}, bf16[2,512,256]{2,1,0:T(8,128)(2,1)S(1)}, u32[]{:S(2)}, u32[]{:S(2)}) collective-permute-start(bf16[2,512,256]{2,1,0:T(8,128)(2,1)} %pack.4), channel_id=1, source_target_pairs={{0,2},{1,3},{2,0},{3,1},{4,6},{5,7},{6,4},{7,5},{8,10},{9,11},{10,... | collective-permute-start | bytes 1572872 | tf_op jit(solution)/shard_map/ppermute | solution.py:21
  212.0 26.4 %collective-permute-start.2 = (bf16[2,512,256]{2,1,0:T(8,128)(2,1)}, bf16[2,512,256]{2,1,0:T(8,128)(2,1)S(1)}, u32[]{:S(2)}, u32[]{:S(2)}) collective-permute-start(bf16[2,512,256]{2,1,0:T(8,128)(2,1)} %pack.4), channel_id=1, source_target_pairs={{0,4},{1,5},{2,6},{3,7},{4,0},{5,1},{6,2},{7,3},{8,12},{9,13},{10,... | collective-permute-start | bytes 1572872 | tf_op jit(solution)/shard_map/ppermute | solution.py:21
  225.0 15.8 %copy-start.2 = (bf16[2,512,256]{2,1,0:T(8,128)(2,1)}, bf16[2,512,256]{2,1,0:T(8,128)(2,1)S(1)}, u32[]{:S(2)}) copy-start(bf16[2,512,256]{2,1,0:T(8,128)(2,1)S(1)} %collective-permute-done.refs_2_) | copy-start | bytes 1572868
  225.0 14.9 %collective-permute-start.21 = (bf16[2,512,256]{2,1,0:T(8,128)(2,1)}, bf16[2,512,256]{2,1,0:T(8,128)(2,1)}, u32[]{:S(2)}, u32[]{:S(2)}) collective-permute-start(bf16[2,512,256]{2,1,0:T(8,128)(2,1)} %get-tuple-element.63), channel_id=1, source_target_pairs={{0,1},{1,0},{2,3},{3,2},{4,5},{5,4},{6,7},{7,6},{8,9},{9,8},{10,11... | collective-permute-start | bytes 1572872 | tf_op jit(solution)/shard_map/ppermute | solution.py:21
  236.5 4.3 copy-start.3
  236.5 21.4 %collective-permute-start.22 = (bf16[2,512,256]{2,1,0:T(8,128)(2,1)}, bf16[2,512,256]{2,1,0:T(8,128)(2,1)}, u32[]{:S(2)}, u32[]{:S(2)}) collective-permute-start(bf16[2,512,256]{2,1,0:T(8,128)(2,1)} %get-tuple-element.64), channel_id=1, source_target_pairs={{0,2},{1,3},{2,0},{3,1},{4,6},{5,7},{6,4},{7,5},{8,10},{9,11},{10,... | collective-permute-start | bytes 1572872 | tf_op jit(solution)/shard_map/ppermute | solution.py:21
  238.4 0.8 copy-start.4
  239.2 88.1 %collective-permute-start.36 = (f32[4,2,2,2,64,256]{5,4,3,2,1,0:T(8,128)}, f32[4,2,2,2,64,256]{5,4,3,2,1,0:T(8,128)S(1)}, u32[]{:S(2)}, u32[]{:S(2)}) collective-permute-start(f32[4,2,2,2,64,256]{5,4,3,2,1,0:T(8,128)} %get-tuple-element.91), channel_id=1, source_target_pairs={{0,8},{8,0},{16,24},{24,16},{1,9},{9,1},{17,25},{25,17},{2,10},{10... | collective-permute-start | bytes 6291464 | tf_op jit(solution)/shard_map/ppermute | solution.py:21
  239.9 26.7 %collective-permute-start.23 = (bf16[2,512,256]{2,1,0:T(8,128)(2,1)}, bf16[2,512,256]{2,1,0:T(8,128)(2,1)S(1)}, u32[]{:S(2)}, u32[]{:S(2)}) collective-permute-start(bf16[2,512,256]{2,1,0:T(8,128)(2,1)} %get-tuple-element.65), channel_id=1, source_target_pairs={{0,4},{1,5},{2,6},{3,7},{4,0},{5,1},{6,2},{7,3},{8,12},{9,13},{10,... | collective-permute-start | bytes 1572872 | tf_op jit(solution)/shard_map/ppermute | solution.py:21
  257.9 8.7 %collective-permute-start.24 = (bf16[1,512,256]{2,1,0:T(8,128)(2,1)}, bf16[1,512,256]{2,1,0:T(8,128)(2,1)S(1)}, u32[]{:S(2)}, u32[]{:S(2)}) collective-permute-start(bf16[1,512,256]{2,1,0:T(8,128)(2,1)} %get-tuple-element.71), channel_id=1, source_target_pairs={{0,1},{1,0},{2,3},{3,2},{4,5},{5,4},{6,7},{7,6},{8,9},{9,8},{10,11... | collective-permute-start | bytes 786440 | tf_op jit(solution)/shard_map/ppermute | solution.py:21
  266.6 60.7 %copy-start.5 = (bf16[2,512,256]{2,1,0:T(8,128)(2,1)}, bf16[2,512,256]{2,1,0:T(8,128)(2,1)S(1)}, u32[]{:S(2)}) copy-start(bf16[2,512,256]{2,1,0:T(8,128)(2,1)S(1)} %collective-permute-done.23.refs_2_) | copy-start | bytes 1572868
  266.6 12.6 %collective-permute-start.25 = (bf16[1,512,256]{2,1,0:T(8,128)(2,1)}, bf16[1,512,256]{2,1,0:T(8,128)(2,1)S(1)}, u32[]{:S(2)}, u32[]{:S(2)}) collective-permute-start(bf16[1,512,256]{2,1,0:T(8,128)(2,1)} %get-tuple-element.72), channel_id=1, source_target_pairs={{0,2},{1,3},{2,0},{3,1},{4,6},{5,7},{6,4},{7,5},{8,10},{9,11},{10,... | collective-permute-start | bytes 786440 | tf_op jit(solution)/shard_map/ppermute | solution.py:21
  266.7 14.7 %collective-permute-start.26 = (bf16[1,512,256]{2,1,0:T(8,128)(2,1)}, bf16[1,512,256]{2,1,0:T(8,128)(2,1)S(1)}, u32[]{:S(2)}, u32[]{:S(2)}) collective-permute-start(bf16[1,512,256]{2,1,0:T(8,128)(2,1)} %get-tuple-element.73), channel_id=1, source_target_pairs={{0,4},{1,5},{2,6},{3,7},{4,0},{5,1},{6,2},{7,3},{8,12},{9,13},{10,... | collective-permute-start | bytes 786440 | tf_op jit(solution)/shard_map/ppermute | solution.py:21
  279.3 48.1 %copy-start.12 = (bf16[1,512,256]{2,1,0:T(8,128)(2,1)}, bf16[1,512,256]{2,1,0:T(8,128)(2,1)S(1)}, u32[]{:S(2)}) copy-start(bf16[1,512,256]{2,1,0:T(8,128)(2,1)S(1)} %collective-permute-done.25) | copy-start | bytes 786436
  279.3 50.7 %collective-permute-start.18 = (bf16[2,512,768]{2,1,0:T(8,128)(2,1)}, bf16[2,512,768]{2,1,0:T(8,128)(2,1)}, u32[]{:S(2)}, u32[]{:S(2)}) collective-permute-start(bf16[2,512,768]{2,1,0:T(8,128)(2,1)} %get-tuple-element.60), channel_id=1, source_target_pairs={{0,1},{1,0},{2,3},{3,2},{4,5},{5,4},{6,7},{7,6},{8,9},{9,8},{10,11... | collective-permute-start | bytes 4718600 | tf_op jit(solution)/shard_map/ppermute | solution.py:21
  281.4 48.6 %copy-start.13 = (bf16[1,512,256]{2,1,0:T(8,128)(2,1)}, bf16[1,512,256]{2,1,0:T(8,128)(2,1)S(1)}, u32[]{:S(2)}) copy-start(bf16[1,512,256]{2,1,0:T(8,128)(2,1)S(1)} %collective-permute-done.26) | copy-start | bytes 786436
  281.4 39.1 %collective-permute-start.27 = (bf16[1,512,256]{2,1,0:T(8,128)(2,1)}, bf16[1,512,256]{2,1,0:T(8,128)(2,1)S(1)}, u32[]{:S(2)}, u32[]{:S(2)}) collective-permute-start(bf16[1,512,256]{2,1,0:T(8,128)(2,1)} %get-tuple-element.75), channel_id=1, source_target_pairs={{0,1},{1,0},{2,3},{3,2},{4,5},{5,4},{6,7},{7,6},{8,9},{9,8},{10,11... | collective-permute-start | bytes 786440 | tf_op jit(solution)/shard_map/ppermute | solution.py:21
  320.4 9.5 %copy-start.14 = (bf16[1,512,256]{2,1,0:T(8,128)(2,1)}, bf16[1,512,256]{2,1,0:T(8,128)(2,1)S(1)}, u32[]{:S(2)}) copy-start(bf16[1,512,256]{2,1,0:T(8,128)(2,1)S(1)} %collective-permute-done.27) | copy-start | bytes 786436
  320.4 6.6 %collective-permute-start.28 = (bf16[1,512,256]{2,1,0:T(8,128)(2,1)}, bf16[1,512,256]{2,1,0:T(8,128)(2,1)S(1)}, u32[]{:S(2)}, u32[]{:S(2)}) collective-permute-start(bf16[1,512,256]{2,1,0:T(8,128)(2,1)} %get-tuple-element.76), channel_id=1, source_target_pairs={{0,2},{1,3},{2,0},{3,1},{4,6},{5,7},{6,4},{7,5},{8,10},{9,11},{10,... | collective-permute-start | bytes 786440 | tf_op jit(solution)/shard_map/ppermute | solution.py:21
  327.0 2.9 copy-start.15
  327.0 67.2 %collective-permute-start.19 = (bf16[2,512,768]{2,1,0:T(8,128)(2,1)}, bf16[2,512,768]{2,1,0:T(8,128)(2,1)}, u32[]{:S(2)}, u32[]{:S(2)}) collective-permute-start(bf16[2,512,768]{2,1,0:T(8,128)(2,1)} %get-tuple-element.61), channel_id=1, source_target_pairs={{0,2},{1,3},{2,0},{3,1},{4,6},{5,7},{6,4},{7,5},{8,10},{9,11},{10,... | collective-permute-start | bytes 4718600 | tf_op jit(solution)/shard_map/ppermute | solution.py:21
  327.3 11.2 %copy-start.1 = (f32[4,2,2,2,64,256]{5,4,3,2,1,0:T(8,128)}, f32[4,2,2,2,64,256]{5,4,3,2,1,0:T(8,128)S(1)}, u32[]{:S(2)}) copy-start(f32[4,2,2,2,64,256]{5,4,3,2,1,0:T(8,128)S(1)} %collective-permute-done.36.recv_ref) | copy-start | bytes 6291460
  327.3 68.7 %collective-permute-start.20 = (bf16[2,512,768]{2,1,0:T(8,128)(2,1)}, bf16[2,512,768]{2,1,0:T(8,128)(2,1)}, u32[]{:S(2)}, u32[]{:S(2)}) collective-permute-start(bf16[2,512,768]{2,1,0:T(8,128)(2,1)} %get-tuple-element.62), channel_id=1, source_target_pairs={{0,4},{1,5},{2,6},{3,7},{4,0},{5,1},{6,2},{7,3},{8,12},{9,13},{10,... | collective-permute-start | bytes 4718600 | tf_op jit(solution)/shard_map/ppermute | solution.py:21
  329.9 66.2 %collective-permute-start.15 = (bf16[2,512,768]{2,1,0:T(8,128)(2,1)}, bf16[2,512,768]{2,1,0:T(8,128)(2,1)}, u32[]{:S(2)}, u32[]{:S(2)}) collective-permute-start(bf16[2,512,768]{2,1,0:T(8,128)(2,1)} %get-tuple-element.57), channel_id=1, source_target_pairs={{0,1},{1,0},{2,3},{3,2},{4,5},{5,4},{6,7},{7,6},{8,9},{9,8},{10,11... | collective-permute-start | bytes 4718600 | tf_op jit(solution)/shard_map/ppermute | solution.py:21
  330.5 72.0 %collective-permute-start.30 = (f32[4,2,2,2,64,256]{5,4,3,2,1,0:T(8,128)}, f32[4,2,2,2,64,256]{5,4,3,2,1,0:T(8,128)}, u32[]{:S(2)}, u32[]{:S(2)}) collective-permute-start(f32[4,2,2,2,64,256]{5,4,3,2,1,0:T(8,128)} %get-tuple-element.79), channel_id=1, source_target_pairs={{0,8},{8,0},{16,24},{24,16},{1,9},{9,1},{17,25},{25,17},{2,10},{10... | collective-permute-start | bytes 6291464 | tf_op jit(solution)/shard_map/ppermute | solution.py:21
  338.5 163.9 %collective-permute-start.35 = (f32[12,1,2,2,64,256]{5,4,3,2,1,0:T(8,128)}, f32[12,1,2,2,64,256]{5,4,3,2,1,0:T(8,128)S(1)}, u32[]{:S(2)}, u32[]{:S(2)}) collective-permute-start(f32[12,1,2,2,64,256]{5,4,3,2,1,0:T(8,128)} %get-tuple-element.89), channel_id=1, source_target_pairs={{0,16},{8,24},{16,0},{24,8},{1,17},{9,25},{17,1},{25,9},{2,18},{10... | collective-permute-start | bytes 9437192 | tf_op jit(solution)/shard_map/ppermute | solution.py:21
  394.3 115.1 %collective-permute-start.33 = (f32[12,1,2,2,64,256]{5,4,3,2,1,0:T(8,128)}, f32[12,1,2,2,64,256]{5,4,3,2,1,0:T(8,128)}, u32[]{:S(2)}, u32[]{:S(2)}) collective-permute-start(f32[12,1,2,2,64,256]{5,4,3,2,1,0:T(8,128)} %get-tuple-element.85), channel_id=1, source_target_pairs={{0,16},{8,24},{16,0},{24,8},{1,17},{9,25},{17,1},{25,9},{2,18},{10... | collective-permute-start | bytes 9437192 | tf_op jit(solution)/shard_map/ppermute | solution.py:21
  396.0 67.5 %collective-permute-start.16 = (bf16[2,512,768]{2,1,0:T(8,128)(2,1)}, bf16[2,512,768]{2,1,0:T(8,128)(2,1)}, u32[]{:S(2)}, u32[]{:S(2)}) collective-permute-start(bf16[2,512,768]{2,1,0:T(8,128)(2,1)} %get-tuple-element.58), channel_id=1, source_target_pairs={{0,2},{1,3},{2,0},{3,1},{4,6},{5,7},{6,4},{7,5},{8,10},{9,11},{10,... | collective-permute-start | bytes 4718600 | tf_op jit(solution)/shard_map/ppermute | solution.py:21
  396.1 69.5 %collective-permute-start.17 = (bf16[2,512,768]{2,1,0:T(8,128)(2,1)}, bf16[2,512,768]{2,1,0:T(8,128)(2,1)}, u32[]{:S(2)}, u32[]{:S(2)}) collective-permute-start(bf16[2,512,768]{2,1,0:T(8,128)(2,1)} %get-tuple-element.59), channel_id=1, source_target_pairs={{0,4},{1,5},{2,6},{3,7},{4,0},{5,1},{6,2},{7,3},{8,12},{9,13},{10,... | collective-permute-start | bytes 4718600 | tf_op jit(solution)/shard_map/ppermute | solution.py:21
  402.5 97.2 %collective-permute-start.37 = (f32[4,1,2,2,64,256]{5,4,3,2,1,0:T(8,128)}, f32[4,1,2,2,64,256]{5,4,3,2,1,0:T(8,128)}, u32[]{:S(2)}, u32[]{:S(2)}) collective-permute-start(f32[4,1,2,2,64,256]{5,4,3,2,1,0:T(8,128)} %get-tuple-element.93), channel_id=1, source_target_pairs={{0,16},{8,24},{16,0},{24,8},{1,17},{9,25},{17,1},{25,9},{2,18},{10... | collective-permute-start | bytes 3145736 | tf_op jit(solution)/shard_map/ppermute | solution.py:21
  463.5 58.3 %collective-permute-start.31 = (f32[4,1,2,2,64,256]{5,4,3,2,1,0:T(8,128)}, f32[4,1,2,2,64,256]{5,4,3,2,1,0:T(8,128)}, u32[]{:S(2)}, u32[]{:S(2)}) collective-permute-start(f32[4,1,2,2,64,256]{5,4,3,2,1,0:T(8,128)} %get-tuple-element.81), channel_id=1, source_target_pairs={{0,16},{8,24},{16,0},{24,8},{1,17},{9,25},{17,1},{25,9},{2,18},{10... | collective-permute-start | bytes 3145736 | tf_op jit(solution)/shard_map/ppermute | solution.py:21
  465.6 14.4 %collective-permute-start.29 = (bf16[1,512,256]{2,1,0:T(8,128)(2,1)}, bf16[1,512,256]{2,1,0:T(8,128)(2,1)}, u32[]{:S(2)}, u32[]{:S(2)}) collective-permute-start(bf16[1,512,256]{2,1,0:T(8,128)(2,1)} %get-tuple-element.77), channel_id=1, source_target_pairs={{0,4},{1,5},{2,6},{3,7},{4,0},{5,1},{6,2},{7,3},{8,12},{9,13},{10,... | collective-permute-start | bytes 786440 | tf_op jit(solution)/shard_map/ppermute | solution.py:21
  502.4 1.8 copy-start

commit v5 on v4

--- a/solution.py
+++ b/solution.py
@@ -350,7 +350,10 @@
                     block = array[None, :, start * width : (start + rows) * width]
                 else:
                     block = pack_call(start, rows, width, array)
-                parts.append([partner(block, "mp", bit) for bit in range(bits)])
+                sent = []
+                for bit in range(bits):
+                    sent.append(partner(block, "mp", bit))
+                parts.append(sent)
             arrived.append([parts[kind][bit] for bit in range(bits) for kind in range(2)])
         else:
             pair = pack_call(start, rows, width, inputs, out_grad)
@@ -388,7 +391,10 @@
         totals = total_call(start, rows, 0, acc, returned[group], totals)
     ends = []
     for kind in range(2):
-        ends.append(last_total(starts[-1], sizes[-1], acc[kind], returned[-1][kind], totals[kind]))
+        if kind == 0:
+            ends += total_call(starts[-1], sizes[-1], kind, acc, returned[-1][kind], totals[:1])
+        else:
+            ends.append(last_total(starts[-1], sizes[-1], acc[kind], returned[-1][kind], totals[kind]))
     return (*ends, *grads)
 
 

time: 526 us -> 506 us (0.962)
  waiting for transfers between devices: 317 us -> 296 us
    ppermute x38, waiting for transfers between devices: 317 us -> 296 us  [partner(): return lax.ppermute(value, axis, pairs)]
    pallas_call x3 -> x4, Pallas kernels: 14.1 us -> 16.2 us  [total_call(): pl.pallas_call(functools.partial(total_body, bits, kinds), grid=(rows, 2)...]
  transfers between devices with their start and end apart: 38 -> 38, of which waited for: 22 -> 22; matrix products, arithmetic and copies ran while one was open for 1% -> 1% of each run, Pallas kernels for 28% -> 30%
where the time goes in v5:
time: 506 us; the launch traced here: 505 us
  waiting for transfers between devices  296 us (58%)
  Pallas kernels  157 us (31%)
  starting transfers between devices  42.2 us (8%)
  local copies, waits for them, and re-layouts  6.5 us (1%)
    ppermute x38, waiting for transfers between devices, partner(): return lax.ppermute(value, axis, pairs)  296 us
    pallas_call x4, Pallas kernels, main_call(): pl.pallas_call(functools.partial(main_body, dims), grid_spec=pltpu.Prefet...  91.3 us
    ppermute x38, starting transfers between devices, partner(): return lax.ppermute(value, axis, pairs)  42.2 us
    pallas_call x4, Pallas kernels, halve_call(): pl.pallas_call(halve_body, grid_spec=pltpu.PrefetchScalarGridSpec(num_sca...  23.4 us
    pallas_call x4, Pallas kernels, total_call(): pl.pallas_call(functools.partial(total_body, bits, kinds), grid=(rows, 2)...  16.2 us
    pallas_call x4, Pallas kernels, grads_call(): pl.pallas_call(grads_body, grid=(cols // block,), in_specs=[spec, spec] +...  15.6 us
    pallas_call x4, Pallas kernels, pack_call(): pl.pallas_call(pack_body, grid=(rows,), in_specs=[column] * kinds, out_sp...  10.4 us
  transfers between devices with their start and end apart: 38, of which 22 were waited for; matrix products, arithmetic and copies ran while one was open for 1% of the time, Pallas kernels for 30%

profile of v5, /device:TPU:0, one launch (start us, length us, event | category | flops | bytes accessed | tf_op | source)
XLA Modules:
  0.0 504.5 jit_solution(16528377532295460289)
XLA Ops:
  0.6 3.4 pack.6
  4.0 3.0 collective-permute-start.6
  7.0 1.6 collective-permute-start.7
  8.5 2.6 collective-permute-start.8
  11.1 1.7 pack.7
  13.3 1.0 slice_bitcast_fusion
  14.8 32.4 %collective-permute-done.10.refs_3_ = bf16[1,512,256]{2,1,0:T(8,128)(2,1)S(1)} collective-permute-done((bf16[1,512,256]{2,1,0:T(8,128)(2,1)}, bf16[1,512,256]{2,1,0:T(8,128)(2,1)S(1)}, u32[]{:S(2)}, u32[]{:S(2)}) %collective-permute-start.10) | collective-permute-done | bytes 262176 | tf_op jit(solution)/shard_map/ppermute | solution.py:21
  47.2 1.8 collective-permute-start.12
  49.0 34.7 %collective-permute-done.11.refs_4_ = bf16[1,512,256]{2,1,0:T(8,128)(2,1)S(1)} collective-permute-done((bf16[1,512,256]{2,1,0:T(8,128)(2,1)S(1)}, bf16[1,512,256]{2,1,0:T(8,128)(2,1)S(1)}, u32[]{:S(2)}, u32[]{:S(2)}) %collective-permute-start.11) | collective-permute-done | bytes 262176 | tf_op jit(solution)/shard_map/ppermute | solution.py:21
  83.8 2.6 collective-permute-start.13
  86.4 6.3 %collective-permute-done.12.refs_5_ = bf16[1,512,256]{2,1,0:T(8,128)(2,1)S(1)} collective-permute-done((bf16[1,512,256]{2,1,0:T(8,128)(2,1)}, bf16[1,512,256]{2,1,0:T(8,128)(2,1)S(1)}, u32[]{:S(2)}, u32[]{:S(2)}) %collective-permute-start.12) | collective-permute-done | bytes 262176 | tf_op jit(solution)/shard_map/ppermute | solution.py:21
  92.8 10.4 %collective-permute-done.13.refs_6_ = bf16[1,512,256]{2,1,0:T(8,128)(2,1)S(1)} collective-permute-done((bf16[1,512,256]{2,1,0:T(8,128)(2,1)S(1)}, bf16[1,512,256]{2,1,0:T(8,128)(2,1)S(1)}, u32[]{:S(2)}, u32[]{:S(2)}) %collective-permute-start.13) | collective-permute-done | bytes 262176 | tf_op jit(solution)/shard_map/ppermute | solution.py:21
  103.2 3.5 pack.5
  106.7 1.2 collective-permute-done.14.refs_7_
  107.9 0.8 collective-permute-start.3
  108.7 0.9 collective-permute-done.9.refs_2_
  109.5 4.0 collective-permute-start.4
  113.6 3.5 collective-permute-start.5
  119.2 14.5 %columns.4 = (f32[2,8,512,256]{3,2,1,0:T(8,128)}, bf16[2,512,256]{2,1,0:T(8,128)(2,1)}, bf16[2,512,256]{2,1,0:T(8,128)(2,1)}, bf16[2,512,256]{2,1,0:T(8,128)(2,1...) custom-call(s32[8]{0:T(128)} %reshape.38.slots_ref, s32[1]{0:T(128)} %bitcast.parity_ref, ...), custom_call_target="tpu_custom_call" | custom-call | flops 3221225472 | bytes 23592960 | tf_op jit(solution)/shard_map/columns/pallas_call | solution.py:191
  133.8 29.8 %columns.5 = (f32[2,8,512,256]{3,2,1,0:T(8,128)}, bf16[2,512,768]{2,1,0:T(8,128)(2,1)}, bf16[2,512,768]{2,1,0:T(8,128)(2,1)}, bf16[2,512,768]{2,1,0:T(8,128)(2,1...) custom-call(s32[24]{0:T(128)} %reshape.37.slots_ref, s32[1]{0:T(128)} %bitcast.parity_ref, ...), custom_call_target="tpu_custom_call" | custom-call | flops 9663676416 | bytes 45613056 | tf_op jit(solution)/shard_map/columns/pallas_call | solution.py:191
  163.7 12.9 %collective-permute-done.4.refs_3_ = bf16[2,512,768]{2,1,0:T(8,128)(2,1)} collective-permute-done((bf16[2,512,768]{2,1,0:T(8,128)(2,1)}, bf16[2,512,768]{2,1,0:T(8,128)(2,1)}, u32[]{:S(2)}, u32[]{:S(2)}) %collective-permute-start.4) | collective-permute-done | bytes 1572896 | tf_op jit(solution)/shard_map/ppermute | solution.py:21
  176.6 2.1 collective-permute-done.5.refs_4_
  178.7 29.8 %columns.6 = (f32[2,8,512,256]{3,2,1,0:T(8,128)}, bf16[2,512,768]{2,1,0:T(8,128)(2,1)}, bf16[2,512,768]{2,1,0:T(8,128)(2,1)}, bf16[2,512,768]{2,1,0:T(8,128)(2,1...) custom-call(s32[24]{0:T(128)} %reshape.36.slots_ref, s32[1]{0:T(128)} %bitcast.parity_ref, ...), custom_call_target="tpu_custom_call" | custom-call | flops 9663676416 | bytes 45613056 | tf_op jit(solution)/shard_map/columns/pallas_call | solution.py:191
  208.6 1.9 pack.4
  210.5 1.5 collective-permute-start
  212.0 2.1 collective-permute-start.2
  214.1 10.9 %collective-permute-done.refs_2_ = bf16[2,512,256]{2,1,0:T(8,128)(2,1)S(1)} collective-permute-done((bf16[2,512,256]{2,1,0:T(8,128)(2,1)}, bf16[2,512,256]{2,1,0:T(8,128)(2,1)S(1)}, u32[]{:S(2)}, u32[]{:S(2)}) %collective-permute-start) | collective-permute-done | bytes 524320 | tf_op jit(solution)/shard_map/ppermute | solution.py:21
  225.0 1.5 collective-permute-start.24
  226.5 10.0 %collective-permute-done.1.refs_3_ = bf16[2,512,256]{2,1,0:T(8,128)(2,1)S(1)} collective-permute-done((bf16[2,512,256]{2,1,0:T(8,128)(2,1)}, bf16[2,512,256]{2,1,0:T(8,128)(2,1)S(1)}, u32[]{:S(2)}, u32[]{:S(2)}) %collective-permute-start.1) | collective-permute-done | bytes 524320 | tf_op jit(solution)/shard_map/ppermute | solution.py:21
  236.5 1.9 collective-permute-done.2.refs_4_
  238.4 0.8 copy-done.4
  239.9 0.9 collective-permute-start.26
  240.8 17.1 %columns.7 = (f32[2,8,512,256]{3,2,1,0:T(8,128)}, bf16[1,512,256]{2,1,0:T(8,128)(2,1)}, bf16[1,512,256]{2,1,0:T(8,128)(2,1)}, bf16[1,512,256]{2,1,0:T(8,128)(2,1...) custom-call(s32[8]{0:T(128)} %reshape.34.slots_ref, ...), custom_call_target="tpu_custom_call" | custom-call | flops 3221225472 | bytes 23592960 | tf_op jit(solution)/shard_map/columns/pallas_call | solution.py:191
  258.5 8.1 %collective-permute-done.26.refs_2_ = bf16[2,512,256]{2,1,0:T(8,128)(2,1)S(1)} collective-permute-done((bf16[2,512,256]{2,1,0:T(8,128)(2,1)}, bf16[2,512,256]{2,1,0:T(8,128)(2,1)S(1)}, u32[]{:S(2)}, u32[]{:S(2)}) %collective-permute-start.26) | collective-permute-done | bytes 524320 | tf_op jit(solution)/shard_map/ppermute | solution.py:21
  267.2 7.5 %collective-permute-done.28 = bf16[1,512,256]{2,1,0:T(8,128)(2,1)S(1)} collective-permute-done((bf16[1,512,256]{2,1,0:T(8,128)(2,1)}, bf16[1,512,256]{2,1,0:T(8,128)(2,1)S(1)}, u32[]{:S(2)}, u32[]{:S(2)}) %collective-permute-start.28) | collective-permute-done | bytes 262176 | tf_op jit(solution)/shard_map/ppermute | solution.py:21
  275.4 1.1 collective-permute-start.16
  276.5 6.2 %collective-permute-done.16.refs_1_ = bf16[1,512,256]{2,1,0:T(8,128)(2,1)S(1)} collective-permute-done((bf16[1,512,256]{2,1,0:T(8,128)(2,1)}, bf16[1,512,256]{2,1,0:T(8,128)(2,1)S(1)}, u32[]{:S(2)}, u32[]{:S(2)}) %collective-permute-start.16) | collective-permute-done | bytes 262176 | tf_op jit(solution)/shard_map/ppermute | solution.py:21
  282.6 0.9 collective-permute-start.17
  283.5 12.0 %collective-permute-done.17.refs_2_ = bf16[1,512,256]{2,1,0:T(8,128)(2,1)S(1)} collective-permute-done((bf16[1,512,256]{2,1,0:T(8,128)(2,1)}, bf16[1,512,256]{2,1,0:T(8,128)(2,1)S(1)}, u32[]{:S(2)}, u32[]{:S(2)}) %collective-permute-start.17) | collective-permute-done | bytes 262176 | tf_op jit(solution)/shard_map/ppermute | solution.py:21
  295.6 2.2 collective-permute-start.23
  297.8 12.4 %collective-permute-done.21.refs_0_ = bf16[2,512,768]{2,1,0:T(8,128)(2,1)} collective-permute-done((bf16[2,512,768]{2,1,0:T(8,128)(2,1)}, bf16[2,512,768]{2,1,0:T(8,128)(2,1)}, u32[]{:S(2)}, u32[]{:S(2)}) %collective-permute-start.21) | collective-permute-done | bytes 1572896 | tf_op jit(solution)/shard_map/ppermute | solution.py:21
  310.6 8.0 %halve.6 = (f32[12,1,2,2,64,256]{5,4,3,2,1,0:T(8,128)}, f32[12,1,2,2,64,256]{5,4,3,2,1,0:T(8,128)}) custom-call(s32[1]{0:T(128)} %bitcast.6.parity_ref, f32[12,2,2,2,64,256]{5,4,3,2,1,0:T(8,128)} %get-tuple-element.86.keep_ref, f32[12,2,2,2,64,256]{5,4,3,2,1,0:T(8,128)} %collective-permute-done.34.recv_ref), custom_call_target="tpu_custom_call" | custom-call | flops 1572864 | bytes 18874368 | tf_op jit(solution)/shard_map/halve/pallas_call | solution.py:241
  318.7 1.6 collective-permute-start.35
  320.3 7.9 %halve.5 = (f32[12,1,2,2,64,256]{5,4,3,2,1,0:T(8,128)}, f32[12,1,2,2,64,256]{5,4,3,2,1,0:T(8,128)}) custom-call(s32[1]{0:T(128)} %bitcast.6.parity_ref, f32[12,2,2,2,64,256]{5,4,3,2,1,0:T(8,128)} %get-tuple-element.82.keep_ref, f32[12,2,2,2,64,256]{5,4,3,2,1,0:T(8,128)} %collective-permute-done.32.recv_ref), custom_call_target="tpu_custom_call" | custom-call | flops 1572864 | bytes 18874368 | tf_op jit(solution)/shard_map/halve/pallas_call | solution.py:241
  328.2 36.5 %collective-permute-done.22.refs_1_ = bf16[2,512,768]{2,1,0:T(8,128)(2,1)} collective-permute-done((bf16[2,512,768]{2,1,0:T(8,128)(2,1)}, bf16[2,512,768]{2,1,0:T(8,128)(2,1)}, u32[]{:S(2)}, u32[]{:S(2)}) %collective-permute-start.22) | collective-permute-done | bytes 1572896 | tf_op jit(solution)/shard_map/ppermute | solution.py:21
  364.7 1.5 collective-permute-start.33
  366.8 2.2 collective-permute-start.20
  369.0 3.7 halve.7
  372.7 1.5 collective-permute-start.37
  374.2 3.8 halve.4
  378.0 57.2 %collective-permute-done.19.refs_1_ = bf16[2,512,768]{2,1,0:T(8,128)(2,1)} collective-permute-done((bf16[2,512,768]{2,1,0:T(8,128)(2,1)}, bf16[2,512,768]{2,1,0:T(8,128)(2,1)}, u32[]{:S(2)}, u32[]{:S(2)}) %collective-permute-start.19) | collective-permute-done | bytes 1572896 | tf_op jit(solution)/shard_map/ppermute | solution.py:21
  435.3 1.5 collective-permute-start.31
  437.5 2.4 totals.4
  440.0 5.8 %totals.5 = (bf16[512,2048]{1,0:T(8,128)(2,1)}, bf16[512,2048]{1,0:T(8,128)(2,1)}) custom-call(f32[2,8,512,256]{3,2,1,0:T(8,128)} %get-tuple-element.56.acc_ref, bf16[2,512,768]{2,1,0:T(8,128)(2,1)} %collective-permute-done.21.refs_0_, bf16[2,512,768]{2,1,0:T(8,128)(2,1)} %collective-permute-done.22.refs_1_, ...), custom_call_target="tpu_custom_call", output_to_operand_aliasing={{0}: (4, {}), {1}: (5, {})} | custom-call | flops 2359296 | bytes 9437184 | tf_op jit(solution)/shard_map/totals/pallas_call | solution.py:300
  445.8 5.8 %totals.6 = (bf16[512,2048]{1,0:T(8,128)(2,1)}, bf16[512,2048]{1,0:T(8,128)(2,1)}) custom-call(f32[2,8,512,256]{3,2,1,0:T(8,128)} %get-tuple-element.56.acc_ref, bf16[2,512,768]{2,1,0:T(8,128)(2,1)} %collective-permute-done.18.refs_0_, bf16[2,512,768]{2,1,0:T(8,128)(2,1)} %collective-permute-done.19.refs_1_, ...), custom_call_target="tpu_custom_call", output_to_operand_aliasing={{0}: (4, {}), {1}: (5, {})} | custom-call | flops 2359296 | bytes 9437184 | tf_op jit(solution)/shard_map/totals/pallas_call | solution.py:300
  451.7 2.0 totals.7
  453.7 2.0 fusion.1
  455.7 24.2 %collective-permute-done.37.recv_ref = f32[4,1,2,2,64,256]{5,4,3,2,1,0:T(8,128)} collective-permute-done((f32[4,1,2,2,64,256]{5,4,3,2,1,0:T(8,128)}, f32[4,1,2,2,64,256]{5,4,3,2,1,0:T(8,128)}, u32[]{:S(2)}, u32[]{:S(2)}) %collective-permute-start.37) | collective-permute-done | bytes 1048608 | tf_op jit(solution)/shard_map/ppermute | solution.py:21
  479.9 2.6 grads.4
  482.5 1.8 copy-done
  484.3 5.2 %grads.5 = (f32[2,32,64,256]{3,2,1,0:T(8,128)}, f32[2,32,64,256]{3,2,1,0:T(8,128)}) custom-call(f32[12,1,2,2,64,256]{5,4,3,2,1,0:T(8,128)} %get-tuple-element.88.keep_ref, f32[12,1,2,2,64,256]{5,4,3,2,1,0:T(8,128)} %copy-done, f32[2,32,64,256]{3,2,1,0:T(8,128)} %get-tuple-element.94.refs_0_, ...), custom_call_target="tpu_custom_call", output_to_operand_aliasing={{0}: (2, {}), {1}: (3, {})} | custom-call | flops 786432 | bytes 9437184 | tf_op jit(solution)/shard_map/grads/pallas_call | solution.py:269
  489.5 5.2 %grads.6 = (f32[2,32,64,256]{3,2,1,0:T(8,128)}, f32[2,32,64,256]{3,2,1,0:T(8,128)}) custom-call(f32[12,1,2,2,64,256]{5,4,3,2,1,0:T(8,128)} %get-tuple-element.84.keep_ref, f32[12,1,2,2,64,256]{5,4,3,2,1,0:T(8,128)} %collective-permute-done.33.recv_ref, f32[2,32,64,256]{3,2,1,0:T(8,128)} %get-tuple-element.96.refs_0_, ...), custom_call_target="tpu_custom_call", output_to_operand_aliasing={{0}: (2, {}), {1}: (3, {})} | custom-call | flops 786432 | bytes 9437184 | tf_op jit(solution)/shard_map/grads/pallas_call | solution.py:269
  494.6 7.3 %collective-permute-done.31.recv_ref = f32[4,1,2,2,64,256]{5,4,3,2,1,0:T(8,128)} collective-permute-done((f32[4,1,2,2,64,256]{5,4,3,2,1,0:T(8,128)}, f32[4,1,2,2,64,256]{5,4,3,2,1,0:T(8,128)}, u32[]{:S(2)}, u32[]{:S(2)}) %collective-permute-start.31) | collective-permute-done | bytes 1048608 | tf_op jit(solution)/shard_map/ppermute | solution.py:21
  501.9 2.6 grads.7
  (79 shorter events, 8.0 us)
Async XLA Ops:
  4.0 109.6 %collective-permute-start.6 = (bf16[2,512,768]{2,1,0:T(8,128)(2,1)}, bf16[2,512,768]{2,1,0:T(8,128)(2,1)S(1)}, u32[]{:S(2)}, u32[]{:S(2)}) collective-permute-start(bf16[2,512,768]{2,1,0:T(8,128)(2,1)} %pack.6), channel_id=1, source_target_pairs={{0,1},{1,0},{2,3},{3,2},{4,5},{5,4},{6,7},{7,6},{8,9},{9,8},{10,11... | collective-permute-start | bytes 4718600 | tf_op jit(solution)/shard_map/ppermute | solution.py:21
  7.0 126.8 %collective-permute-start.7 = (bf16[2,512,768]{2,1,0:T(8,128)(2,1)}, bf16[2,512,768]{2,1,0:T(8,128)(2,1)}, u32[]{:S(2)}, u32[]{:S(2)}) collective-permute-start(bf16[2,512,768]{2,1,0:T(8,128)(2,1)} %pack.6), channel_id=1, source_target_pairs={{0,2},{1,3},{2,0},{3,1},{4,6},{5,7},{6,4},{7,5},{8,10},{9,11},{10,... | collective-permute-start | bytes 4718600 | tf_op jit(solution)/shard_map/ppermute | solution.py:21
  8.5 125.2 %collective-permute-start.8 = (bf16[2,512,768]{2,1,0:T(8,128)(2,1)}, bf16[2,512,768]{2,1,0:T(8,128)(2,1)}, u32[]{:S(2)}, u32[]{:S(2)}) collective-permute-start(bf16[2,512,768]{2,1,0:T(8,128)(2,1)} %pack.6), channel_id=1, source_target_pairs={{0,4},{1,5},{2,6},{3,7},{4,0},{5,1},{6,2},{7,3},{8,12},{9,13},{10,... | collective-permute-start | bytes 4718600 | tf_op jit(solution)/shard_map/ppermute | solution.py:21
  12.8 34.4 %collective-permute-start.10 = (bf16[1,512,256]{2,1,0:T(8,128)(2,1)}, bf16[1,512,256]{2,1,0:T(8,128)(2,1)S(1)}, u32[]{:S(2)}, u32[]{:S(2)}) collective-permute-start(bf16[1,512,256]{2,1,0:T(8,128)(2,1)} %pack.7), channel_id=1, source_target_pairs={{0,1},{1,0},{2,3},{3,2},{4,5},{5,4},{6,7},{7,6},{8,9},{9,8},{10,11... | collective-permute-start | bytes 786440 | tf_op jit(solution)/shard_map/ppermute | solution.py:21
  14.3 69.5 %collective-permute-start.11 = (bf16[1,512,256]{2,1,0:T(8,128)(2,1)S(1)}, bf16[1,512,256]{2,1,0:T(8,128)(2,1)S(1)}, u32[]{:S(2)}, u32[]{:S(2)}) collective-permute-start(bf16[1,512,256]{2,1,0:T(8,128)(2,1)S(1)} %slice_bitcast_fusion), channel_id=1, source_target_pairs={{0,2},{1,3},{2,0},{3,1},{4,6},{5,7},{6,4},{7,5},{8,10},{9,11},{10,... | collective-permute-start | bytes 786440 | tf_op jit(solution)/shard_map/ppermute | solution.py:21
  47.2 59.5 %copy-start.6 = (bf16[1,512,256]{2,1,0:T(8,128)(2,1)}, bf16[1,512,256]{2,1,0:T(8,128)(2,1)S(1)}, u32[]{:S(2)}) copy-start(bf16[1,512,256]{2,1,0:T(8,128)(2,1)S(1)} %collective-permute-done.10.refs_3_) | copy-start | bytes 786436
  47.2 45.5 %collective-permute-start.12 = (bf16[1,512,256]{2,1,0:T(8,128)(2,1)}, bf16[1,512,256]{2,1,0:T(8,128)(2,1)S(1)}, u32[]{:S(2)}, u32[]{:S(2)}) collective-permute-start(bf16[1,512,256]{2,1,0:T(8,128)(2,1)} %pack.7), channel_id=1, source_target_pairs={{0,2},{1,3},{2,0},{3,1},{4,6},{5,7},{6,4},{7,5},{8,10},{9,11},{10,... | collective-permute-start | bytes 786440 | tf_op jit(solution)/shard_map/ppermute | solution.py:21
  83.8 22.9 %copy-start.7 = (bf16[1,512,256]{2,1,0:T(8,128)(2,1)}, bf16[1,512,256]{2,1,0:T(8,128)(2,1)S(1)}, u32[]{:S(2)}) copy-start(bf16[1,512,256]{2,1,0:T(8,128)(2,1)S(1)} %collective-permute-done.11.refs_4_) | copy-start | bytes 786436
  83.8 19.4 %collective-permute-start.13 = (bf16[1,512,256]{2,1,0:T(8,128)(2,1)S(1)}, bf16[1,512,256]{2,1,0:T(8,128)(2,1)S(1)}, u32[]{:S(2)}, u32[]{:S(2)}) collective-permute-start(bf16[1,512,256]{2,1,0:T(8,128)(2,1)S(1)} %slice_bitcast_fusion), channel_id=1, source_target_pairs={{0,4},{1,5},{2,6},{3,7},{4,0},{5,1},{6,2},{7,3},{8,12},{9,13},{10,... | collective-permute-start | bytes 786440 | tf_op jit(solution)/shard_map/ppermute | solution.py:21
  92.7 13.9 %copy-start.8 = (bf16[1,512,256]{2,1,0:T(8,128)(2,1)}, bf16[1,512,256]{2,1,0:T(8,128)(2,1)S(1)}, u32[]{:S(2)}) copy-start(bf16[1,512,256]{2,1,0:T(8,128)(2,1)S(1)} %collective-permute-done.12.refs_5_) | copy-start | bytes 786436
  92.7 15.2 %collective-permute-start.14 = (bf16[1,512,256]{2,1,0:T(8,128)(2,1)}, bf16[1,512,256]{2,1,0:T(8,128)(2,1)S(1)}, u32[]{:S(2)}, u32[]{:S(2)}) collective-permute-start(bf16[1,512,256]{2,1,0:T(8,128)(2,1)} %pack.7), channel_id=1, source_target_pairs={{0,4},{1,5},{2,6},{3,7},{4,0},{5,1},{6,2},{7,3},{8,12},{9,13},{10,... | collective-permute-start | bytes 786440 | tf_op jit(solution)/shard_map/ppermute | solution.py:21
  103.2 3.5 copy-start.9
  103.2 6.4 %collective-permute-start.9 = (bf16[1,512,256]{2,1,0:T(8,128)(2,1)S(1)}, bf16[1,512,256]{2,1,0:T(8,128)(2,1)S(1)}, u32[]{:S(2)}, u32[]{:S(2)}) collective-permute-start(bf16[1,512,256]{2,1,0:T(8,128)(2,1)S(1)} %slice_bitcast_fusion), channel_id=1, source_target_pairs={{0,1},{1,0},{2,3},{3,2},{4,5},{5,4},{6,7},{7,6},{8,9},{9,8},{10,11... | collective-permute-start | bytes 786440 | tf_op jit(solution)/shard_map/ppermute | solution.py:21
  103.2 13.9 %copy-start.16 = (s32[2,32]{1,0:T(2,128)S(1)}, s32[2,32]{1,0:T(2,128)}, u32[]{:S(2)}) copy-start(s32[2,32]{1,0:T(2,128)} %param.9) | copy-start | bytes 772
  107.9 11.3 %copy-start.10 = (bf16[1,512,256]{2,1,0:T(8,128)(2,1)}, bf16[1,512,256]{2,1,0:T(8,128)(2,1)S(1)}, u32[]{:S(2)}) copy-start(bf16[1,512,256]{2,1,0:T(8,128)(2,1)S(1)} %collective-permute-done.14.refs_7_) | copy-start | bytes 786436
  107.9 55.8 %collective-permute-start.3 = (bf16[2,512,768]{2,1,0:T(8,128)(2,1)}, bf16[2,512,768]{2,1,0:T(8,128)(2,1)}, u32[]{:S(2)}, u32[]{:S(2)}) collective-permute-start(bf16[2,512,768]{2,1,0:T(8,128)(2,1)} %pack.5), channel_id=1, source_target_pairs={{0,1},{1,0},{2,3},{3,2},{4,5},{5,4},{6,7},{7,6},{8,9},{9,8},{10,11... | collective-permute-start | bytes 4718600 | tf_op jit(solution)/shard_map/ppermute | solution.py:21
  109.5 9.6 %copy-start.11 = (bf16[1,512,256]{2,1,0:T(8,128)(2,1)}, bf16[1,512,256]{2,1,0:T(8,128)(2,1)S(1)}, u32[]{:S(2)}) copy-start(bf16[1,512,256]{2,1,0:T(8,128)(2,1)S(1)} %collective-permute-done.9.refs_2_) | copy-start | bytes 786436
  109.5 67.1 %collective-permute-start.4 = (bf16[2,512,768]{2,1,0:T(8,128)(2,1)}, bf16[2,512,768]{2,1,0:T(8,128)(2,1)}, u32[]{:S(2)}, u32[]{:S(2)}) collective-permute-start(bf16[2,512,768]{2,1,0:T(8,128)(2,1)} %pack.5), channel_id=1, source_target_pairs={{0,2},{1,3},{2,0},{3,1},{4,6},{5,7},{6,4},{7,5},{8,10},{9,11},{10,... | collective-permute-start | bytes 4718600 | tf_op jit(solution)/shard_map/ppermute | solution.py:21
  113.6 4.1 copy-start.17
  113.6 65.1 %collective-permute-start.5 = (bf16[2,512,768]{2,1,0:T(8,128)(2,1)}, bf16[2,512,768]{2,1,0:T(8,128)(2,1)}, u32[]{:S(2)}, u32[]{:S(2)}) collective-permute-start(bf16[2,512,768]{2,1,0:T(8,128)(2,1)} %pack.5), channel_id=1, source_target_pairs={{0,4},{1,5},{2,6},{3,7},{4,0},{5,1},{6,2},{7,3},{8,12},{9,13},{10,... | collective-permute-start | bytes 4718600 | tf_op jit(solution)/shard_map/ppermute | solution.py:21
  163.6 147.0 %collective-permute-start.34 = (f32[12,2,2,2,64,256]{5,4,3,2,1,0:T(8,128)}, f32[12,2,2,2,64,256]{5,4,3,2,1,0:T(8,128)}, u32[]{:S(2)}, u32[]{:S(2)}) collective-permute-start(f32[12,2,2,2,64,256]{5,4,3,2,1,0:T(8,128)} %get-tuple-element.87), channel_id=1, source_target_pairs={{0,8},{8,0},{16,24},{24,16},{1,9},{9,1},{17,25},{25,17},{2,10},{10... | collective-permute-start | bytes 18874376 | tf_op jit(solution)/shard_map/ppermute | solution.py:21
  208.5 110.1 %collective-permute-start.32 = (f32[12,2,2,2,64,256]{5,4,3,2,1,0:T(8,128)}, f32[12,2,2,2,64,256]{5,4,3,2,1,0:T(8,128)}, u32[]{:S(2)}, u32[]{:S(2)}) collective-permute-start(f32[12,2,2,2,64,256]{5,4,3,2,1,0:T(8,128)} %get-tuple-element.83), channel_id=1, source_target_pairs={{0,8},{8,0},{16,24},{24,16},{1,9},{9,1},{17,25},{25,17},{2,10},{10... | collective-permute-start | bytes 18874376 | tf_op jit(solution)/shard_map/ppermute | solution.py:21
  210.5 14.5 %collective-permute-start = (bf16[2,512,256]{2,1,0:T(8,128)(2,1)}, bf16[2,512,256]{2,1,0:T(8,128)(2,1)S(1)}, u32[]{:S(2)}, u32[]{:S(2)}) collective-permute-start(bf16[2,512,256]{2,1,0:T(8,128)(2,1)} %pack.4), channel_id=1, source_target_pairs={{0,1},{1,0},{2,3},{3,2},{4,5},{5,4},{6,7},{7,6},{8,9},{9,8},{10,11... | collective-permute-start | bytes 1572872 | tf_op jit(solution)/shard_map/ppermute | solution.py:21
  212.0 24.5 %collective-permute-start.1 = (bf16[2,512,256]{2,1,0:T(8,128)(2,1)}, bf16[2,512,256]{2,1,0:T(8,128)(2,1)S(1)}, u32[]{:S(2)}, u32[]{:S(2)}) collective-permute-start(bf16[2,512,256]{2,1,0:T(8,128)(2,1)} %pack.4), channel_id=1, source_target_pairs={{0,2},{1,3},{2,0},{3,1},{4,6},{5,7},{6,4},{7,5},{8,10},{9,11},{10,... | collective-permute-start | bytes 1572872 | tf_op jit(solution)/shard_map/ppermute | solution.py:21
  212.0 26.4 %collective-permute-start.2 = (bf16[2,512,256]{2,1,0:T(8,128)(2,1)}, bf16[2,512,256]{2,1,0:T(8,128)(2,1)S(1)}, u32[]{:S(2)}, u32[]{:S(2)}) collective-permute-start(bf16[2,512,256]{2,1,0:T(8,128)(2,1)} %pack.4), channel_id=1, source_target_pairs={{0,4},{1,5},{2,6},{3,7},{4,0},{5,1},{6,2},{7,3},{8,12},{9,13},{10,... | collective-permute-start | bytes 1572872 | tf_op jit(solution)/shard_map/ppermute | solution.py:21
  225.0 15.8 %copy-start.2 = (bf16[2,512,256]{2,1,0:T(8,128)(2,1)}, bf16[2,512,256]{2,1,0:T(8,128)(2,1)S(1)}, u32[]{:S(2)}) copy-start(bf16[2,512,256]{2,1,0:T(8,128)(2,1)S(1)} %collective-permute-done.refs_2_) | copy-start | bytes 1572868
  225.0 14.9 %collective-permute-start.24 = (bf16[2,512,256]{2,1,0:T(8,128)(2,1)}, bf16[2,512,256]{2,1,0:T(8,128)(2,1)}, u32[]{:S(2)}, u32[]{:S(2)}) collective-permute-start(bf16[2,512,256]{2,1,0:T(8,128)(2,1)} %get-tuple-element.66), channel_id=1, source_target_pairs={{0,1},{1,0},{2,3},{3,2},{4,5},{5,4},{6,7},{7,6},{8,9},{9,8},{10,11... | collective-permute-start | bytes 1572872 | tf_op jit(solution)/shard_map/ppermute | solution.py:21
  236.5 4.3 copy-start.3
  236.5 21.4 %collective-permute-start.25 = (bf16[2,512,256]{2,1,0:T(8,128)(2,1)}, bf16[2,512,256]{2,1,0:T(8,128)(2,1)}, u32[]{:S(2)}, u32[]{:S(2)}) collective-permute-start(bf16[2,512,256]{2,1,0:T(8,128)(2,1)} %get-tuple-element.67), channel_id=1, source_target_pairs={{0,2},{1,3},{2,0},{3,1},{4,6},{5,7},{6,4},{7,5},{8,10},{9,11},{10,... | collective-permute-start | bytes 1572872 | tf_op jit(solution)/shard_map/ppermute | solution.py:21
  238.4 0.8 copy-start.4
  239.2 56.3 %collective-permute-start.36 = (f32[4,2,2,2,64,256]{5,4,3,2,1,0:T(8,128)}, f32[4,2,2,2,64,256]{5,4,3,2,1,0:T(8,128)S(1)}, u32[]{:S(2)}, u32[]{:S(2)}) collective-permute-start(f32[4,2,2,2,64,256]{5,4,3,2,1,0:T(8,128)} %get-tuple-element.91), channel_id=1, source_target_pairs={{0,8},{8,0},{16,24},{24,16},{1,9},{9,1},{17,25},{25,17},{2,10},{10... | collective-permute-start | bytes 6291464 | tf_op jit(solution)/shard_map/ppermute | solution.py:21
  239.9 26.7 %collective-permute-start.26 = (bf16[2,512,256]{2,1,0:T(8,128)(2,1)}, bf16[2,512,256]{2,1,0:T(8,128)(2,1)S(1)}, u32[]{:S(2)}, u32[]{:S(2)}) collective-permute-start(bf16[2,512,256]{2,1,0:T(8,128)(2,1)} %get-tuple-element.68), channel_id=1, source_target_pairs={{0,4},{1,5},{2,6},{3,7},{4,0},{5,1},{6,2},{7,3},{8,12},{9,13},{10,... | collective-permute-start | bytes 1572872 | tf_op jit(solution)/shard_map/ppermute | solution.py:21
  257.9 8.7 %collective-permute-start.27 = (bf16[1,512,256]{2,1,0:T(8,128)(2,1)}, bf16[1,512,256]{2,1,0:T(8,128)(2,1)S(1)}, u32[]{:S(2)}, u32[]{:S(2)}) collective-permute-start(bf16[1,512,256]{2,1,0:T(8,128)(2,1)} %get-tuple-element.75), channel_id=1, source_target_pairs={{0,1},{1,0},{2,3},{3,2},{4,5},{5,4},{6,7},{7,6},{8,9},{9,8},{10,11... | collective-permute-start | bytes 786440 | tf_op jit(solution)/shard_map/ppermute | solution.py:21
  266.6 28.9 %copy-start.5 = (bf16[2,512,256]{2,1,0:T(8,128)(2,1)}, bf16[2,512,256]{2,1,0:T(8,128)(2,1)S(1)}, u32[]{:S(2)}) copy-start(bf16[2,512,256]{2,1,0:T(8,128)(2,1)S(1)} %collective-permute-done.26.refs_2_) | copy-start | bytes 1572868
  266.6 8.1 %collective-permute-start.28 = (bf16[1,512,256]{2,1,0:T(8,128)(2,1)}, bf16[1,512,256]{2,1,0:T(8,128)(2,1)S(1)}, u32[]{:S(2)}, u32[]{:S(2)}) collective-permute-start(bf16[1,512,256]{2,1,0:T(8,128)(2,1)} %get-tuple-element.76), channel_id=1, source_target_pairs={{0,2},{1,3},{2,0},{3,1},{4,6},{5,7},{6,4},{7,5},{8,10},{9,11},{10,... | collective-permute-start | bytes 786440 | tf_op jit(solution)/shard_map/ppermute | solution.py:21
  266.6 8.6 %collective-permute-start.15 = (bf16[1,512,256]{2,1,0:T(8,128)(2,1)}, bf16[1,512,256]{2,1,0:T(8,128)(2,1)S(1)}, u32[]{:S(2)}, u32[]{:S(2)}) collective-permute-start(bf16[1,512,256]{2,1,0:T(8,128)(2,1)} %get-tuple-element.57), channel_id=1, source_target_pairs={{0,1},{1,0},{2,3},{3,2},{4,5},{5,4},{6,7},{7,6},{8,9},{9,8},{10,11... | collective-permute-start | bytes 786440 | tf_op jit(solution)/shard_map/ppermute | solution.py:21
  274.7 0.7 copy-start.15
  274.7 35.4 %collective-permute-start.21 = (bf16[2,512,768]{2,1,0:T(8,128)(2,1)}, bf16[2,512,768]{2,1,0:T(8,128)(2,1)}, u32[]{:S(2)}, u32[]{:S(2)}) collective-permute-start(bf16[2,512,768]{2,1,0:T(8,128)(2,1)} %get-tuple-element.63), channel_id=1, source_target_pairs={{0,1},{1,0},{2,3},{3,2},{4,5},{5,4},{6,7},{7,6},{8,9},{9,8},{10,11... | collective-permute-start | bytes 4718600 | tf_op jit(solution)/shard_map/ppermute | solution.py:21
  275.4 43.2 %copy-start.12 = (bf16[1,512,256]{2,1,0:T(8,128)(2,1)}, bf16[1,512,256]{2,1,0:T(8,128)(2,1)S(1)}, u32[]{:S(2)}) copy-start(bf16[1,512,256]{2,1,0:T(8,128)(2,1)S(1)} %collective-permute-done.15.refs_0_) | copy-start | bytes 786436
  275.4 7.2 %collective-permute-start.16 = (bf16[1,512,256]{2,1,0:T(8,128)(2,1)}, bf16[1,512,256]{2,1,0:T(8,128)(2,1)S(1)}, u32[]{:S(2)}, u32[]{:S(2)}) collective-permute-start(bf16[1,512,256]{2,1,0:T(8,128)(2,1)} %get-tuple-element.58), channel_id=1, source_target_pairs={{0,2},{1,3},{2,0},{3,1},{4,6},{5,7},{6,4},{7,5},{8,10},{9,11},{10,... | collective-permute-start | bytes 786440 | tf_op jit(solution)/shard_map/ppermute | solution.py:21
  282.6 36.0 %copy-start.13 = (bf16[1,512,256]{2,1,0:T(8,128)(2,1)}, bf16[1,512,256]{2,1,0:T(8,128)(2,1)S(1)}, u32[]{:S(2)}) copy-start(bf16[1,512,256]{2,1,0:T(8,128)(2,1)S(1)} %collective-permute-done.16.refs_1_) | copy-start | bytes 786436
  282.6 12.9 %collective-permute-start.17 = (bf16[1,512,256]{2,1,0:T(8,128)(2,1)}, bf16[1,512,256]{2,1,0:T(8,128)(2,1)S(1)}, u32[]{:S(2)}, u32[]{:S(2)}) collective-permute-start(bf16[1,512,256]{2,1,0:T(8,128)(2,1)} %get-tuple-element.59), channel_id=1, source_target_pairs={{0,4},{1,5},{2,6},{3,7},{4,0},{5,1},{6,2},{7,3},{8,12},{9,13},{10,... | collective-permute-start | bytes 786440 | tf_op jit(solution)/shard_map/ppermute | solution.py:21
  295.5 23.1 %copy-start.14 = (bf16[1,512,256]{2,1,0:T(8,128)(2,1)}, bf16[1,512,256]{2,1,0:T(8,128)(2,1)S(1)}, u32[]{:S(2)}) copy-start(bf16[1,512,256]{2,1,0:T(8,128)(2,1)S(1)} %collective-permute-done.17.refs_2_) | copy-start | bytes 786436
  295.5 69.1 %collective-permute-start.22 = (bf16[2,512,768]{2,1,0:T(8,128)(2,1)}, bf16[2,512,768]{2,1,0:T(8,128)(2,1)}, u32[]{:S(2)}, u32[]{:S(2)}) collective-permute-start(bf16[2,512,768]{2,1,0:T(8,128)(2,1)} %get-tuple-element.64), channel_id=1, source_target_pairs={{0,2},{1,3},{2,0},{3,1},{4,6},{5,7},{6,4},{7,5},{8,10},{9,11},{10,... | collective-permute-start | bytes 4718600 | tf_op jit(solution)/shard_map/ppermute | solution.py:21
  295.6 23.1 %copy-start.1 = (f32[4,2,2,2,64,256]{5,4,3,2,1,0:T(8,128)}, f32[4,2,2,2,64,256]{5,4,3,2,1,0:T(8,128)S(1)}, u32[]{:S(2)}) copy-start(f32[4,2,2,2,64,256]{5,4,3,2,1,0:T(8,128)S(1)} %collective-permute-done.36.recv_ref) | copy-start | bytes 6291460
  295.6 71.3 %collective-permute-start.23 = (bf16[2,512,768]{2,1,0:T(8,128)(2,1)}, bf16[2,512,768]{2,1,0:T(8,128)(2,1)}, u32[]{:S(2)}, u32[]{:S(2)}) collective-permute-start(bf16[2,512,768]{2,1,0:T(8,128)(2,1)} %get-tuple-element.65), channel_id=1, source_target_pairs={{0,4},{1,5},{2,6},{3,7},{4,0},{5,1},{6,2},{7,3},{8,12},{9,13},{10,... | collective-permute-start | bytes 4718600 | tf_op jit(solution)/shard_map/ppermute | solution.py:21
  310.1 56.7 %collective-permute-start.18 = (bf16[2,512,768]{2,1,0:T(8,128)(2,1)}, bf16[2,512,768]{2,1,0:T(8,128)(2,1)}, u32[]{:S(2)}, u32[]{:S(2)}) collective-permute-start(bf16[2,512,768]{2,1,0:T(8,128)(2,1)} %get-tuple-element.60), channel_id=1, source_target_pairs={{0,1},{1,0},{2,3},{3,2},{4,5},{5,4},{6,7},{7,6},{8,9},{9,8},{10,11... | collective-permute-start | bytes 4718600 | tf_op jit(solution)/shard_map/ppermute | solution.py:21
  310.6 62.1 %collective-permute-start.30 = (f32[4,2,2,2,64,256]{5,4,3,2,1,0:T(8,128)}, f32[4,2,2,2,64,256]{5,4,3,2,1,0:T(8,128)}, u32[]{:S(2)}, u32[]{:S(2)}) collective-permute-start(f32[4,2,2,2,64,256]{5,4,3,2,1,0:T(8,128)} %get-tuple-element.79), channel_id=1, source_target_pairs={{0,8},{8,0},{16,24},{24,16},{1,9},{9,1},{17,25},{25,17},{2,10},{10... | collective-permute-start | bytes 6291464 | tf_op jit(solution)/shard_map/ppermute | solution.py:21
  318.7 163.9 %collective-permute-start.35 = (f32[12,1,2,2,64,256]{5,4,3,2,1,0:T(8,128)}, f32[12,1,2,2,64,256]{5,4,3,2,1,0:T(8,128)S(1)}, u32[]{:S(2)}, u32[]{:S(2)}) collective-permute-start(f32[12,1,2,2,64,256]{5,4,3,2,1,0:T(8,128)} %get-tuple-element.89), channel_id=1, source_target_pairs={{0,16},{8,24},{16,0},{24,8},{1,17},{9,25},{17,1},{25,9},{2,18},{10... | collective-permute-start | bytes 9437192 | tf_op jit(solution)/shard_map/ppermute | solution.py:21
  364.7 124.8 %collective-permute-start.33 = (f32[12,1,2,2,64,256]{5,4,3,2,1,0:T(8,128)}, f32[12,1,2,2,64,256]{5,4,3,2,1,0:T(8,128)}, u32[]{:S(2)}, u32[]{:S(2)}) collective-permute-start(f32[12,1,2,2,64,256]{5,4,3,2,1,0:T(8,128)} %get-tuple-element.85), channel_id=1, source_target_pairs={{0,16},{8,24},{16,0},{24,8},{1,17},{9,25},{17,1},{25,9},{2,18},{10... | collective-permute-start | bytes 9437192 | tf_op jit(solution)/shard_map/ppermute | solution.py:21
  366.8 68.4 %collective-permute-start.19 = (bf16[2,512,768]{2,1,0:T(8,128)(2,1)}, bf16[2,512,768]{2,1,0:T(8,128)(2,1)}, u32[]{:S(2)}, u32[]{:S(2)}) collective-permute-start(bf16[2,512,768]{2,1,0:T(8,128)(2,1)} %get-tuple-element.61), channel_id=1, source_target_pairs={{0,2},{1,3},{2,0},{3,1},{4,6},{5,7},{6,4},{7,5},{8,10},{9,11},{10,... | collective-permute-start | bytes 4718600 | tf_op jit(solution)/shard_map/ppermute | solution.py:21
  366.8 70.4 %collective-permute-start.20 = (bf16[2,512,768]{2,1,0:T(8,128)(2,1)}, bf16[2,512,768]{2,1,0:T(8,128)(2,1)}, u32[]{:S(2)}, u32[]{:S(2)}) collective-permute-start(bf16[2,512,768]{2,1,0:T(8,128)(2,1)} %get-tuple-element.62), channel_id=1, source_target_pairs={{0,4},{1,5},{2,6},{3,7},{4,0},{5,1},{6,2},{7,3},{8,12},{9,13},{10,... | collective-permute-start | bytes 4718600 | tf_op jit(solution)/shard_map/ppermute | solution.py:21
  372.7 107.2 %collective-permute-start.37 = (f32[4,1,2,2,64,256]{5,4,3,2,1,0:T(8,128)}, f32[4,1,2,2,64,256]{5,4,3,2,1,0:T(8,128)}, u32[]{:S(2)}, u32[]{:S(2)}) collective-permute-start(f32[4,1,2,2,64,256]{5,4,3,2,1,0:T(8,128)} %get-tuple-element.93), channel_id=1, source_target_pairs={{0,16},{8,24},{16,0},{24,8},{1,17},{9,25},{17,1},{25,9},{2,18},{10... | collective-permute-start | bytes 3145736 | tf_op jit(solution)/shard_map/ppermute | solution.py:21
  435.3 66.6 %collective-permute-start.31 = (f32[4,1,2,2,64,256]{5,4,3,2,1,0:T(8,128)}, f32[4,1,2,2,64,256]{5,4,3,2,1,0:T(8,128)}, u32[]{:S(2)}, u32[]{:S(2)}) collective-permute-start(f32[4,1,2,2,64,256]{5,4,3,2,1,0:T(8,128)} %get-tuple-element.81), channel_id=1, source_target_pairs={{0,16},{8,24},{16,0},{24,8},{1,17},{9,25},{17,1},{25,9},{2,18},{10... | collective-permute-start | bytes 3145736 | tf_op jit(solution)/shard_map/ppermute | solution.py:21
  437.2 16.5 %collective-permute-start.29 = (bf16[1,512,256]{2,1,0:T(8,128)(2,1)}, bf16[1,512,256]{2,1,0:T(8,128)(2,1)}, u32[]{:S(2)}, u32[]{:S(2)}) collective-permute-start(bf16[1,512,256]{2,1,0:T(8,128)(2,1)} %get-tuple-element.77), channel_id=1, source_target_pairs={{0,4},{1,5},{2,6},{3,7},{4,0},{5,1},{6,2},{7,3},{8,12},{9,13},{10,... | collective-permute-start | bytes 786440 | tf_op jit(solution)/shard_map/ppermute | solution.py:21
  482.5 1.8 copy-start

commit v6 on v5

--- a/solution.py
+++ b/solution.py
@@ -11,7 +11,7 @@
 def row_groups(local):
     edge = max(1, local // 8)
     middle = local - 2 * edge
-    sizes = [edge, middle - middle // 2, middle // 2, edge] if middle >= 0 else [local]
+    sizes = [edge, middle - middle // 3, middle // 3, edge] if middle >= 0 else [local]
     return [size for size in sizes if size > 0]
 
 
@@ -19,6 +19,13 @@
     mask = 2**distance
     pairs = [(source, source ^ mask) for source in range(lax.axis_size(axis))]
     return lax.ppermute(value, axis, pairs)
+
+
+def partners_of(values):
+    arrived = []
+    for bit, value in enumerate(values):
+        arrived.append(partner(value, "mp", bit))
+    return arrived
 
 
 def gelu_pair(hidden):
@@ -313,8 +320,9 @@
     _, _, width = acc.shape
     for row in range(rows):
         lanes = slice(row * width, (row + 1) * width)
-        total = acc[start + row]
-        for value in arrived:
+        total = acc[start + row] + arrived[0][0, :, lanes].astype(jnp.float32)
+        total = lax.optimization_barrier(total)
+        for value in arrived[1:]:
             total = total + value[0, :, lanes].astype(jnp.float32)
         whole = lax.dynamic_update_slice(whole, total.astype(whole.dtype), (0, (start + row) * width))
     return whole
@@ -350,14 +358,11 @@
                     block = array[None, :, start * width : (start + rows) * width]
                 else:
                     block = pack_call(start, rows, width, array)
-                sent = []
-                for bit in range(bits):
-                    sent.append(partner(block, "mp", bit))
-                parts.append(sent)
+                parts.append(partners_of([block] * bits))
             arrived.append([parts[kind][bit] for bit in range(bits) for kind in range(2)])
         else:
             pair = pack_call(start, rows, width, inputs, out_grad)
-            arrived.append([partner(pair, "mp", bit) for bit in range(bits)])
+            arrived.append(partners_of([pair] * bits))
 
     acc = None
     returned = []
@@ -374,10 +379,10 @@
         if group == last:
             parts = []
             for kind in range(2):
-                parts.append([partner(sends[2 * bit + kind], "mp", bit) for bit in range(bits)])
+                parts.append(partners_of(sends[kind::2]))
             returned.append(parts)
         else:
-            returned.append([partner(sends[bit], "mp", bit) for bit in range(bits)])
+            returned.append(partners_of(sends))
         for bit in range(1, dp_bits):
             recv = partner(send, "dp", bit - 1)
             keep, send = halve_call(per_row, parities[bit], keep, recv)

time: 506 us -> 607 us (1.20)
  waiting for transfers between devices: 296 us -> 404 us
    ppermute x38, waiting for transfers between devices: 296 us -> 404 us  [partner(): return lax.ppermute(value, axis, pairs)]
  transfers between devices with their start and end apart: 38 -> 38, of which waited for: 22 -> 20; matrix products, arithmetic and copies ran while one was open for 1% -> 1% of each run, Pallas kernels for 30% -> 18%
where the time goes in v6:
time: 607 us; the launch traced here: 605 us
  waiting for transfers between devices  404 us (67%)
  Pallas kernels  153 us (25%)
  starting transfers between devices  39.2 us (6%)
  local copies, waits for them, and re-layouts  6.19 us (1%)
    ppermute x38, waiting for transfers between devices, partner(): return lax.ppermute(value, axis, pairs)  404 us
    pallas_call x4, Pallas kernels, main_call(): pl.pallas_call(functools.partial(main_body, dims), grid_spec=pltpu.Prefet...  91.6 us
    ppermute x38, starting transfers between devices, partner(): return lax.ppermute(value, axis, pairs)  39.2 us
    pallas_call x4, Pallas kernels, halve_call(): pl.pallas_call(halve_body, grid_spec=pltpu.PrefetchScalarGridSpec(num_sca...  21.9 us
    pallas_call x4, Pallas kernels, total_call(): pl.pallas_call(functools.partial(total_body, bits, kinds), grid=(rows, 2)...  16.1 us
    pallas_call x4, Pallas kernels, grads_call(): pl.pallas_call(grads_body, grid=(cols // block,), in_specs=[spec, spec] +...  14.2 us
  transfers between devices with their start and end apart: 38, of which 20 were waited for; matrix products, arithmetic and copies ran while one was open for 1% of the time, Pallas kernels for 18%

profile of v6, /device:TPU:0, one launch (start us, length us, event | category | flops | bytes accessed | tf_op | source)
XLA Modules:
  0.0 605.3 jit_solution(1292414721708112567)
XLA Ops:
  0.6 3.8 pack.6
  4.4 3.0 collective-permute-start.6
  7.4 1.6 collective-permute-start.7
  9.0 2.6 collective-permute-start.8
  11.5 1.7 pack.7
  13.7 1.0 slice_bitcast_fusion
  15.2 43.6 %collective-permute-done.10.refs_3_ = bf16[1,512,256]{2,1,0:T(8,128)(2,1)S(1)} collective-permute-done((bf16[1,512,256]{2,1,0:T(8,128)(2,1)}, bf16[1,512,256]{2,1,0:T(8,128)(2,1)S(1)}, u32[]{:S(2)}, u32[]{:S(2)}) %collective-permute-start.10) | collective-permute-done | bytes 262176 | tf_op jit(solution)/shard_map/ppermute | solution.py:21
  58.8 1.8 collective-permute-start.12
  60.7 46.0 %collective-permute-done.11.refs_4_ = bf16[1,512,256]{2,1,0:T(8,128)(2,1)S(1)} collective-permute-done((bf16[1,512,256]{2,1,0:T(8,128)(2,1)S(1)}, bf16[1,512,256]{2,1,0:T(8,128)(2,1)S(1)}, u32[]{:S(2)}, u32[]{:S(2)}) %collective-permute-start.11) | collective-permute-done | bytes 262176 | tf_op jit(solution)/shard_map/ppermute | solution.py:21
  106.7 2.6 collective-permute-start.13
  109.3 6.3 %collective-permute-done.12.refs_5_ = bf16[1,512,256]{2,1,0:T(8,128)(2,1)S(1)} collective-permute-done((bf16[1,512,256]{2,1,0:T(8,128)(2,1)}, bf16[1,512,256]{2,1,0:T(8,128)(2,1)S(1)}, u32[]{:S(2)}, u32[]{:S(2)}) %collective-permute-start.12) | collective-permute-done | bytes 262176 | tf_op jit(solution)/shard_map/ppermute | solution.py:21
  115.7 10.4 %collective-permute-done.13.refs_6_ = bf16[1,512,256]{2,1,0:T(8,128)(2,1)S(1)} collective-permute-done((bf16[1,512,256]{2,1,0:T(8,128)(2,1)S(1)}, bf16[1,512,256]{2,1,0:T(8,128)(2,1)S(1)}, u32[]{:S(2)}, u32[]{:S(2)}) %collective-permute-start.13) | collective-permute-done | bytes 262176 | tf_op jit(solution)/shard_map/ppermute | solution.py:21
  127.4 3.3 collective-permute-done.14.refs_7_
  130.8 1.6 collective-permute-done.9.refs_2_
  132.5 0.7 copy-done.12
  133.1 14.6 %columns.4 = (f32[2,8,512,256]{3,2,1,0:T(8,128)}, bf16[2,512,256]{2,1,0:T(8,128)(2,1)}, bf16[2,512,256]{2,1,0:T(8,128)(2,1)}, bf16[2,512,256]{2,1,0:T(8,128)(2,1...) custom-call(s32[8]{0:T(128)} %reshape.38.slots_ref, s32[1]{0:T(128)} %bitcast.parity_ref, ...), custom_call_target="tpu_custom_call" | custom-call | flops 3221225472 | bytes 23592960 | tf_op jit(solution)/shard_map/columns/pallas_call | solution.py:198
  147.8 36.3 %columns.5 = (f32[2,8,512,256]{3,2,1,0:T(8,128)}, bf16[2,512,1024]{2,1,0:T(8,128)(2,1)}, bf16[2,512,1024]{2,1,0:T(8,128)(2,1)}, bf16[2,512,1024]{2,1,0:T(8,128)(...) custom-call(s32[32]{0:T(128)} %reshape.37.slots_ref, s32[1]{0:T(128)} %bitcast.parity_ref, ...), custom_call_target="tpu_custom_call" | custom-call | flops 12884901888 | bytes 56623104 | tf_op jit(solution)/shard_map/columns/pallas_call | solution.py:198
  184.2 2.1 pack.5
  186.2 2.2 collective-permute-start.4
  188.4 3.4 collective-permute-start.5
  191.8 1.9 pack.4
  193.7 1.5 collective-permute-start
  195.8 16.7 %collective-permute-done.3.refs_2_ = bf16[2,512,512]{2,1,0:T(8,128)(2,1)S(1)} collective-permute-done((bf16[2,512,512]{2,1,0:T(8,128)(2,1)}, bf16[2,512,512]{2,1,0:T(8,128)(2,1)S(1)}, u32[]{:S(2)}, u32[]{:S(2)}) %collective-permute-start.3) | collective-permute-done | bytes 1048608 | tf_op jit(solution)/shard_map/ppermute | solution.py:21
  212.5 22.0 %collective-permute-done.4.refs_3_ = bf16[2,512,512]{2,1,0:T(8,128)(2,1)} collective-permute-done((bf16[2,512,512]{2,1,0:T(8,128)(2,1)}, bf16[2,512,512]{2,1,0:T(8,128)(2,1)}, u32[]{:S(2)}, u32[]{:S(2)}) %collective-permute-start.4) | collective-permute-done | bytes 1048608 | tf_op jit(solution)/shard_map/ppermute | solution.py:21
  234.5 3.4 collective-permute-done.5.refs_4_
  237.9 23.6 %columns.6 = (f32[2,8,512,256]{3,2,1,0:T(8,128)}, bf16[2,512,512]{2,1,0:T(8,128)(2,1)}, bf16[2,512,512]{2,1,0:T(8,128)(2,1)}, bf16[2,512,512]{2,1,0:T(8,128)(2,1...) custom-call(s32[16]{0:T(128)} %reshape.36.slots_ref, s32[1]{0:T(128)} %bitcast.parity_ref, ...), custom_call_target="tpu_custom_call" | custom-call | flops 6442450944 | bytes 34603008 | tf_op jit(solution)/shard_map/columns/pallas_call | solution.py:198
  262.0 2.6 collective-permute-start.2
  264.6 22.4 %collective-permute-done.1.refs_3_ = bf16[2,512,256]{2,1,0:T(8,128)(2,1)} collective-permute-done((bf16[2,512,256]{2,1,0:T(8,128)(2,1)S(1)}, bf16[2,512,256]{2,1,0:T(8,128)(2,1)}, u32[]{:S(2)}, u32[]{:S(2)}) %collective-permute-start.1) | collective-permute-done | bytes 524320 | tf_op jit(solution)/shard_map/ppermute | solution.py:21
  286.9 1.5 collective-permute-start.24
  288.5 12.1 %collective-permute-done.24.refs_0_ = bf16[2,512,256]{2,1,0:T(8,128)(2,1)} collective-permute-done((bf16[2,512,256]{2,1,0:T(8,128)(2,1)}, bf16[2,512,256]{2,1,0:T(8,128)(2,1)}, u32[]{:S(2)}, u32[]{:S(2)}) %collective-permute-start.24) | collective-permute-done | bytes 524320 | tf_op jit(solution)/shard_map/ppermute | solution.py:21
  301.8 0.8 copy-done.5
  302.5 1.1 collective-permute-start.18
  303.6 17.1 %columns.7 = (f32[2,8,512,256]{3,2,1,0:T(8,128)}, bf16[1,512,256]{2,1,0:T(8,128)(2,1)}, bf16[1,512,256]{2,1,0:T(8,128)(2,1)}, bf16[1,512,256]{2,1,0:T(8,128)(2,1...) custom-call(s32[8]{0:T(128)} %reshape.34.slots_ref, ...), custom_call_target="tpu_custom_call" | custom-call | flops 3221225472 | bytes 23592960 | tf_op jit(solution)/shard_map/columns/pallas_call | solution.py:198
  320.7 4.3 collective-permute-done.26.refs_2_
  325.0 1.5 collective-permute-start.27
  327.1 7.4 %collective-permute-done.27 = bf16[1,512,256]{2,1,0:T(8,128)(2,1)S(1)} collective-permute-done((bf16[1,512,256]{2,1,0:T(8,128)(2,1)}, bf16[1,512,256]{2,1,0:T(8,128)(2,1)S(1)}, u32[]{:S(2)}, u32[]{:S(2)}) %collective-permute-start.27) | collective-permute-done | bytes 262176 | tf_op jit(solution)/shard_map/ppermute | solution.py:21
  334.6 4.5 collective-permute-done.15.refs_0_
  339.2 2.3 collective-permute-start.17
  341.5 9.0 %halve.6 = (f32[16,1,2,2,64,256]{5,4,3,2,1,0:T(8,128)}, f32[16,1,2,2,64,256]{5,4,3,2,1,0:T(8,128)}) custom-call(s32[1]{0:T(128)} %bitcast.6.parity_ref, f32[16,2,2,2,64,256]{5,4,3,2,1,0:T(8,128)} %get-tuple-element.86.keep_ref, f32[16,2,2,2,64,256]{5,4,3,2,1,0:T(8,128)} %collective-permute-done.34.recv_ref), custom_call_target="tpu_custom_call" | custom-call | flops 2097152 | bytes 25165824 | tf_op jit(solution)/shard_map/halve/pallas_call | solution.py:248
  350.5 18.8 %collective-permute-done.16.refs_1_ = bf16[1,512,256]{2,1,0:T(8,128)(2,1)} collective-permute-done((bf16[1,512,256]{2,1,0:T(8,128)(2,1)}, bf16[1,512,256]{2,1,0:T(8,128)(2,1)}, u32[]{:S(2)}, u32[]{:S(2)}) %collective-permute-start.16) | collective-permute-done | bytes 262176 | tf_op jit(solution)/shard_map/ppermute | solution.py:21
  369.3 1.5 collective-permute-start.35
  370.9 4.0 halve.7
  374.9 0.9 collective-permute-start.37
  375.8 43.3 %collective-permute-done.20.refs_2_ = bf16[2,512,512]{2,1,0:T(8,128)(2,1)S(1)} collective-permute-done((bf16[2,512,512]{2,1,0:T(8,128)(2,1)}, bf16[2,512,512]{2,1,0:T(8,128)(2,1)S(1)}, u32[]{:S(2)}, u32[]{:S(2)}) %collective-permute-start.20) | collective-permute-done | bytes 1048608 | tf_op jit(solution)/shard_map/ppermute | solution.py:21
  419.1 1.0 copy-done.4
  420.1 1.5 collective-permute-start.21
  421.6 60.3 %collective-permute-done.37.recv_ref = f32[4,1,2,2,64,256]{5,4,3,2,1,0:T(8,128)} collective-permute-done((f32[4,1,2,2,64,256]{5,4,3,2,1,0:T(8,128)}, f32[4,1,2,2,64,256]{5,4,3,2,1,0:T(8,128)}, u32[]{:S(2)}, u32[]{:S(2)}) %collective-permute-start.37) | collective-permute-done | bytes 1048608 | tf_op jit(solution)/shard_map/ppermute | solution.py:21
  481.9 2.3 collective-permute-start.23
  484.2 5.1 halve.5
  489.3 1.5 collective-permute-start.33
  490.8 3.8 halve.4
  495.1 75.3 %collective-permute-done.22.refs_1_ = bf16[2,512,1024]{2,1,0:T(8,128)(2,1)} collective-permute-done((bf16[2,512,1024]{2,1,0:T(8,128)(2,1)}, bf16[2,512,1024]{2,1,0:T(8,128)(2,1)}, u32[]{:S(2)}, u32[]{:S(2)}) %collective-permute-start.22) | collective-permute-done | bytes 2097184 | tf_op jit(solution)/shard_map/ppermute | solution.py:21
  570.4 1.8 collective-permute-done.23.refs_2_
  572.1 0.8 collective-permute-start.29
  573.0 2.5 totals.4
  575.5 1.1 convert_add_fusion.2
  576.6 2.6 grads.4
  579.2 7.4 %totals.5 = (bf16[512,2048]{1,0:T(8,128)(2,1)}, bf16[512,2048]{1,0:T(8,128)(2,1)}) custom-call(f32[2,8,512,256]{3,2,1,0:T(8,128)} %get-tuple-element.56.acc_ref, bf16[2,512,1024]{2,1,0:T(8,128)(2,1)} %copy-done, bf16[2,512,1024]{2,1,0:T(8,128)(2,1)} %collective-permute-done.22.refs_1_, ...), custom_call_target="tpu_custom_call", output_to_operand_aliasing={{0}: (4, {}), {1}: (5, {})} | custom-call | flops 3145728 | bytes 12582912 | tf_op jit(solution)/shard_map/totals/pallas_call | solution.py:307
  586.6 4.2 totals.6
  590.8 2.0 totals.7
  592.8 0.8 fusion.1
  593.6 5.7 grads.5
  599.4 3.3 grads.6
  602.7 2.6 grads.7
  (78 shorter events, 6.4 us)
Async XLA Ops:
  4.4 121.7 %copy-start.16 = (s32[2,32]{1,0:T(2,128)S(1)}, s32[2,32]{1,0:T(2,128)}, u32[]{:S(2)}) copy-start(s32[2,32]{1,0:T(2,128)} %param.9) | copy-start | bytes 772
  4.4 143.4 %collective-permute-start.6 = (bf16[2,512,1024]{2,1,0:T(8,128)(2,1)}, bf16[2,512,1024]{2,1,0:T(8,128)(2,1)}, u32[]{:S(2)}, u32[]{:S(2)}) collective-permute-start(bf16[2,512,1024]{2,1,0:T(8,128)(2,1)} %pack.6), channel_id=1, source_target_pairs={{0,1},{1,0},{2,3},{3,2},{4,5},{5,4},{6,7},{7,6},{8,9},{9,8},{10,11... | collective-permute-start | bytes 6291464 | tf_op jit(solution)/shard_map/ppermute | solution.py:21
  7.4 140.4 %collective-permute-start.7 = (bf16[2,512,1024]{2,1,0:T(8,128)(2,1)}, bf16[2,512,1024]{2,1,0:T(8,128)(2,1)}, u32[]{:S(2)}, u32[]{:S(2)}) collective-permute-start(bf16[2,512,1024]{2,1,0:T(8,128)(2,1)} %pack.6), channel_id=1, source_target_pairs={{0,2},{1,3},{2,0},{3,1},{4,6},{5,7},{6,4},{7,5},{8,10},{9,11},{10,... | collective-permute-start | bytes 6291464 | tf_op jit(solution)/shard_map/ppermute | solution.py:21
  9.0 138.8 %collective-permute-start.8 = (bf16[2,512,1024]{2,1,0:T(8,128)(2,1)}, bf16[2,512,1024]{2,1,0:T(8,128)(2,1)}, u32[]{:S(2)}, u32[]{:S(2)}) collective-permute-start(bf16[2,512,1024]{2,1,0:T(8,128)(2,1)} %pack.6), channel_id=1, source_target_pairs={{0,4},{1,5},{2,6},{3,7},{4,0},{5,1},{6,2},{7,3},{8,12},{9,13},{10,... | collective-permute-start | bytes 6291464 | tf_op jit(solution)/shard_map/ppermute | solution.py:21
  13.2 45.6 %collective-permute-start.10 = (bf16[1,512,256]{2,1,0:T(8,128)(2,1)}, bf16[1,512,256]{2,1,0:T(8,128)(2,1)S(1)}, u32[]{:S(2)}, u32[]{:S(2)}) collective-permute-start(bf16[1,512,256]{2,1,0:T(8,128)(2,1)} %pack.7), channel_id=1, source_target_pairs={{0,1},{1,0},{2,3},{3,2},{4,5},{5,4},{6,7},{7,6},{8,9},{9,8},{10,11... | collective-permute-start | bytes 786440 | tf_op jit(solution)/shard_map/ppermute | solution.py:21
  14.7 91.9 %collective-permute-start.11 = (bf16[1,512,256]{2,1,0:T(8,128)(2,1)S(1)}, bf16[1,512,256]{2,1,0:T(8,128)(2,1)S(1)}, u32[]{:S(2)}, u32[]{:S(2)}) collective-permute-start(bf16[1,512,256]{2,1,0:T(8,128)(2,1)S(1)} %slice_bitcast_fusion), channel_id=1, source_target_pairs={{0,2},{1,3},{2,0},{3,1},{4,6},{5,7},{6,4},{7,5},{8,10},{9,11},{10,... | collective-permute-start | bytes 786440 | tf_op jit(solution)/shard_map/ppermute | solution.py:21
  58.8 73.6 %copy-start.7 = (bf16[1,512,256]{2,1,0:T(8,128)(2,1)}, bf16[1,512,256]{2,1,0:T(8,128)(2,1)S(1)}, u32[]{:S(2)}) copy-start(bf16[1,512,256]{2,1,0:T(8,128)(2,1)S(1)} %collective-permute-done.10.refs_3_) | copy-start | bytes 786436
  58.8 56.7 %collective-permute-start.12 = (bf16[1,512,256]{2,1,0:T(8,128)(2,1)}, bf16[1,512,256]{2,1,0:T(8,128)(2,1)S(1)}, u32[]{:S(2)}, u32[]{:S(2)}) collective-permute-start(bf16[1,512,256]{2,1,0:T(8,128)(2,1)} %pack.7), channel_id=1, source_target_pairs={{0,2},{1,3},{2,0},{3,1},{4,6},{5,7},{6,4},{7,5},{8,10},{9,11},{10,... | collective-permute-start | bytes 786440 | tf_op jit(solution)/shard_map/ppermute | solution.py:21
  106.6 25.8 %copy-start.8 = (bf16[1,512,256]{2,1,0:T(8,128)(2,1)}, bf16[1,512,256]{2,1,0:T(8,128)(2,1)S(1)}, u32[]{:S(2)}) copy-start(bf16[1,512,256]{2,1,0:T(8,128)(2,1)S(1)} %collective-permute-done.11.refs_4_) | copy-start | bytes 786436
  106.7 19.4 %collective-permute-start.13 = (bf16[1,512,256]{2,1,0:T(8,128)(2,1)S(1)}, bf16[1,512,256]{2,1,0:T(8,128)(2,1)S(1)}, u32[]{:S(2)}, u32[]{:S(2)}) collective-permute-start(bf16[1,512,256]{2,1,0:T(8,128)(2,1)S(1)} %slice_bitcast_fusion), channel_id=1, source_target_pairs={{0,4},{1,5},{2,6},{3,7},{4,0},{5,1},{6,2},{7,3},{8,12},{9,13},{10,... | collective-permute-start | bytes 786440 | tf_op jit(solution)/shard_map/ppermute | solution.py:21
  115.6 16.9 %copy-start.9 = (bf16[1,512,256]{2,1,0:T(8,128)(2,1)}, bf16[1,512,256]{2,1,0:T(8,128)(2,1)S(1)}, u32[]{:S(2)}) copy-start(bf16[1,512,256]{2,1,0:T(8,128)(2,1)S(1)} %collective-permute-done.12.refs_5_) | copy-start | bytes 786436
  115.6 15.2 %collective-permute-start.14 = (bf16[1,512,256]{2,1,0:T(8,128)(2,1)}, bf16[1,512,256]{2,1,0:T(8,128)(2,1)S(1)}, u32[]{:S(2)}, u32[]{:S(2)}) collective-permute-start(bf16[1,512,256]{2,1,0:T(8,128)(2,1)} %pack.7), channel_id=1, source_target_pairs={{0,4},{1,5},{2,6},{3,7},{4,0},{5,1},{6,2},{7,3},{8,12},{9,13},{10,... | collective-permute-start | bytes 786440 | tf_op jit(solution)/shard_map/ppermute | solution.py:21
  126.1 6.4 %copy-start.10 = (bf16[1,512,256]{2,1,0:T(8,128)(2,1)}, bf16[1,512,256]{2,1,0:T(8,128)(2,1)S(1)}, u32[]{:S(2)}) copy-start(bf16[1,512,256]{2,1,0:T(8,128)(2,1)S(1)} %collective-permute-done.13.refs_6_) | copy-start | bytes 786436
  126.1 6.4 %collective-permute-start.9 = (bf16[1,512,256]{2,1,0:T(8,128)(2,1)S(1)}, bf16[1,512,256]{2,1,0:T(8,128)(2,1)S(1)}, u32[]{:S(2)}, u32[]{:S(2)}) collective-permute-start(bf16[1,512,256]{2,1,0:T(8,128)(2,1)S(1)} %slice_bitcast_fusion), channel_id=1, source_target_pairs={{0,1},{1,0},{2,3},{3,2},{4,5},{5,4},{6,7},{7,6},{8,9},{9,8},{10,11... | collective-permute-start | bytes 786440 | tf_op jit(solution)/shard_map/ppermute | solution.py:21
  130.8 1.7 copy-start.11
  132.4 0.7 copy-start.12
  184.1 155.1 %collective-permute-start.34 = (f32[16,2,2,2,64,256]{5,4,3,2,1,0:T(8,128)}, f32[16,2,2,2,64,256]{5,4,3,2,1,0:T(8,128)}, u32[]{:S(2)}, u32[]{:S(2)}) collective-permute-start(f32[16,2,2,2,64,256]{5,4,3,2,1,0:T(8,128)} %get-tuple-element.87), channel_id=1, source_target_pairs={{0,8},{8,0},{16,24},{24,16},{1,9},{9,1},{17,25},{25,17},{2,10},{10... | collective-permute-start | bytes 25165832 | tf_op jit(solution)/shard_map/ppermute | solution.py:21
  186.2 26.2 %collective-permute-start.3 = (bf16[2,512,512]{2,1,0:T(8,128)(2,1)}, bf16[2,512,512]{2,1,0:T(8,128)(2,1)S(1)}, u32[]{:S(2)}, u32[]{:S(2)}) collective-permute-start(bf16[2,512,512]{2,1,0:T(8,128)(2,1)} %pack.5), channel_id=1, source_target_pairs={{0,1},{1,0},{2,3},{3,2},{4,5},{5,4},{6,7},{7,6},{8,9},{9,8},{10,11... | collective-permute-start | bytes 3145736 | tf_op jit(solution)/shard_map/ppermute | solution.py:21
  186.2 48.3 %collective-permute-start.4 = (bf16[2,512,512]{2,1,0:T(8,128)(2,1)}, bf16[2,512,512]{2,1,0:T(8,128)(2,1)}, u32[]{:S(2)}, u32[]{:S(2)}) collective-permute-start(bf16[2,512,512]{2,1,0:T(8,128)(2,1)} %pack.5), channel_id=1, source_target_pairs={{0,2},{1,3},{2,0},{3,1},{4,6},{5,7},{6,4},{7,5},{8,10},{9,11},{10,... | collective-permute-start | bytes 3145736 | tf_op jit(solution)/shard_map/ppermute | solution.py:21
  188.4 49.5 %collective-permute-start.5 = (bf16[2,512,512]{2,1,0:T(8,128)(2,1)}, bf16[2,512,512]{2,1,0:T(8,128)(2,1)}, u32[]{:S(2)}, u32[]{:S(2)}) collective-permute-start(bf16[2,512,512]{2,1,0:T(8,128)(2,1)} %pack.5), channel_id=1, source_target_pairs={{0,4},{1,5},{2,6},{3,7},{4,0},{5,1},{6,2},{7,3},{8,12},{9,13},{10,... | collective-permute-start | bytes 3145736 | tf_op jit(solution)/shard_map/ppermute | solution.py:21
  193.7 68.4 %collective-permute-start = (bf16[2,512,256]{2,1,0:T(8,128)(2,1)}, bf16[2,512,256]{2,1,0:T(8,128)(2,1)}, u32[]{:S(2)}, u32[]{:S(2)}) collective-permute-start(bf16[2,512,256]{2,1,0:T(8,128)(2,1)} %pack.4), channel_id=1, source_target_pairs={{0,1},{1,0},{2,3},{3,2},{4,5},{5,4},{6,7},{7,6},{8,9},{9,8},{10,11... | collective-permute-start | bytes 1572872 | tf_op jit(solution)/shard_map/ppermute | solution.py:21
  212.5 25.4 %copy-start.2 = (bf16[2,512,512]{2,1,0:T(8,128)(2,1)}, bf16[2,512,512]{2,1,0:T(8,128)(2,1)S(1)}, u32[]{:S(2)}) copy-start(bf16[2,512,512]{2,1,0:T(8,128)(2,1)S(1)} %collective-permute-done.3.refs_2_) | copy-start | bytes 3145732
  212.5 114.0 %collective-permute-start.36 = (f32[4,2,2,2,64,256]{5,4,3,2,1,0:T(8,128)}, f32[4,2,2,2,64,256]{5,4,3,2,1,0:T(8,128)S(1)}, u32[]{:S(2)}, u32[]{:S(2)}) collective-permute-start(f32[4,2,2,2,64,256]{5,4,3,2,1,0:T(8,128)} %get-tuple-element.91), channel_id=1, source_target_pairs={{0,8},{8,0},{16,24},{24,16},{1,9},{9,1},{17,25},{25,17},{2,10},{10... | collective-permute-start | bytes 6291464 | tf_op jit(solution)/shard_map/ppermute | solution.py:21
  237.9 23.7 %copy-start.6 = (bf16[2,512,256]{2,1,0:T(8,128)(2,1)S(1)}, bf16[2,512,256]{2,1,0:T(8,128)(2,1)}, u32[]{:S(2)}) copy-start(bf16[2,512,256]{2,1,0:T(8,128)(2,1)} %pack.4) | copy-start | bytes 1572868
  261.5 220.4 %collective-permute-start.32 = (f32[8,2,2,2,64,256]{5,4,3,2,1,0:T(8,128)}, f32[8,2,2,2,64,256]{5,4,3,2,1,0:T(8,128)}, u32[]{:S(2)}, u32[]{:S(2)}) collective-permute-start(f32[8,2,2,2,64,256]{5,4,3,2,1,0:T(8,128)} %get-tuple-element.83), channel_id=1, source_target_pairs={{0,8},{8,0},{16,24},{24,16},{1,9},{9,1},{17,25},{25,17},{2,10},{10... | collective-permute-start | bytes 12582920 | tf_op jit(solution)/shard_map/ppermute | solution.py:21
  261.6 25.3 %collective-permute-start.1 = (bf16[2,512,256]{2,1,0:T(8,128)(2,1)S(1)}, bf16[2,512,256]{2,1,0:T(8,128)(2,1)}, u32[]{:S(2)}, u32[]{:S(2)}) collective-permute-start(bf16[2,512,256]{2,1,0:T(8,128)(2,1)S(1)} %copy-done.6), channel_id=1, source_target_pairs={{0,2},{1,3},{2,0},{3,1},{4,6},{5,7},{6,4},{7,5},{8,10},{9,11},{10,... | collective-permute-start | bytes 1572872 | tf_op jit(solution)/shard_map/ppermute | solution.py:21
  262.0 26.4 %collective-permute-start.2 = (bf16[2,512,256]{2,1,0:T(8,128)(2,1)S(1)}, bf16[2,512,256]{2,1,0:T(8,128)(2,1)}, u32[]{:S(2)}, u32[]{:S(2)}) collective-permute-start(bf16[2,512,256]{2,1,0:T(8,128)(2,1)S(1)} %copy-done.6), channel_id=1, source_target_pairs={{0,4},{1,5},{2,6},{3,7},{4,0},{5,1},{6,2},{7,3},{8,12},{9,13},{10,... | collective-permute-start | bytes 1572872 | tf_op jit(solution)/shard_map/ppermute | solution.py:21
  286.9 13.7 %collective-permute-start.24 = (bf16[2,512,256]{2,1,0:T(8,128)(2,1)}, bf16[2,512,256]{2,1,0:T(8,128)(2,1)}, u32[]{:S(2)}, u32[]{:S(2)}) collective-permute-start(bf16[2,512,256]{2,1,0:T(8,128)(2,1)} %get-tuple-element.66), channel_id=1, source_target_pairs={{0,1},{1,0},{2,3},{3,2},{4,5},{5,4},{6,7},{7,6},{8,9},{9,8},{10,11... | collective-permute-start | bytes 1572872 | tf_op jit(solution)/shard_map/ppermute | solution.py:21
  288.4 13.3 %collective-permute-start.25 = (bf16[2,512,256]{2,1,0:T(8,128)(2,1)}, bf16[2,512,256]{2,1,0:T(8,128)(2,1)S(1)}, u32[]{:S(2)}, u32[]{:S(2)}) collective-permute-start(bf16[2,512,256]{2,1,0:T(8,128)(2,1)} %get-tuple-element.67), channel_id=1, source_target_pairs={{0,2},{1,3},{2,0},{3,1},{4,6},{5,7},{6,4},{7,5},{8,10},{9,11},{10,... | collective-permute-start | bytes 1572872 | tf_op jit(solution)/shard_map/ppermute | solution.py:21
  300.7 24.4 %collective-permute-start.26 = (bf16[2,512,256]{2,1,0:T(8,128)(2,1)}, bf16[2,512,256]{2,1,0:T(8,128)(2,1)}, u32[]{:S(2)}, u32[]{:S(2)}) collective-permute-start(bf16[2,512,256]{2,1,0:T(8,128)(2,1)} %get-tuple-element.68), channel_id=1, source_target_pairs={{0,4},{1,5},{2,6},{3,7},{4,0},{5,1},{6,2},{7,3},{8,12},{9,13},{10,... | collective-permute-start | bytes 1572872 | tf_op jit(solution)/shard_map/ppermute | solution.py:21
  301.8 0.8 copy-start.5
  302.5 68.2 %collective-permute-start.18 = (bf16[2,512,512]{2,1,0:T(8,128)(2,1)}, bf16[2,512,512]{2,1,0:T(8,128)(2,1)S(1)}, u32[]{:S(2)}, u32[]{:S(2)}) collective-permute-start(bf16[2,512,512]{2,1,0:T(8,128)(2,1)} %get-tuple-element.60), channel_id=1, source_target_pairs={{0,1},{1,0},{2,3},{3,2},{4,5},{5,4},{6,7},{7,6},{8,9},{9,8},{10,11... | collective-permute-start | bytes 3145736 | tf_op jit(solution)/shard_map/ppermute | solution.py:21
  325.0 9.4 %collective-permute-start.27 = (bf16[1,512,256]{2,1,0:T(8,128)(2,1)}, bf16[1,512,256]{2,1,0:T(8,128)(2,1)S(1)}, u32[]{:S(2)}, u32[]{:S(2)}) collective-permute-start(bf16[1,512,256]{2,1,0:T(8,128)(2,1)} %get-tuple-element.75), channel_id=1, source_target_pairs={{0,1},{1,0},{2,3},{3,2},{4,5},{5,4},{6,7},{7,6},{8,9},{9,8},{10,11... | collective-permute-start | bytes 786440 | tf_op jit(solution)/shard_map/ppermute | solution.py:21
  326.5 23.9 %copy-start.1 = (f32[4,2,2,2,64,256]{5,4,3,2,1,0:T(8,128)}, f32[4,2,2,2,64,256]{5,4,3,2,1,0:T(8,128)S(1)}, u32[]{:S(2)}) copy-start(f32[4,2,2,2,64,256]{5,4,3,2,1,0:T(8,128)S(1)} %collective-permute-done.36.recv_ref) | copy-start | bytes 6291460
  326.5 12.6 %collective-permute-start.15 = (bf16[1,512,256]{2,1,0:T(8,128)(2,1)}, bf16[1,512,256]{2,1,0:T(8,128)(2,1)S(1)}, u32[]{:S(2)}, u32[]{:S(2)}) collective-permute-start(bf16[1,512,256]{2,1,0:T(8,128)(2,1)} %get-tuple-element.57), channel_id=1, source_target_pairs={{0,1},{1,0},{2,3},{3,2},{4,5},{5,4},{6,7},{7,6},{8,9},{9,8},{10,11... | collective-permute-start | bytes 786440 | tf_op jit(solution)/shard_map/ppermute | solution.py:21
  334.4 4.7 copy-start.14
  334.4 40.5 %collective-permute-start.19 = (bf16[2,512,512]{2,1,0:T(8,128)(2,1)}, bf16[2,512,512]{2,1,0:T(8,128)(2,1)}, u32[]{:S(2)}, u32[]{:S(2)}) collective-permute-start(bf16[2,512,512]{2,1,0:T(8,128)(2,1)} %get-tuple-element.61), channel_id=1, source_target_pairs={{0,2},{1,3},{2,0},{3,1},{4,6},{5,7},{6,4},{7,5},{8,10},{9,11},{10,... | collective-permute-start | bytes 3145736 | tf_op jit(solution)/shard_map/ppermute | solution.py:21
  339.1 11.4 %copy-start.13 = (bf16[1,512,256]{2,1,0:T(8,128)(2,1)}, bf16[1,512,256]{2,1,0:T(8,128)(2,1)S(1)}, u32[]{:S(2)}) copy-start(bf16[1,512,256]{2,1,0:T(8,128)(2,1)S(1)} %collective-permute-done.15.refs_0_) | copy-start | bytes 786436
  339.1 30.2 %collective-permute-start.16 = (bf16[1,512,256]{2,1,0:T(8,128)(2,1)}, bf16[1,512,256]{2,1,0:T(8,128)(2,1)}, u32[]{:S(2)}, u32[]{:S(2)}) collective-permute-start(bf16[1,512,256]{2,1,0:T(8,128)(2,1)} %get-tuple-element.58), channel_id=1, source_target_pairs={{0,2},{1,3},{2,0},{3,1},{4,6},{5,7},{6,4},{7,5},{8,10},{9,11},{10,... | collective-permute-start | bytes 786440 | tf_op jit(solution)/shard_map/ppermute | solution.py:21
  339.2 31.6 %collective-permute-start.17 = (bf16[1,512,256]{2,1,0:T(8,128)(2,1)}, bf16[1,512,256]{2,1,0:T(8,128)(2,1)}, u32[]{:S(2)}, u32[]{:S(2)}) collective-permute-start(bf16[1,512,256]{2,1,0:T(8,128)(2,1)} %get-tuple-element.59), channel_id=1, source_target_pairs={{0,4},{1,5},{2,6},{3,7},{4,0},{5,1},{6,2},{7,3},{8,12},{9,13},{10,... | collective-permute-start | bytes 786440 | tf_op jit(solution)/shard_map/ppermute | solution.py:21
  369.3 224.4 %collective-permute-start.35 = (f32[16,1,2,2,64,256]{5,4,3,2,1,0:T(8,128)}, f32[16,1,2,2,64,256]{5,4,3,2,1,0:T(8,128)}, u32[]{:S(2)}, u32[]{:S(2)}) collective-permute-start(f32[16,1,2,2,64,256]{5,4,3,2,1,0:T(8,128)} %get-tuple-element.89), channel_id=1, source_target_pairs={{0,16},{8,24},{16,0},{24,8},{1,17},{9,25},{17,1},{25,9},{2,18},{10... | collective-permute-start | bytes 12582920 | tf_op jit(solution)/shard_map/ppermute | solution.py:21
  370.8 118.5 %collective-permute-start.30 = (f32[4,2,2,2,64,256]{5,4,3,2,1,0:T(8,128)}, f32[4,2,2,2,64,256]{5,4,3,2,1,0:T(8,128)}, u32[]{:S(2)}, u32[]{:S(2)}) collective-permute-start(f32[4,2,2,2,64,256]{5,4,3,2,1,0:T(8,128)} %get-tuple-element.79), channel_id=1, source_target_pairs={{0,8},{8,0},{16,24},{24,16},{1,9},{9,1},{17,25},{25,17},{2,10},{10... | collective-permute-start | bytes 6291464 | tf_op jit(solution)/shard_map/ppermute | solution.py:21
  370.8 4.1 copy-start.3
  370.8 48.3 %collective-permute-start.20 = (bf16[2,512,512]{2,1,0:T(8,128)(2,1)}, bf16[2,512,512]{2,1,0:T(8,128)(2,1)S(1)}, u32[]{:S(2)}, u32[]{:S(2)}) collective-permute-start(bf16[2,512,512]{2,1,0:T(8,128)(2,1)} %get-tuple-element.62), channel_id=1, source_target_pairs={{0,4},{1,5},{2,6},{3,7},{4,0},{5,1},{6,2},{7,3},{8,12},{9,13},{10,... | collective-permute-start | bytes 3145736 | tf_op jit(solution)/shard_map/ppermute | solution.py:21
  374.9 107.0 %collective-permute-start.37 = (f32[4,1,2,2,64,256]{5,4,3,2,1,0:T(8,128)}, f32[4,1,2,2,64,256]{5,4,3,2,1,0:T(8,128)}, u32[]{:S(2)}, u32[]{:S(2)}) collective-permute-start(f32[4,1,2,2,64,256]{5,4,3,2,1,0:T(8,128)} %get-tuple-element.93), channel_id=1, source_target_pairs={{0,16},{8,24},{16,0},{24,8},{1,17},{9,25},{17,1},{25,9},{2,18},{10... | collective-permute-start | bytes 3145736 | tf_op jit(solution)/shard_map/ppermute | solution.py:21
  419.1 1.0 copy-start.4
  420.1 74.5 %collective-permute-start.21 = (bf16[2,512,1024]{2,1,0:T(8,128)(2,1)}, bf16[2,512,1024]{2,1,0:T(8,128)(2,1)S(1)}, u32[]{:S(2)}, u32[]{:S(2)}) collective-permute-start(bf16[2,512,1024]{2,1,0:T(8,128)(2,1)} %get-tuple-element.63), channel_id=1, source_target_pairs={{0,1},{1,0},{2,3},{3,2},{4,5},{5,4},{6,7},{7,6},{8,9},{9,8},{10,11... | collective-permute-start | bytes 6291464 | tf_op jit(solution)/shard_map/ppermute | solution.py:21
  481.9 88.5 %collective-permute-start.22 = (bf16[2,512,1024]{2,1,0:T(8,128)(2,1)}, bf16[2,512,1024]{2,1,0:T(8,128)(2,1)}, u32[]{:S(2)}, u32[]{:S(2)}) collective-permute-start(bf16[2,512,1024]{2,1,0:T(8,128)(2,1)} %get-tuple-element.64), channel_id=1, source_target_pairs={{0,2},{1,3},{2,0},{3,1},{4,6},{5,7},{6,4},{7,5},{8,10},{9,11},{10,... | collective-permute-start | bytes 6291464 | tf_op jit(solution)/shard_map/ppermute | solution.py:21
  481.9 90.2 %collective-permute-start.23 = (bf16[2,512,1024]{2,1,0:T(8,128)(2,1)}, bf16[2,512,1024]{2,1,0:T(8,128)(2,1)}, u32[]{:S(2)}, u32[]{:S(2)}) collective-permute-start(bf16[2,512,1024]{2,1,0:T(8,128)(2,1)} %get-tuple-element.65), channel_id=1, source_target_pairs={{0,4},{1,5},{2,6},{3,7},{4,0},{5,1},{6,2},{7,3},{8,12},{9,13},{10,... | collective-permute-start | bytes 6291464 | tf_op jit(solution)/shard_map/ppermute | solution.py:21
  489.3 110.1 %collective-permute-start.33 = (f32[8,1,2,2,64,256]{5,4,3,2,1,0:T(8,128)}, f32[8,1,2,2,64,256]{5,4,3,2,1,0:T(8,128)}, u32[]{:S(2)}, u32[]{:S(2)}) collective-permute-start(f32[8,1,2,2,64,256]{5,4,3,2,1,0:T(8,128)} %get-tuple-element.85), channel_id=1, source_target_pairs={{0,16},{8,24},{16,0},{24,8},{1,17},{9,25},{17,1},{25,9},{2,18},{10... | collective-permute-start | bytes 6291464 | tf_op jit(solution)/shard_map/ppermute | solution.py:21
  494.6 80.9 %copy-start = (bf16[2,512,1024]{2,1,0:T(8,128)(2,1)}, bf16[2,512,1024]{2,1,0:T(8,128)(2,1)S(1)}, u32[]{:S(2)}) copy-start(bf16[2,512,1024]{2,1,0:T(8,128)(2,1)S(1)} %collective-permute-done.21.refs_0_) | copy-start | bytes 6291460
  494.6 108.1 %collective-permute-start.31 = (f32[4,1,2,2,64,256]{5,4,3,2,1,0:T(8,128)}, f32[4,1,2,2,64,256]{5,4,3,2,1,0:T(8,128)}, u32[]{:S(2)}, u32[]{:S(2)}) collective-permute-start(f32[4,1,2,2,64,256]{5,4,3,2,1,0:T(8,128)} %get-tuple-element.81), channel_id=1, source_target_pairs={{0,16},{8,24},{16,0},{24,8},{1,17},{9,25},{17,1},{25,9},{2,18},{10... | collective-permute-start | bytes 3145736 | tf_op jit(solution)/shard_map/ppermute | solution.py:21
  570.4 22.5 %collective-permute-start.28 = (bf16[1,512,256]{2,1,0:T(8,128)(2,1)}, bf16[1,512,256]{2,1,0:T(8,128)(2,1)S(1)}, u32[]{:S(2)}, u32[]{:S(2)}) collective-permute-start(bf16[1,512,256]{2,1,0:T(8,128)(2,1)} %get-tuple-element.76), channel_id=1, source_target_pairs={{0,2},{1,3},{2,0},{3,1},{4,6},{5,7},{6,4},{7,5},{8,10},{9,11},{10,... | collective-permute-start | bytes 786440 | tf_op jit(solution)/shard_map/ppermute | solution.py:21
  572.1 20.7 %collective-permute-start.29 = (bf16[1,512,256]{2,1,0:T(8,128)(2,1)}, bf16[1,512,256]{2,1,0:T(8,128)(2,1)S(1)}, u32[]{:S(2)}, u32[]{:S(2)}) collective-permute-start(bf16[1,512,256]{2,1,0:T(8,128)(2,1)} %get-tuple-element.77), channel_id=1, source_target_pairs={{0,4},{1,5},{2,6},{3,7},{4,0},{5,1},{6,2},{7,3},{8,12},{9,13},{10,... | collective-permute-start | bytes 786440 | tf_op jit(solution)/shard_map/ppermute | solution.py:21
  573.0 2.5 copy-start.15
